TPU v7x, 32 devices: a whole 2x2x4 slice. The times are simulated.
32 devices in a mesh: expert: 8 (over z, y), shard: 4 (over x, core).
Axes of the slice: x: 2, y: 2, z: 4, core: 2. Of those that a mesh axis runs over, the one named last changes fastest.
Arguments:
- tokens: bfloat16 [2, 4096, 2048], P(None, ('expert', 'shard')), may hold values from -6 to 6
- cotangent: bfloat16 [2, 4096, 2048], P(None, ('expert', 'shard')), may hold values from -6 to 6
- qkv_weight: bfloat16 [2048, 6144], replicated, may hold values from -0.125 to 0.125
- out_weight: bfloat16 [2048, 2048], replicated, may hold values from -1.75 to 1.75
- router_weight: bfloat16 [2048, 16], replicated, may hold values from -0.0625 to 0.0625
- attn_gain: float32 [2048], replicated, may hold values from 0.5 to 1.5
- moe_gain: float32 [2048], replicated, may hold values from 0.5 to 1.5
- head_gains: float32 [256], replicated, may hold values from 0.5 to 1.5
- gate_weight: bfloat16 [16, 2048, 1024], P('expert', 'shard'), may hold values from -0.125 to 0.125
- up_weight: bfloat16 [16, 2048, 1024], P('expert', 'shard'), may hold values from -0.125 to 0.125
- down_weight: bfloat16 [16, 1024, 2048], P('expert', 'shard'), may hold values from -3 to 3
- permutation: int32 [2, 4, 1024], P(None, 'shard'), may hold values from 0 to 1023, each once within a row
- lengths: int32 [2, 4, 3], P(None, 'shard'), may hold values from 1 to 682, 1024 in all within a row
- routes: int32 [2, 4096, 8], P(None, ('expert', 'shard')), may hold values from 0 to 15, all different within a row
Outputs:
- output: bfloat16 [2, 4096, 2048], P(None, ('expert', 'shard'))
- input_grad: bfloat16 [2, 4096, 2048], P(None, ('expert', 'shard'))
- qkv_grad: float32 [2048, 6144], P(('expert', 'shard'))
- out_grad: float32 [2048, 2048], P(('expert', 'shard'))
- router_grad: float32 [2048, 16], P(('expert', 'shard'))
- attn_gain_grad: float32 [2048], P(('expert', 'shard'))
- moe_gain_grad: float32 [2048], P(('expert', 'shard'))
- head_gain_grad: float32 [256], P(('expert', 'shard'))
- gate_grad: float32 [16, 2048, 1024], P('expert', 'shard')
- up_grad: float32 [16, 2048, 1024], P('expert', 'shard')
- down_grad: float32 [16, 1024, 2048], P('expert', 'shard')
Inputs may be any that keep to these rules, and one draw needn't show every extreme that they name: `lengths`: each row sums to 1024; its largest entry is 682. `routes`: the 8 experts of a token differ.
All inputs are finite; a program needn't handle non-finite values.
Results may differ from a plain program's by a relative error of at most 0.03.
Values may be sent and summed in bfloat16 or wider, within the bound.
No kernel may reach another device: no remote copies, remote signals or barrier semaphores. Data moves between devices by JAX's collectives and lax.ppermute only.
A program may use at most 448 MiB of HBM per device.

v0:
```python
import jax
import jax.numpy as jnp
from jax import lax
from jax.sharding import PartitionSpec as P

HEAD = 128


EPS = 1e-06
ROPE_BASE = 10000.0
NEGATIVE = -1e30


def rms_scale(values, gain_vec):
    return values * lax.rsqrt(jnp.mean(values * values, axis=-1, keepdims=True) + EPS) * gain_vec


def rotate(values, cosine, sine):
    half_size = values.shape[-1] // 2
    lower_half = values[..., :half_size]
    upper_half = values[..., half_size:]
    return jnp.concatenate(
        [lower_half * cosine - upper_half * sine, upper_half * cosine + lower_half * sine], axis=-1
    )


def places(perm_row, length_row):
    seq_ends = jnp.cumsum(length_row)
    seg_ids = jnp.sum((perm_row[:, None] >= seq_ends[None, :]).astype(jnp.int32), axis=1)
    starts = seq_ends - length_row
    pick_mask = seg_ids[:, None] == jnp.arange(length_row.shape[0], dtype=jnp.int32)[None, :]
    seq_begin = jnp.sum(jnp.where(pick_mask, starts[None, :], 0), axis=1)
    return (seg_ids, perm_row - seq_begin)


def angles(positions):
    half_size = HEAD // 2
    frequency = jnp.power(ROPE_BASE, -2.0 * jnp.arange(half_size, dtype=jnp.float32) / HEAD)
    turned = positions.astype(jnp.float32)[:, None] * frequency[None, :]
    return (jnp.cos(turned)[:, None, :], jnp.sin(turned)[:, None, :])


def head_prep(qkv_out, head_gains, cosine, sine):
    model_width = qkv_out.shape[1] // 3
    row_count = qkv_out.shape[0]
    query_rows = qkv_out[:, :model_width].reshape(row_count, model_width // HEAD, HEAD)
    key_rows = qkv_out[:, model_width : 2 * model_width].reshape(
        row_count, model_width // HEAD, HEAD
    )
    value_rows = qkv_out[:, 2 * model_width :]
    query_rows = rotate(rms_scale(query_rows, head_gains[:HEAD]), cosine, sine)
    key_rows = rotate(rms_scale(key_rows, head_gains[HEAD:]), cosine, sine)
    return (
        query_rows.reshape(row_count, model_width),
        key_rows.reshape(row_count, model_width),
        value_rows,
    )


def swiglu(gate_in, up_in):
    return jax.nn.silu(gate_in) * up_in


def accumulate(running, term):
    if running is None:
        return term
    return jax.tree.map(jnp.add, running, term)


def local(
    tokens,
    cotangent,
    qkv_weight,
    out_weight,
    router_weight,
    attn_gain,
    moe_gain,
    head_gains,
    gate_weight,
    up_weight,
    down_weight,
    permutation,
    lengths,
    routes,
):
    micro_count, row_count, model_width = tokens.shape
    head_count = model_width // HEAD
    score_scale = HEAD ** (-0.5)
    expert_axis = lax.axis_size("expert")
    local_count = gate_weight.shape[0]
    expert_count = local_count * expert_axis
    top_count = routes.shape[2]
    capacity = row_count * top_count // expert_count
    slot_count = expert_count * capacity
    group_rows = permutation.shape[2]
    own_index = lax.axis_index("expert")
    expert_ids = jnp.arange(expert_count, dtype=jnp.int32)
    outputs = []
    input_grads = []
    dense_total = None
    expert_total = None
    for micro_step in range(micro_count):
        full_gate, full_up, full_down = (
            lax.all_gather(gate_weight, "shard", axis=1, tiled=True),
            lax.all_gather(up_weight, "shard", axis=1, tiled=True),
            lax.all_gather(down_weight, "shard", axis=1, tiled=True),
        )
        inputs = tokens[micro_step].astype(jnp.float32)
        seg_all, pos_all = places(permutation[micro_step, 0], lengths[micro_step, 0])
        seg_own = lax.dynamic_slice_in_dim(seg_all, own_index * row_count, row_count)
        pos_own = lax.dynamic_slice_in_dim(pos_all, own_index * row_count, row_count)
        cosine, sine = angles(pos_own)
        normed_attn = rms_scale(inputs, attn_gain).astype(jnp.bfloat16)
        qkv_out = jnp.dot(normed_attn, qkv_weight, preferred_element_type=jnp.float32)
        query_rows, key_rows, value_rows = head_prep(qkv_out, head_gains, cosine, sine)
        query_low = query_rows.astype(jnp.bfloat16)
        key_low = key_rows.astype(jnp.bfloat16)
        value_low = value_rows.astype(jnp.bfloat16)
        all_keys, all_values = (
            lax.all_gather(key_low, "expert", axis=0, tiled=True),
            lax.all_gather(value_low, "expert", axis=0, tiled=True),
        )
        query_h = query_low.reshape(row_count, head_count, HEAD)
        keys_h = all_keys.reshape(group_rows, head_count, HEAD)
        values_h = all_values.reshape(group_rows, head_count, HEAD)
        same_seq = (seg_own[:, None] == seg_all[None, :])[None]
        raw_scores = (
            jnp.einsum("qhd,khd->hqk", query_h, keys_h, preferred_element_type=jnp.float32)
            * score_scale
        )
        scores = jnp.where(same_seq, raw_scores, NEGATIVE)
        top_score = jnp.max(scores, axis=-1, keepdims=True)
        exp_terms = jnp.exp(scores - top_score)
        row_total = jnp.sum(exp_terms, axis=-1, keepdims=True)
        probs = exp_terms / row_total
        log_total = top_score + jnp.log(row_total)
        attended = (
            jnp.einsum(
                "hqk,khd->qhd",
                probs.astype(jnp.bfloat16),
                values_h,
                preferred_element_type=jnp.float32,
            )
            .reshape(row_count, model_width)
            .astype(jnp.bfloat16)
        )
        mixed = inputs + jnp.dot(attended, out_weight, preferred_element_type=jnp.float32)
        normed_moe = rms_scale(mixed, moe_gain).astype(jnp.bfloat16)
        logits = jnp.dot(normed_moe, router_weight, preferred_element_type=jnp.float32)
        exp_logits = jnp.exp(logits - jnp.max(logits, axis=-1, keepdims=True))
        router = exp_logits / jnp.sum(exp_logits, axis=-1, keepdims=True)
        flat_routes = routes[micro_step].reshape(-1)
        route_hot = flat_routes[:, None] == expert_ids[None, :]
        hot_int = route_hot.astype(jnp.int32)
        earlier = jnp.cumsum(hot_int, axis=0) - hot_int
        slot_ids = jnp.sum(earlier * hot_int, axis=1)
        keep_pair = slot_ids < capacity
        target = jnp.where(keep_pair, flat_routes * capacity + slot_ids, slot_count)
        safe_target = jnp.minimum(target, slot_count - 1)
        pair_rows = jnp.repeat(normed_moe, top_count, axis=0)
        dispatch = (
            jnp.zeros((slot_count + 1, model_width), jnp.bfloat16)
            .at[target]
            .set(pair_rows)[:slot_count]
        )
        dispatch = dispatch.reshape(expert_axis, local_count, capacity, model_width)
        arrived = lax.all_to_all(
            dispatch, "expert", split_axis=0, concat_axis=2, tiled=True
        ).reshape(local_count, expert_axis * capacity, model_width)
        gate_act = jnp.einsum(
            "erd,edf->erf", arrived, full_gate, preferred_element_type=jnp.float32
        )
        up_act = jnp.einsum("erd,edf->erf", arrived, full_up, preferred_element_type=jnp.float32)
        hidden_act, swiglu_pull = jax.vjp(swiglu, gate_act, up_act)
        hidden_low = hidden_act.astype(jnp.bfloat16)
        expert_out = jnp.einsum(
            "erf,efd->erd", hidden_low, full_down, preferred_element_type=jnp.float32
        ).astype(jnp.bfloat16)
        returned = lax.all_to_all(
            expert_out.reshape(1, local_count, expert_axis * capacity, model_width),
            "expert",
            split_axis=2,
            concat_axis=0,
            tiled=True,
        ).reshape(slot_count, model_width)
        picked = (
            returned[safe_target].astype(jnp.float32).reshape(row_count, top_count, model_width)
        )
        pair_hot = route_hot.reshape(row_count, top_count, expert_count)
        keep_grid = keep_pair.reshape(row_count, top_count)
        gate_vals = jnp.sum(jnp.where(pair_hot, router[:, None, :], 0.0), axis=-1)
        pair_weight = jnp.where(keep_grid, gate_vals, 0.0)
        moe_part = jnp.sum(pair_weight[:, :, None] * picked, axis=1)
        outputs.append((mixed + moe_part).astype(jnp.bfloat16))
        grad_out = cotangent[micro_step].astype(jnp.float32)
        d_pairs = (
            (pair_weight[:, :, None] * grad_out[:, None, :])
            .reshape(-1, model_width)
            .astype(jnp.bfloat16)
        )
        d_result = (
            jnp.zeros((slot_count + 1, model_width), jnp.bfloat16)
            .at[target]
            .set(d_pairs)[:slot_count]
        )
        d_gates = jnp.where(keep_grid, jnp.sum(picked * grad_out[:, None, :], axis=-1), 0.0)
        d_router = jnp.sum(jnp.where(pair_hot, d_gates[:, :, None], 0.0), axis=1)
        d_logits = (
            router * (d_router - jnp.sum(router * d_router, axis=-1, keepdims=True))
        ).astype(jnp.bfloat16)
        d_arrived_out = lax.all_to_all(
            d_result.reshape(expert_axis, local_count, capacity, model_width),
            "expert",
            split_axis=0,
            concat_axis=2,
            tiled=True,
        ).reshape(local_count, expert_axis * capacity, model_width)
        d_hidden = jnp.einsum(
            "erd,efd->erf", d_arrived_out, full_down, preferred_element_type=jnp.float32
        )
        d_gate_act, d_up_act = swiglu_pull(d_hidden)
        d_gate_low = d_gate_act.astype(jnp.bfloat16)
        d_up_low = d_up_act.astype(jnp.bfloat16)
        down_term = jnp.einsum(
            "erf,erd->efd", hidden_low, d_arrived_out, preferred_element_type=jnp.float32
        )
        gate_term = jnp.einsum(
            "erd,erf->edf", arrived, d_gate_low, preferred_element_type=jnp.float32
        )
        up_term = jnp.einsum("erd,erf->edf", arrived, d_up_low, preferred_element_type=jnp.float32)
        d_rows = (
            jnp.einsum("erf,edf->erd", d_gate_low, full_gate, preferred_element_type=jnp.float32)
            + jnp.einsum("erf,edf->erd", d_up_low, full_up, preferred_element_type=jnp.float32)
        ).astype(jnp.bfloat16)
        d_back = lax.all_to_all(
            d_rows.reshape(1, local_count, expert_axis * capacity, model_width),
            "expert",
            split_axis=2,
            concat_axis=0,
            tiled=True,
        ).reshape(slot_count, model_width)
        d_fetched = jnp.where(keep_pair[:, None], d_back[safe_target].astype(jnp.float32), 0.0)
        d_normed = jnp.sum(d_fetched.reshape(row_count, top_count, model_width), axis=1)
        d_normed = d_normed + jnp.dot(d_logits, router_weight.T, preferred_element_type=jnp.float32)
        router_term = jnp.dot(normed_moe.T, d_logits, preferred_element_type=jnp.float32)
        _, moe_norm_pull = jax.vjp(rms_scale, mixed, moe_gain)
        d_mixed_norm, moe_gain_term = moe_norm_pull(d_normed)
        d_mixed = grad_out + d_mixed_norm
        d_attn = d_mixed.astype(jnp.bfloat16)
        out_term = jnp.dot(attended.T, d_attn, preferred_element_type=jnp.float32)
        d_attended = jnp.dot(d_attn, out_weight.T, preferred_element_type=jnp.float32).astype(
            jnp.bfloat16
        )
        d_attended_h = d_attended.reshape(row_count, head_count, HEAD)
        again_raw = (
            jnp.einsum("qhd,khd->hqk", query_h, keys_h, preferred_element_type=jnp.float32)
            * score_scale
        )
        probs_back = jnp.exp(jnp.where(same_seq, again_raw, NEGATIVE) - log_total)
        d_probs = jnp.einsum(
            "qhd,khd->hqk", d_attended_h, values_h, preferred_element_type=jnp.float32
        )
        row_delta = jnp.sum(probs_back * d_probs, axis=-1, keepdims=True)
        d_scores = (probs_back * (d_probs - row_delta)).astype(jnp.bfloat16)
        d_query = (
            jnp.einsum("hqk,khd->qhd", d_scores, keys_h, preferred_element_type=jnp.float32)
            * score_scale
        )
        d_keys = (
            jnp.einsum("hqk,qhd->khd", d_scores, query_h, preferred_element_type=jnp.float32)
            * score_scale
        ).reshape(group_rows, model_width)
        d_values = jnp.einsum(
            "hqk,qhd->khd",
            probs_back.astype(jnp.bfloat16),
            d_attended_h,
            preferred_element_type=jnp.float32,
        ).reshape(group_rows, model_width)
        d_key_own, d_value_own = (
            lax.psum_scatter(
                d_keys.astype(jnp.bfloat16), "expert", scatter_dimension=0, tiled=True
            ).astype(jnp.float32),
            lax.psum_scatter(
                d_values.astype(jnp.bfloat16), "expert", scatter_dimension=0, tiled=True
            ).astype(jnp.float32),
        )
        _, head_pull = jax.vjp(
            lambda qkv_in, gains_in: head_prep(qkv_in, gains_in, cosine, sine), qkv_out, head_gains
        )
        d_qkv, head_term = head_pull(
            (d_query.reshape(row_count, model_width), d_key_own, d_value_own)
        )
        d_qkv_low = d_qkv.astype(jnp.bfloat16)
        qkv_term = jnp.dot(normed_attn.T, d_qkv_low, preferred_element_type=jnp.float32)
        d_normed_attn = jnp.dot(d_qkv_low, qkv_weight.T, preferred_element_type=jnp.float32)
        _, attn_norm_pull = jax.vjp(rms_scale, inputs, attn_gain)
        d_inputs_norm, attn_gain_term = attn_norm_pull(d_normed_attn)
        input_grads.append((d_mixed + d_inputs_norm).astype(jnp.bfloat16))
        dense_piece = (
            lax.psum_scatter(qkv_term, ("expert", "shard"), scatter_dimension=0, tiled=True),
            lax.psum_scatter(out_term, ("expert", "shard"), scatter_dimension=0, tiled=True),
            lax.psum_scatter(router_term, ("expert", "shard"), scatter_dimension=0, tiled=True),
            lax.psum_scatter(attn_gain_term, ("expert", "shard"), scatter_dimension=0, tiled=True),
            lax.psum_scatter(moe_gain_term, ("expert", "shard"), scatter_dimension=0, tiled=True),
            lax.psum_scatter(head_term, ("expert", "shard"), scatter_dimension=0, tiled=True),
        )
        expert_piece = (
            lax.psum_scatter(
                gate_term.astype(jnp.bfloat16), "shard", scatter_dimension=1, tiled=True
            ).astype(jnp.float32),
            lax.psum_scatter(
                up_term.astype(jnp.bfloat16), "shard", scatter_dimension=1, tiled=True
            ).astype(jnp.float32),
            lax.psum_scatter(
                down_term.astype(jnp.bfloat16), "shard", scatter_dimension=1, tiled=True
            ).astype(jnp.float32),
        )
        dense_total = accumulate(dense_total, dense_piece)
        expert_total = accumulate(expert_total, expert_piece)
    return (
        jnp.stack(outputs),
        jnp.stack(input_grads),
        dense_total[0],
        dense_total[1],
        dense_total[2],
        dense_total[3],
        dense_total[4],
        dense_total[5],
        expert_total[0],
        expert_total[1],
        expert_total[2],
    )


def solution(mesh):
    return jax.shard_map(
        local,
        mesh=mesh,
        in_specs=(
            P(None, ("expert", "shard"), None),
            P(None, ("expert", "shard"), None),
            P(),
            P(),
            P(),
            P(),
            P(),
            P(),
            P("expert", "shard", None),
            P("expert", "shard", None),
            P("expert", "shard", None),
            P(None, "shard", None),
            P(None, "shard", None),
            P(None, ("expert", "shard"), None),
        ),
        out_specs=(
            P(None, ("expert", "shard"), None),
            P(None, ("expert", "shard"), None),
            P(("expert", "shard"), None),
            P(("expert", "shard"), None),
            P(("expert", "shard"), None),
            P(("expert", "shard")),
            P(("expert", "shard")),
            P(("expert", "shard")),
            P("expert", "shard", None),
            P("expert", "shard", None),
            P("expert", "shard", None),
        ),
        check_vma=False,
    )
```

profile of v0, /device:TPU:8, one launch (start us, length us, event | category | flops | bytes accessed | tf_op | source)
XLA Modules:
  0.0 2869.8 jit_solution(16022105452572920121)
XLA Ops:
  13.0 10.3 fusion.120
  31.4 10.5 fusion.117
  67.0 61.7 %all-gather.10.cloned.1.call-done = bf16[1024,2048]{0,1:T(8,128)(2,1)} async-done(((bf16[128,2048]{0,1:T(8,128)(2,1)}), bf16[1024,2048]{0,1:T(8,128)(2,1)}) %all-gather.10.cloned.1.call-update) | async-done | bytes 4194320 | tf_op jit(solution)/shard_map/all_gather | solution.py:120
  138.3 65.9 %all-gather.8.cloned.1.call-done = bf16[1024,2048]{1,0:T(8,128)(2,1)} async-done(((bf16[128,2048]{1,0:T(8,128)(2,1)}), bf16[1024,2048]{1,0:T(8,128)(2,1)}) %all-gather.8.cloned.1.call-update) | async-done | bytes 4194320 | tf_op jit(solution)/shard_map/all_gather | solution.py:121
  219.2 9.6 scatter_custom_fusion.2
  240.3 9.1 scatter_custom_fusion
  254.2 75.1 %all-to-all-done.4 = bf16[8,2,64,2048]{3,2,1,0:T(8,128)(2,1)} async-done(((bf16[8,2,64,2048]{3,2,1,0:T(8,128)(2,1)}), bf16[8,2,64,2048]{3,2,1,0:T(8,128)(2,1)}, u32[]{:S(2)}, u32[]{:S(2)}) %all-to-all-start.4) | async-done | bytes 4194336 | tf_op jit(solution)/shard_map/all_to_all | solution.py:211
  329.3 7.3 all-to-all-start
  346.3 113.7 %all-to-all-done = bf16[8,2,64,2048]{3,2,1,0:T(8,128)(2,1)} async-done(((bf16[8,2,64,2048]{3,2,1,0:T(8,128)(2,1)}), bf16[8,2,64,2048]{3,2,1,0:T(8,128)(2,1)}, u32[]{:S(2)}, u32[]{:S(2)}) %all-to-all-start) | async-done | bytes 4194336 | tf_op jit(solution)/shard_map/all_to_all | solution.py:167
  464.8 11.2 fusion.164
  476.0 11.2 fusion.163
  487.1 13.0 multiply_convert_fusion.5
  500.2 7.6 convert_bitcast_fusion.1
  507.8 8.4 copy.490
  516.2 8.3 all-to-all-start.1
  527.1 11.8 fusion.167
  538.9 12.9 fusion.22
  551.8 8.7 copy.511
  560.5 102.4 %all-to-all-done.1 = bf16[1,2,512,2048]{3,1,0,2:T(2,128)(2,1)} async-done(((bf16[1,2,512,2048]{3,1,0,2:T(2,128)(2,1)}), bf16[1,2,512,2048]{3,1,0,2:T(2,128)(2,1)}, u32[]{:S(2)}, u32[]{:S(2)}) %all-to-all-start.1) | async-done | bytes 4194336 | tf_op jit(solution)/shard_map/all_to_all | solution.py:179
  662.9 7.9 all-to-all-start.5
  686.5 7.2 fusion.69
  704.8 11.6 gather_fusion
  722.6 38.1 %all-to-all-done.5 = bf16[1,2,512,2048]{3,1,0,2:T(2,128)(2,1)} async-done(((bf16[1,2,512,2048]{3,1,0,2:T(2,128)(2,1)}), bf16[1,2,512,2048]{3,1,0,2:T(2,128)(2,1)}, u32[]{:S(2)}, u32[]{:S(2)}) %all-to-all-start.5) | async-done | bytes 4194336 | tf_op jit(solution)/shard_map/all_to_all | solution.py:235
  766.8 11.5 gather_fusion.2
  788.6 9.8 scatter_custom_fusion.3
  810.3 9.0 scatter_custom_fusion.1
  824.2 76.3 %all-to-all-done.6 = bf16[8,2,64,2048]{3,2,1,0:T(8,128)(2,1)} async-done(((bf16[8,2,64,2048]{3,2,1,0:T(8,128)(2,1)}), bf16[8,2,64,2048]{3,2,1,0:T(8,128)(2,1)}, u32[]{:S(2)}, u32[]{:S(2)}) %all-to-all-start.6) | async-done | bytes 4194336 | tf_op jit(solution)/shard_map/all_to_all | solution.py:211
  900.4 7.2 all-to-all-start.2
  912.4 85.3 %all-to-all-done.2 = bf16[8,2,64,2048]{3,2,1,0:T(8,128)(2,1)} async-done(((bf16[8,2,64,2048]{3,2,1,0:T(8,128)(2,1)}), bf16[8,2,64,2048]{3,2,1,0:T(8,128)(2,1)}, u32[]{:S(2)}, u32[]{:S(2)}) %all-to-all-start.2) | async-done | bytes 4194336 | tf_op jit(solution)/shard_map/all_to_all | solution.py:167
  1000.6 10.9 fusion.166
  1017.7 12.4 multiply_convert_fusion.4
  1031.5 9.4 convert_bitcast_fusion
  1040.8 8.6 copy.507
  1049.4 7.2 all-to-all-start.3
  1056.6 11.8 fusion.168
  1068.4 12.9 fusion.23
  1081.4 8.9 copy.530
  1090.3 56.2 %all-to-all-done.3 = bf16[1,2,512,2048]{3,1,0,2:T(2,128)(2,1)} async-done(((bf16[1,2,512,2048]{3,1,0,2:T(2,128)(2,1)}), bf16[1,2,512,2048]{3,1,0,2:T(2,128)(2,1)}, u32[]{:S(2)}, u32[]{:S(2)}) %all-to-all-start.3) | async-done | bytes 4194336 | tf_op jit(solution)/shard_map/all_to_all | solution.py:179
  1160.0 11.6 gather_fusion.1
  1177.6 66.1 %all-to-all-done.7 = bf16[1,2,512,2048]{3,1,0,2:T(2,128)(2,1)} async-done(((bf16[1,2,512,2048]{3,1,0,2:T(2,128)(2,1)}), bf16[1,2,512,2048]{3,1,0,2:T(2,128)(2,1)}, u32[]{:S(2)}, u32[]{:S(2)}) %all-to-all-start.7) | async-done | bytes 4194336 | tf_op jit(solution)/shard_map/all_to_all | solution.py:235
  1249.7 11.8 gather_fusion.3
  1349.1 10.6 convolution_convert_fusion.3
  1359.8 11.0 convolution_convert_fusion.2
  1371.0 10.8 convolution_convert_fusion.5
  1381.9 10.7 convolution_convert_fusion.4
  1392.9 11.0 convolution_convert_fusion.1
  1404.0 10.7 convolution_convert_fusion
  1418.1 8.1 convolution_add_fusion.1
  1443.0 31.5 %reduce-scatter.42.cloned.1.call-done = bf16[128,2048]{1,0:T(8,128)(2,1)} async-done(((bf16[1024,2048]{1,0:T(8,128)(2,1)}), bf16[128,2048]{1,0:T(8,128)(2,1)}) %reduce-scatter.42.cloned.1.call-update) | async-done | bytes 524304
  1512.3 53.5 %reduce-scatter.44.cloned.1.call-done = bf16[128,2048]{1,0:T(8,128)(2,1)} async-done(((bf16[1024,2048]{1,0:T(8,128)(2,1)}), bf16[128,2048]{1,0:T(8,128)(2,1)}) %reduce-scatter.44.cloned.1.call-update) | async-done | bytes 524304
  1567.8 89.7 %reduce-scatter.40.cloned.1.call-done = bf16[128,2048]{1,0:T(8,128)(2,1)} async-done(((bf16[1024,2048]{1,0:T(8,128)(2,1)}), bf16[128,2048]{1,0:T(8,128)(2,1)}) %reduce-scatter.40.cloned.1.call-update) | async-done | bytes 524304
  1659.6 21.3 fusion.113
  1680.9 32.9 %convolution_add_fusion = f32[2048,6144]{1,0:T(8,128)} fusion(f32[2048,6144]{1,0:T(8,128)} %fusion.113, f32[128,2048]{0,1:T(8,128)} %bitcast.405, f32[128,2048]{0,1:T(8,128)} %bitcast.407, bf16[128,2048]{0,1:T(8,128)(2,1)} %copy.570, f32[128]{0:T(128)S(1)} %copy-done.95, f32[2048]{0:T(1024)S(1)} %copy-done.57, bf16[2,128,2048]{2,1,0:T(8,128)(2,1)S(1)} %copy-done.8), kind=kOutput, calls=%fused_computation.8 | convolution fusion | flops 3238002688 | bytes 103817728 | tf_op jit(solution)/shard_map/dot_general | solution.py:294
  1716.7 58.6 %reduce-scatter.48.cloned.1.call-done = f32[64,16]{1,0:T(8,128)} async-done(((f32[2048,16]{1,0:T(8,128)}), f32[64,16]{1,0:T(8,128)}) %reduce-scatter.48.cloned.1.call-update) | async-done | bytes 4112
  1776.7 14.9 fusion.115
  1791.6 15.6 fusion.81
  1807.2 61.2 %all-reduce.21 = (f32[2048]{0:T(1024)S(1)}, f32[2048]{0:T(1024)S(1)}, f32[256]{0:T(256)S(1)}) all-reduce(f32[2048]{0:T(1024)S(1)} %add.391, f32[2048]{0:T(1024)S(1)} %add.392, f32[256]{0:T(256)S(1)} %add_add_fusion.8), channel_id=15, replica_groups=mesh['expert'=8,'shard'=4] {'expert','shard'}, use_global_device_ids=true, to_apply=%region_65.66.clone | all-reduce | flops 4352 | bytes 34816
  1873.4 66.6 %reduce-scatter.30.cloned.1.call-done = bf16[2,512,1024]{2,1,0:T(8,128)(2,1)} async-done(((bf16[2,2048,1024]{2,1,0:T(8,128)(2,1)}), bf16[2,512,1024]{2,1,0:T(8,128)(2,1)}) %reduce-scatter.30.cloned.1.call-update) | async-done | bytes 2097168 | tf_op jit(solution)/shard_map/reduce_scatter | solution.py:311
  1945.2 69.2 %reduce-scatter.24.cloned.1.call-done = bf16[2,512,1024]{2,1,0:T(8,128)(2,1)} async-done(((bf16[2,2048,1024]{2,1,0:T(8,128)(2,1)}), bf16[2,512,1024]{2,1,0:T(8,128)(2,1)}) %reduce-scatter.24.cloned.1.call-update) | async-done | bytes 2097168 | tf_op jit(solution)/shard_map/reduce_scatter | solution.py:308
  2014.4 74.2 %reduce-scatter.26.cloned.1.call-done = bf16[2,512,1024]{2,1,0:T(8,128)(2,1)} async-done(((bf16[2,2048,1024]{2,1,0:T(8,128)(2,1)}), bf16[2,512,1024]{2,1,0:T(8,128)(2,1)}) %reduce-scatter.26.cloned.1.call-update) | async-done | bytes 2097168 | tf_op jit(solution)/shard_map/reduce_scatter | solution.py:308
  2093.8 69.1 %reduce-scatter.32.cloned.1.call-done = bf16[2,256,2048]{2,1,0:T(8,128)(2,1)} async-done(((bf16[2,1024,2048]{2,1,0:T(8,128)(2,1)}), bf16[2,256,2048]{2,1,0:T(8,128)(2,1)}) %reduce-scatter.32.cloned.1.call-update) | async-done | bytes 2097168 | tf_op jit(solution)/shard_map/reduce_scatter | solution.py:314
  2162.9 74.2 %reduce-scatter.34.cloned.1.call-done = bf16[2,256,2048]{2,1,0:T(8,128)(2,1)} async-done(((bf16[2,1024,2048]{2,1,0:T(8,128)(2,1)}), bf16[2,256,2048]{2,1,0:T(8,128)(2,1)}) %reduce-scatter.34.cloned.1.call-update) | async-done | bytes 2097168 | tf_op jit(solution)/shard_map/reduce_scatter | solution.py:314
  2242.2 177.3 %reduce-scatter.38.cloned.1.call-done = f32[64,2048]{1,0:T(8,128)} async-done(((f32[2048,2048]{1,0:T(8,128)}), f32[64,2048]{1,0:T(8,128)}) %reduce-scatter.38.cloned.1.call-update) | async-done | bytes 524304 | tf_op jit(solution)/shard_map/reduce_scatter | solution.py:301
  2419.5 443.3 %reduce-scatter.36.cloned.1.call-done = f32[64,6144]{1,0:T(8,128)} async-done(((f32[2048,6144]{1,0:T(8,128)}), f32[64,6144]{1,0:T(8,128)}) %reduce-scatter.36.cloned.1.call-update) | async-done | bytes 1572880 | tf_op jit(solution)/shard_map/reduce_scatter | solution.py:300
  (499 shorter events, 377.1 us)
Async XLA Ops:
  7.2 211.4 %copy-start = (bf16[2048,16]{0,1:T(8,128)(2,1)S(1)}, bf16[2048,16]{0,1:T(8,128)(2,1)}, u32[]{:S(2)}) copy-start(bf16[2048,16]{0,1:T(8,128)(2,1)} %param.18) | copy-start | bytes 196612
  7.2 121.5 %all-gather.10.cloned.1.call-start = ((), (), s32[]{:S(2)}) async-start(), calls=%async_computation.22 | async-start | bytes 4718592 | tf_op jit(solution)/shard_map/all_gather | solution.py:120
  8.0 40.0 %copy-start.98 = (f32[128]{0:T(128)}, f32[128]{0:T(128)S(1)}, u32[]{:S(2)}) copy-start(f32[128]{0:T(128)S(1)} %get-tuple-element.110) | copy-start | bytes 1540
  8.0 42.5 %copy-start.96 = (f32[128]{0:T(128)}, f32[128]{0:T(128)S(1)}, u32[]{:S(2)}) copy-start(f32[128]{0:T(128)S(1)} %get-tuple-element.109) | copy-start | bytes 1540
  11.1 20.3 copy-start.92
  11.1 12.2 copy-start.94
  26.5 15.4 copy-start.75
  26.5 24.1 copy-start.67
  26.8 23.7 copy-start.13
  28.9 13.0 copy-start.77
  29.7 18.2 copy-start.71
  31.3 16.6 copy-start.15
  48.0 288.8 %copy-start.62 = (f32[128,64]{1,0:T(8,128)}, f32[128,64]{1,0:T(8,128)S(1)}, u32[]{:S(2)}) copy-start(f32[128,64]{1,0:T(8,128)S(1)} %get-tuple-element.123) | copy-start | bytes 98308
  48.0 288.8 %copy-start.64 = (f32[128,64]{1,0:T(8,128)}, f32[128,64]{1,0:T(8,128)S(1)}, u32[]{:S(2)}) copy-start(f32[128,64]{1,0:T(8,128)S(1)} %get-tuple-element.124) | copy-start | bytes 98308
  52.8 75.9 %copy-start.39 = (bf16[128,16,64]{2,0,1:T(8,128)(2,1)}, bf16[128,16,64]{2,0,1:T(8,128)(2,1)S(1)}, u32[]{:S(2)}) copy-start(bf16[128,16,64]{2,0,1:T(8,128)(2,1)S(1)} %get-tuple-element.66) | copy-start | bytes 786436
  52.8 75.9 %copy-start.41 = (bf16[128,16,64]{2,0,1:T(8,128)(2,1)}, bf16[128,16,64]{2,0,1:T(8,128)(2,1)S(1)}, u32[]{:S(2)}) copy-start(bf16[128,16,64]{2,0,1:T(8,128)(2,1)S(1)} %get-tuple-element.67) | copy-start | bytes 786436
  54.2 150.0 %all-gather.8.cloned.1.call-start = ((), (), s32[]{:S(2)}) async-start(), calls=%async_computation.21 | async-start | bytes 4718592 | tf_op jit(solution)/shard_map/all_gather | solution.py:121
  56.3 408.4 %all-gather.14.cloned.1.call-start = ((), (), s32[]{:S(2)}) async-start(), calls=%async_computation.24 | async-start | bytes 10485760 | tf_op jit(solution)/shard_map/all_gather | solution.py:105
  57.1 418.9 %all-gather.12.cloned.1.call-start = ((), (), s32[]{:S(2)}) async-start(), calls=%async_computation.23 | async-start | bytes 10485760 | tf_op jit(solution)/shard_map/all_gather | solution.py:104
  67.0 152.2 %copy-start.24 = (f32[128,2048]{1,0:T(8,128)}, f32[128,2048]{1,0:T(8,128)S(1)}, u32[]{:S(2)}) copy-start(f32[128,2048]{1,0:T(8,128)S(1)} %get-tuple-element.80) | copy-start | bytes 3145732
  133.3 70.9 %copy-start.83 = (f32[16,128]{1,0:T(8,128)}, f32[16,128]{1,0:T(8,128)S(1)}, u32[]{:S(2)}) copy-start(f32[16,128]{1,0:T(8,128)S(1)} %get-tuple-element.127) | copy-start | bytes 24580
  138.3 73.1 %copy-start.90 = (f32[16,128]{1,0:T(8,128)}, f32[16,128]{1,0:T(8,128)S(1)}, u32[]{:S(2)}) copy-start(f32[16,128]{1,0:T(8,128)S(1)} %fusion.8) | copy-start | bytes 24580
  217.5 567.6 %copy-start.9 = (f32[128,2048]{1,0:T(8,128)}, f32[128,2048]{1,0:T(8,128)S(1)}, u32[]{:S(2)}) copy-start(f32[128,2048]{1,0:T(8,128)S(1)} %get-tuple-element.130) | copy-start | bytes 3145732
  233.6 95.7 %all-to-all-start.4 = ((bf16[8,2,64,2048]{3,2,1,0:T(8,128)(2,1)}), bf16[8,2,64,2048]{3,2,1,0:T(8,128)(2,1)}, u32[]{:S(2)}, u32[]{:S(2)}) async-start(bf16[8,2,64,2048]{3,2,1,0:T(8,128)(2,1)} %bitcast.386), calls=%async_computation.4 | async-start | bytes 8388608 | tf_op jit(solution)/shard_map/all_to_all | solution.py:211
  239.8 247.4 %all-gather.16.cloned.1.call-start = ((), (), s32[]{:S(2)}) async-start(), calls=%async_computation.25 | async-start | bytes 10485760 | tf_op jit(solution)/shard_map/all_gather | solution.py:106
  329.3 130.7 %all-to-all-start = ((bf16[8,2,64,2048]{3,2,1,0:T(8,128)(2,1)}), bf16[8,2,64,2048]{3,2,1,0:T(8,128)(2,1)}, u32[]{:S(2)}, u32[]{:S(2)}) async-start(bf16[8,2,64,2048]{3,2,1,0:T(8,128)(2,1)} %bitcast.385), calls=%async_computation | async-start | bytes 8388608 | tf_op jit(solution)/shard_map/all_to_all | solution.py:167
  336.6 340.3 %all-gather.20.cloned.1.call-start = ((), (), s32[]{:S(2)}) async-start(), calls=%async_computation.27 | async-start | bytes 4718592 | tf_op jit(solution)/shard_map/all_gather | solution.py:120
  487.1 13.0 copy-start.107
  516.2 146.7 %all-to-all-start.1 = ((bf16[1,2,512,2048]{3,1,0,2:T(2,128)(2,1)}), bf16[1,2,512,2048]{3,1,0,2:T(2,128)(2,1)}, u32[]{:S(2)}, u32[]{:S(2)}) async-start(bf16[1,2,512,2048]{3,1,0,2:T(2,128)(2,1)} %copy.490), calls=%async_computation.1 | async-start | bytes 8388608 | tf_op jit(solution)/shard_map/all_to_all | solution.py:179
  524.5 162.0 %all-gather.18.cloned.1.call-start = ((), (), s32[]{:S(2)}) async-start(), calls=%async_computation.26 | async-start | bytes 4718592 | tf_op jit(solution)/shard_map/all_gather | solution.py:121
  560.5 116.3 %copy-start.43 = (bf16[128,16,64]{2,0,1:T(8,128)(2,1)S(1)}, bf16[128,16,64]{2,0,1:T(8,128)(2,1)}, u32[]{:S(2)}) copy-start(bf16[128,16,64]{2,0,1:T(8,128)(2,1)} %get-tuple-element.70) | copy-start | bytes 786436
  560.5 116.3 %copy-start.45 = (bf16[128,16,64]{2,0,1:T(8,128)(2,1)S(1)}, bf16[128,16,64]{2,0,1:T(8,128)(2,1)}, u32[]{:S(2)}) copy-start(bf16[128,16,64]{2,0,1:T(8,128)(2,1)} %get-tuple-element.71) | copy-start | bytes 786436
  662.9 97.8 %all-to-all-start.5 = ((bf16[1,2,512,2048]{3,1,0,2:T(2,128)(2,1)}), bf16[1,2,512,2048]{3,1,0,2:T(2,128)(2,1)}, u32[]{:S(2)}, u32[]{:S(2)}) async-start(bf16[1,2,512,2048]{3,1,0,2:T(2,128)(2,1)} %copy.511), calls=%async_computation.5 | async-start | bytes 8388608 | tf_op jit(solution)/shard_map/all_to_all | solution.py:235
  722.6 62.5 %copy-start.85 = (bf16[128,16]{0,1:T(8,128)(2,1)}, bf16[128,16]{0,1:T(8,128)(2,1)S(1)}, u32[]{:S(2)}) copy-start(bf16[128,16]{0,1:T(8,128)(2,1)S(1)} %multiply_convert_fusion.11) | copy-start | bytes 12292
  803.2 97.2 %all-to-all-start.6 = ((bf16[8,2,64,2048]{3,2,1,0:T(8,128)(2,1)}), bf16[8,2,64,2048]{3,2,1,0:T(8,128)(2,1)}, u32[]{:S(2)}, u32[]{:S(2)}) async-start(bf16[8,2,64,2048]{3,2,1,0:T(8,128)(2,1)} %bitcast.388), calls=%async_computation.6 | async-start | bytes 8388608 | tf_op jit(solution)/shard_map/all_to_all | solution.py:211
  900.4 97.3 %all-to-all-start.2 = ((bf16[8,2,64,2048]{3,2,1,0:T(8,128)(2,1)}), bf16[8,2,64,2048]{3,2,1,0:T(8,128)(2,1)}, u32[]{:S(2)}, u32[]{:S(2)}) async-start(bf16[8,2,64,2048]{3,2,1,0:T(8,128)(2,1)} %bitcast.387), calls=%async_computation.2 | async-start | bytes 8388608 | tf_op jit(solution)/shard_map/all_to_all | solution.py:167
  997.7 13.9 slice-start.6
  1049.4 97.1 %all-to-all-start.3 = ((bf16[1,2,512,2048]{3,1,0,2:T(2,128)(2,1)}), bf16[1,2,512,2048]{3,1,0,2:T(2,128)(2,1)}, u32[]{:S(2)}, u32[]{:S(2)}) async-start(bf16[1,2,512,2048]{3,1,0,2:T(2,128)(2,1)} %copy.507), calls=%async_computation.3 | async-start | bytes 8388608 | tf_op jit(solution)/shard_map/all_to_all | solution.py:179
  1090.3 63.6 %copy-start.106 = (f32[128]{0:T(128)S(1)}, f32[128]{0:T(128)}, u32[]{:S(2)}) copy-start(f32[128]{0:T(128)} %copy-done.105) | copy-start | bytes 1540
  1146.5 97.1 %all-to-all-start.7 = ((bf16[1,2,512,2048]{3,1,0,2:T(2,128)(2,1)}), bf16[1,2,512,2048]{3,1,0,2:T(2,128)(2,1)}, u32[]{:S(2)}, u32[]{:S(2)}) async-start(bf16[1,2,512,2048]{3,1,0,2:T(2,128)(2,1)} %copy.530), calls=%async_computation.7 | async-start | bytes 8388608 | tf_op jit(solution)/shard_map/all_to_all | solution.py:235
  1153.5 280.5 %reduce-scatter.46.cloned.1.call-start = ((), (), s32[]{:S(2)}) async-start(), calls=%async_computation.39 | async-start | bytes 4718592
  1249.7 19.6 copy-start.10
  1261.5 15.0 slice-start.4
  1292.8 181.6 %reduce-scatter.42.cloned.1.call-start = ((), (), s32[]{:S(2)}) async-start(), calls=%async_computation.37 | async-start | bytes 4718592
  1317.7 248.1 %reduce-scatter.44.cloned.1.call-start = ((), (), s32[]{:S(2)}) async-start(), calls=%async_computation.38 | async-start | bytes 4718592
  1332.3 325.2 %reduce-scatter.40.cloned.1.call-start = ((), (), s32[]{:S(2)}) async-start(), calls=%async_computation.36 | async-start | bytes 4718592
  1345.9 429.4 %reduce-scatter.48.cloned.1.call-start = ((), (), s32[]{:S(2)}) async-start(), calls=%async_computation.40 | async-start | bytes 1081344
  1348.6 524.8 %reduce-scatter.28.cloned.1.call-start = ((), (), s32[]{:S(2)}) async-start(), calls=%async_computation.30 | async-start | bytes 10485760 | tf_op jit(solution)/shard_map/reduce_scatter | solution.py:311
  1359.8 580.3 %reduce-scatter.30.cloned.1.call-start = ((), (), s32[]{:S(2)}) async-start(), calls=%async_computation.31 | async-start | bytes 10485760 | tf_op jit(solution)/shard_map/reduce_scatter | solution.py:311
  1370.8 643.6 %reduce-scatter.24.cloned.1.call-start = ((), (), s32[]{:S(2)}) async-start(), calls=%async_computation.28 | async-start | bytes 10485760 | tf_op jit(solution)/shard_map/reduce_scatter | solution.py:308
  1381.9 706.7 %reduce-scatter.26.cloned.1.call-start = ((), (), s32[]{:S(2)}) async-start(), calls=%async_computation.29 | async-start | bytes 10485760 | tf_op jit(solution)/shard_map/reduce_scatter | solution.py:308
  1392.7 770.3 %reduce-scatter.32.cloned.1.call-start = ((), (), s32[]{:S(2)}) async-start(), calls=%async_computation.32 | async-start | bytes 10485760 | tf_op jit(solution)/shard_map/reduce_scatter | solution.py:314
  1404.0 833.1 %reduce-scatter.34.cloned.1.call-start = ((), (), s32[]{:S(2)}) async-start(), calls=%async_computation.33 | async-start | bytes 10485760 | tf_op jit(solution)/shard_map/reduce_scatter | solution.py:314
  1414.7 1004.8 %reduce-scatter.38.cloned.1.call-start = ((), (), s32[]{:S(2)}) async-start(), calls=%async_computation.35 | async-start | bytes 17301504 | tf_op jit(solution)/shard_map/reduce_scatter | solution.py:301
  1426.2 1436.5 %reduce-scatter.36.cloned.1.call-start = ((), (), s32[]{:S(2)}) async-start(), calls=%async_computation.34 | async-start | bytes 51904512 | tf_op jit(solution)/shard_map/reduce_scatter | solution.py:300
  1440.6 42.8 %copy-start.63 = (f32[128,64]{1,0:T(8,128)S(1)}, f32[128,64]{1,0:T(8,128)}, u32[]{:S(2)}) copy-start(f32[128,64]{1,0:T(8,128)} %copy-done.62) | copy-start | bytes 98308
  1440.6 42.8 %copy-start.65 = (f32[128,64]{1,0:T(8,128)S(1)}, f32[128,64]{1,0:T(8,128)}, u32[]{:S(2)}) copy-start(f32[128,64]{1,0:T(8,128)} %copy-done.64) | copy-start | bytes 98308
  1504.5 155.0 %copy-start.8 = (bf16[2,128,2048]{2,1,0:T(8,128)(2,1)S(1)}, bf16[2,128,2048]{2,1,0:T(8,128)(2,1)}, u32[]{:S(2)}) copy-start(bf16[2,128,2048]{2,1,0:T(8,128)(2,1)} %param.14) | copy-start | bytes 3145732
  1504.5 155.0 %copy-start.57 = (f32[2048]{0:T(1024)S(1)}, f32[2048]{0:T(1024)}, u32[]{:S(2)}) copy-start(f32[2048]{0:T(1024)} %param.19) | copy-start | bytes 24580
  1504.5 155.0 %copy-start.93 = (f32[128]{0:T(128)S(1)}, f32[128]{0:T(128)}, u32[]{:S(2)}) copy-start(f32[128]{0:T(128)} %copy-done.92) | copy-start | bytes 1540
  1659.6 21.3 copy-start.95
  1791.6 78.6 %copy-start.102 = (f32[128]{0:T(128)S(1)}, f32[128]{0:T(128)}, u32[]{:S(2)}) copy-start(f32[128]{0:T(128)} %copy-done.101) | copy-start | bytes 1540
  1791.6 78.6 %copy-start.104 = (f32[128]{0:T(128)S(1)}, f32[128]{0:T(128)}, u32[]{:S(2)}) copy-start(f32[128]{0:T(128)} %copy-done.103) | copy-start | bytes 1540
  2088.6 774.1 %copy-start.1 = (bf16[2048,16]{0,1:T(8,128)(2,1)S(1)}, bf16[2048,16]{0,1:T(8,128)(2,1)}, u32[]{:S(2)}) copy-start(bf16[2048,16]{0,1:T(8,128)(2,1)} %param.18) | copy-start | bytes 196612
  (81 other events, 334.4 us)
Sparse Core Ops, SparseCore 0:
  54.3 74.3 all-gather.9
  131.4 72.7 all-gather.7
  205.8 57.1 all-gather.13
  264.4 58.2 all-gather.11
  324.2 58.2 all-gather.15
  385.0 95.9 all-gather.19
  527.4 129.9 all-gather.17
  1293.0 88.9 reduce-scatter.45
  1386.6 87.7 reduce-scatter.41
  1477.9 87.7 reduce-scatter.43
  1569.9 87.6 reduce-scatter.39
  1659.6 115.6 reduce-scatter.47
  1778.1 87.2 reduce-scatter.27
  1867.7 72.2 reduce-scatter.29
  1942.6 71.6 reduce-scatter.23
  2016.8 71.7 reduce-scatter.25
  2091.2 71.6 reduce-scatter.31
  2165.4 71.7 reduce-scatter.33
  2240.1 179.3 reduce-scatter.37
  2427.5 435.2 reduce-scatter.35
where the time goes:
time: 2880 us; the launch traced here: 2870 us
  waiting for transfers between devices  1950 us (68%)
  matrix products  398 us (14%)
  local copies, waits for them, and re-layouts  262 us (9%)
  other arithmetic  122 us (4%)
  blocking collectives  61.2 us (2%)
  starting transfers between devices  60.9 us (2%)
    reduce_scatter x1, waiting for transfers between devices, local(): lax.psum_scatter(qkv_term, ('expert', 'shard'), scatter_dimension=0, tile...  443 us
    unnamed x25, waiting for transfers between devices  235 us
    all_to_all x2, waiting for transfers between devices, local(): lax.all_to_all(dispatch, 'expert', split_axis=0, concat_axis=2, tiled=True)  199 us
    reduce_scatter x1, waiting for transfers between devices, local(): lax.psum_scatter(out_term, ('expert', 'shard'), scatter_dimension=0, tile...  177 us
    all_to_all x2, waiting for transfers between devices, local(): lax.all_to_all(expert_out.reshape(1, local_count, expert_axis * capacity,...  159 us
    all_to_all x2, waiting for transfers between devices, local(): lax.all_to_all(d_result.reshape(expert_axis, local_count, capacity, model...  151 us
    reduce_scatter x2, waiting for transfers between devices, local(): lax.psum_scatter(gate_term.astype(jnp.bfloat16), 'shard', scatter_dimensi...  143 us
    reduce_scatter x2, waiting for transfers between devices, local(): lax.psum_scatter(down_term.astype(jnp.bfloat16), 'shard', scatter_dimensi...  143 us
  transfers between devices with their start and end apart: 28, of which 21 were waited for; matrix products, arithmetic and copies ran while one was open for 20% of the time, Pallas kernels for 0%

commit v1 on v0

v1 whole, which is shorter than its diff:
```python
import jax
import jax.numpy as jnp
from jax import lax
from jax.sharding import PartitionSpec as P

HEAD = 128
EPS = 1e-06
ROPE_BASE = 10000.0
NEGATIVE = -1e30
LOW = jnp.bfloat16
F32 = jnp.float32


def rms_scale(values, gain_vec):
    return values * lax.rsqrt(jnp.mean(values * values, axis=-1, keepdims=True) + EPS) * gain_vec


def rotate(values, cosine, sine):
    half_size = values.shape[-1] // 2
    lower_half = values[..., :half_size]
    upper_half = values[..., half_size:]
    return jnp.concatenate(
        [lower_half * cosine - upper_half * sine, upper_half * cosine + lower_half * sine], axis=-1
    )


def places(perm_row, length_row):
    seq_ends = jnp.cumsum(length_row)
    seg_ids = jnp.sum((perm_row[:, None] >= seq_ends[None, :]).astype(jnp.int32), axis=1)
    starts = seq_ends - length_row
    pick_mask = seg_ids[:, None] == jnp.arange(length_row.shape[0], dtype=jnp.int32)[None, :]
    seq_begin = jnp.sum(jnp.where(pick_mask, starts[None, :], 0), axis=1)
    return (seg_ids, perm_row - seq_begin)


def angles(positions):
    half_size = HEAD // 2
    frequency = jnp.power(ROPE_BASE, -2.0 * jnp.arange(half_size, dtype=F32) / HEAD)
    turned = positions.astype(F32)[:, None] * frequency[None, :]
    return (jnp.cos(turned)[:, None, :], jnp.sin(turned)[:, None, :])


def head_prep(qkv_out, head_gains, cosine, sine):
    width = qkv_out.shape[1] // 3
    row_count = qkv_out.shape[0]
    query_rows = qkv_out[:, :width].reshape(row_count, width // HEAD, HEAD)
    key_rows = qkv_out[:, width : 2 * width].reshape(row_count, width // HEAD, HEAD)
    value_rows = qkv_out[:, 2 * width :].reshape(row_count, width // HEAD, HEAD)
    query_rows = rotate(rms_scale(query_rows, head_gains[:HEAD]), cosine, sine)
    key_rows = rotate(rms_scale(key_rows, head_gains[HEAD:]), cosine, sine)
    return (query_rows, key_rows, value_rows)


def swiglu(gate_in, up_in):
    return jax.nn.silu(gate_in) * up_in


def hop(value, axis, step):
    size = lax.axis_size(axis)
    return lax.ppermute(value, axis, [(i, i ^ step) for i in range(size)])


def gather_blocks(value, axis):
    size = lax.axis_size(axis)
    blocks = [None] * size
    blocks[0] = value
    for k in range(size - 2, 0, -2):
        blocks[k] = hop(value, axis, k)
    for k in [0] + list(range(size - 2, 0, -2)):
        blocks[k + 1] = hop(blocks[k], axis, 1)
    return blocks


def scatter_blocks(blocks, axis):
    size = len(blocks)
    half = {}
    for k in list(range(size - 2, 0, -2)) + [0]:
        half[k] = blocks[k].astype(F32) + hop(blocks[k + 1], axis, 1).astype(F32)
    total = half[0]
    for k in range(size - 2, 0, -2):
        total = total + hop(half[k].astype(LOW), axis, k).astype(F32)
    return total


def place_blocks(blocks, own, dim):
    size = blocks[0].shape[dim]
    shape = list(blocks[0].shape)
    shape[dim] = size * len(blocks)
    whole = jnp.zeros(shape, blocks[0].dtype)
    for k, block in enumerate(blocks):
        whole = lax.dynamic_update_slice_in_dim(whole, block, (own ^ k) * size, dim)
    return whole


def take_blocks(whole, own, count, dim):
    size = whole.shape[dim] // count
    return [lax.dynamic_slice_in_dim(whole, (own ^ k) * size, size, dim) for k in range(count)]


def swap(value, axis):
    return lax.all_to_all(value, axis, split_axis=0, concat_axis=0, tiled=True)


def dot(a, b):
    return jnp.dot(a, b, preferred_element_type=F32)


def ein(spec, a, b):
    return jnp.einsum(spec, a, b, preferred_element_type=F32)


def local(
    tokens,
    cotangent,
    qkv_weight,
    out_weight,
    router_weight,
    attn_gain,
    moe_gain,
    head_gains,
    gate_weight,
    up_weight,
    down_weight,
    permutation,
    lengths,
    routes,
):
    micro_count, rows, width = tokens.shape
    score_scale = HEAD ** (-0.5)
    n = lax.axis_size("expert")
    m = lax.axis_size("shard")
    own = lax.axis_index("expert")
    own_shard = lax.axis_index("shard")
    local_count = gate_weight.shape[0]
    expert_count = local_count * n
    top_count = routes.shape[2]
    capacity = rows * top_count // expert_count
    group = n * rows
    part = width // n
    heads = part // HEAD
    ff = gate_weight.shape[2]

    qkv_own = lax.dynamic_slice_in_dim(
        qkv_weight.reshape(width, 3, width), own * part, part, 2
    ).reshape(width, 3 * part)

    inputs = [tokens[i].astype(F32) for i in range(micro_count)]
    normed_attn = [rms_scale(x, attn_gain).astype(LOW) for x in inputs]
    normed_all = [place_blocks(gather_blocks(v, "expert"), own, 0) for v in normed_attn]

    gate_parts = gather_blocks(gate_weight, "shard")
    up_parts = gather_blocks(up_weight, "shard")
    down_parts = gather_blocks(down_weight, "shard")
    full_gate = place_blocks(gate_parts, own_shard, 1)
    full_up = place_blocks(up_parts, own_shard, 1)
    full_down = place_blocks(down_parts, own_shard, 1)

    grad_all = lax.all_gather(cotangent, "expert", axis=1, tiled=True)
    routes_all = lax.all_gather(routes, "expert", axis=0)

    own_experts = own * local_count + jnp.arange(local_count, dtype=jnp.int32)
    slot_iota = jnp.arange(capacity, dtype=jnp.int32)

    saved = []
    for i in range(micro_count):
        seg, pos = places(permutation[i, 0], lengths[i, 0])
        cosine, sine = angles(pos)
        qkv_out = dot(normed_all[i], qkv_own)
        query, key, value = head_prep(qkv_out, head_gains, cosine, sine)
        query, key, value = query.astype(LOW), key.astype(LOW), value.astype(LOW)
        same_seq = (seg[:, None] == seg[None, :])[None]
        raw = ein("qhd,khd->hqk", query, key) * score_scale
        scores = jnp.where(same_seq, raw, NEGATIVE)
        top = jnp.max(scores, axis=-1, keepdims=True)
        terms = jnp.exp(scores - top)
        total = jnp.sum(terms, axis=-1, keepdims=True)
        probs = terms / total
        log_total = top + jnp.log(total)
        attended = ein("hqk,khd->qhd", probs.astype(LOW), value).astype(LOW)
        attended = swap(attended.reshape(n, rows, part), "expert")
        attended = jnp.swapaxes(attended, 0, 1).reshape(rows, width)
        mixed = inputs[i] + dot(attended, out_weight)
        normed_moe = rms_scale(mixed, moe_gain).astype(LOW)
        saved.append(
            dict(
                cosine=cosine, sine=sine, qkv_out=qkv_out, query=query, key=key, value=value,
                same_seq=same_seq, log_total=log_total, attended=attended, mixed=mixed,
                normed_moe=normed_moe,
            )
        )

    experts = []
    for i in range(micro_count):
        normed_moe = saved[i]["normed_moe"]
        moe_all = place_blocks(gather_blocks(normed_moe, "expert"), own, 0)
        logits = dot(moe_all, router_weight)
        exp_logits = jnp.exp(logits - jnp.max(logits, axis=-1, keepdims=True))
        router = exp_logits / jnp.sum(exp_logits, axis=-1, keepdims=True)
        hit = jnp.any(
            routes_all[:, i][:, None, :, :] == own_experts[None, :, None, None], axis=-1
        )
        hot = hit.astype(jnp.int32)
        slot = jnp.cumsum(hot, axis=-1) - hot
        pick = hit[:, :, None, :] & (slot[:, :, None, :] == slot_iota[None, None, :, None])
        pick = jnp.swapaxes(pick, 0, 1)
        pick_low = pick.astype(LOW)
        own_router = lax.dynamic_slice_in_dim(router, own * local_count, local_count, 1)
        own_router = own_router.reshape(n, rows, local_count).transpose(2, 0, 1)
        gate_col = jnp.sum(jnp.where(pick, own_router[:, :, None, :], 0.0), axis=-1)
        blocks_in = moe_all.reshape(n, rows, width)
        blocks_grad = grad_all[i].reshape(n, rows, width)
        buffer = ein("ebct,btd->ebcd", pick_low, blocks_in).astype(LOW)
        buffer = buffer.reshape(local_count, n * capacity, width)
        grad_rows = ein("ebct,btd->ebcd", pick_low, blocks_grad)
        d_result = (gate_col[..., None] * grad_rows).astype(LOW)
        d_result = d_result.reshape(local_count, n * capacity, width)
        gate_act = ein("erd,edf->erf", buffer, full_gate)
        up_act = ein("erd,edf->erf", buffer, full_up)
        hidden, pull = jax.vjp(swiglu, gate_act, up_act)
        hidden = hidden.astype(LOW)
        result = ein("erf,efd->erd", hidden, full_down).astype(LOW)
        result_b = result.reshape(local_count, n, capacity, width)
        d_gate = jnp.sum(result_b.astype(F32) * grad_rows, axis=-1)
        d_gate_tok = jnp.sum(jnp.where(pick, d_gate[..., None], 0.0), axis=2)
        d_gate_tok = jnp.swapaxes(d_gate_tok, 0, 1)
        weigh = (jnp.where(pick, gate_col[..., None], 0.0)).astype(LOW)
        moe_sum = ein("ebct,ebcd->btd", weigh, result_b).astype(LOW)
        d_hidden = ein("erd,efd->erf", d_result, full_down)
        d_gate_act, d_up_act = pull(d_hidden)
        d_gate_act, d_up_act = d_gate_act.astype(LOW), d_up_act.astype(LOW)
        d_buffer = (
            ein("erf,edf->erd", d_gate_act, full_gate) + ein("erf,edf->erd", d_up_act, full_up)
        ).astype(LOW)
        d_sum = ein(
            "ebct,ebcd->btd", pick_low, d_buffer.reshape(local_count, n, capacity, width)
        ).astype(LOW)
        d_gates = swap(d_gate_tok, "expert")
        d_router = d_gates.reshape(expert_count, rows).T
        d_normed = scatter_blocks(take_blocks(d_sum.reshape(group, width), own, n, 0), "expert")
        moe_part = scatter_blocks(
            take_blocks(moe_sum.reshape(group, width), own, n, 0), "expert"
        )
        router_own = lax.dynamic_slice_in_dim(router, own * rows, rows, 0)
        experts.append(
            dict(
                buffer=buffer, hidden=hidden, d_result=d_result, d_gate_act=d_gate_act,
                d_up_act=d_up_act, d_router=d_router, d_normed=d_normed, moe_part=moe_part,
                router=router_own,
            )
        )

    both = {
        name: jnp.concatenate([x[name] for x in experts], axis=1)
        for name in ("buffer", "hidden", "d_result", "d_gate_act", "d_up_act")
    }
    gate_term = ein("erd,erf->edf", both["buffer"], both["d_gate_act"]).astype(LOW)
    up_term = ein("erd,erf->edf", both["buffer"], both["d_up_act"]).astype(LOW)
    down_term = ein("erf,erd->efd", both["hidden"], both["d_result"]).astype(LOW)
    gate_grad, up_grad, down_grad = (
        scatter_blocks(take_blocks(term, own_shard, m, 1), "shard")
        for term in (gate_term, up_term, down_term)
    )

    outputs = [
        (saved[i]["mixed"] + experts[i]["moe_part"]).astype(LOW) for i in range(micro_count)
    ]

    router_term = 0.0
    moe_gain_term = 0.0
    attn_gain_term = 0.0
    head_term = 0.0
    d_mixed_all, d_attn_all, d_qkv_all = [], [], []
    for i in range(micro_count):
        state, moe = saved[i], experts[i]
        grad_out = cotangent[i].astype(F32)
        router = moe["router"]
        d_router = moe["d_router"]
        d_logits = (
            router * (d_router - jnp.sum(router * d_router, axis=-1, keepdims=True))
        ).astype(LOW)
        d_normed = moe["d_normed"] + dot(d_logits, router_weight.T)
        router_term = router_term + dot(state["normed_moe"].T, d_logits)
        _, norm_pull = jax.vjp(rms_scale, state["mixed"], moe_gain)
        d_mixed_norm, gain_term = norm_pull(d_normed)
        moe_gain_term = moe_gain_term + gain_term
        d_mixed = grad_out + d_mixed_norm
        d_attn = d_mixed.astype(LOW)
        d_mixed_all.append(d_mixed)
        d_attn_all.append(d_attn)
        d_attended = dot(d_attn, out_weight.T).astype(LOW)
        d_attended = swap(jnp.swapaxes(d_attended.reshape(rows, n, part), 0, 1), "expert")
        d_attended = d_attended.reshape(group, heads, HEAD)
        query, key, value = state["query"], state["key"], state["value"]
        raw = ein("qhd,khd->hqk", query, key) * score_scale
        probs = jnp.exp(jnp.where(state["same_seq"], raw, NEGATIVE) - state["log_total"])
        d_probs = ein("qhd,khd->hqk", d_attended, value)
        delta = jnp.sum(probs * d_probs, axis=-1, keepdims=True)
        d_scores = (probs * (d_probs - delta)).astype(LOW)
        d_query = ein("hqk,khd->qhd", d_scores, key) * score_scale
        d_key = ein("hqk,qhd->khd", d_scores, query) * score_scale
        d_value = ein("hqk,qhd->khd", probs.astype(LOW), d_attended)
        _, head_pull = jax.vjp(
            lambda qkv_in, gains_in: head_prep(qkv_in, gains_in, state["cosine"], state["sine"]),
            state["qkv_out"],
            head_gains,
        )
        d_qkv, term = head_pull((d_query, d_key, d_value))
        head_term = head_term + term
        d_qkv = d_qkv.astype(LOW)
        d_qkv_all.append(d_qkv)
        d_qkv_rows = swap(d_qkv.reshape(n, rows, 3 * part), "expert")
        d_qkv_rows = d_qkv_rows.reshape(n, rows, 3, part).transpose(1, 2, 0, 3)
        d_normed_attn = dot(d_qkv_rows.reshape(rows, 3 * width), qkv_weight.T)
        _, attn_pull = jax.vjp(rms_scale, inputs[i], attn_gain)
        d_inputs_norm, term = attn_pull(d_normed_attn)
        attn_gain_term = attn_gain_term + term
        state["input_grad"] = (d_mixed + d_inputs_norm).astype(LOW)

    out_term = dot(
        jnp.concatenate([x["attended"] for x in saved], axis=0).T,
        jnp.concatenate(d_attn_all, axis=0),
    ).astype(LOW)
    out_grad = lax.psum_scatter(
        out_term, ("expert", "shard"), scatter_dimension=0, tiled=True
    ).astype(F32)

    qkv_term = dot(
        jnp.concatenate(normed_all, axis=0).T, jnp.concatenate(d_qkv_all, axis=0)
    ).astype(LOW)
    piece = width // (n * m)
    qkv_term = jnp.swapaxes(qkv_term.reshape(n, m, piece * 3 * part), 0, 1)
    qkv_sum = scatter_blocks(take_blocks(qkv_term, own_shard, m, 0), "shard").astype(LOW)
    qkv_rows = swap(qkv_sum.reshape(n, piece, 3 * part), "expert")
    qkv_grad = (
        qkv_rows.reshape(n, piece, 3, part).transpose(1, 2, 0, 3).reshape(piece, 3 * width)
    ).astype(F32)

    world = n * m
    head_piece = 2 * HEAD // world
    small = jnp.concatenate(
        [
            router_term.reshape(world, piece * expert_count),
            attn_gain_term.reshape(world, piece),
            moe_gain_term.reshape(world, piece),
            head_term.reshape(world, head_piece),
        ],
        axis=1,
    )
    used = small.shape[1]
    padded = -(-used // 1024) * 1024
    small = jnp.pad(small, ((0, 0), (0, padded - used))).reshape(world, padded // 128, 128)
    small = jnp.sum(swap(small, ("expert", "shard")), axis=0).reshape(padded)
    a = piece * expert_count
    return (
        jnp.stack(outputs),
        jnp.stack([x["input_grad"] for x in saved]),
        qkv_grad,
        out_grad,
        small[:a].reshape(piece, expert_count),
        small[a : a + piece],
        small[a + piece : a + 2 * piece],
        small[a + 2 * piece : a + 2 * piece + head_piece],
        gate_grad,
        up_grad,
        down_grad,
    )


def solution(mesh):
    return jax.shard_map(
        local,
        mesh=mesh,
        in_specs=(
            P(None, ("expert", "shard"), None),
            P(None, ("expert", "shard"), None),
            P(),
            P(),
            P(),
            P(),
            P(),
            P(),
            P("expert", "shard", None),
            P("expert", "shard", None),
            P("expert", "shard", None),
            P(None, "shard", None),
            P(None, "shard", None),
            P(None, ("expert", "shard"), None),
        ),
        out_specs=(
            P(None, ("expert", "shard"), None),
            P(None, ("expert", "shard"), None),
            P(("expert", "shard"), None),
            P(("expert", "shard"), None),
            P(("expert", "shard"), None),
            P(("expert", "shard")),
            P(("expert", "shard")),
            P(("expert", "shard")),
            P("expert", "shard", None),
            P("expert", "shard", None),
            P("expert", "shard", None),
        ),
        check_vma=False,
    )
```

time: 2880 us -> 1410 us (0.49)
  waiting for transfers between devices: 1950 us -> 534 us
  matrix products: 398 us -> 303 us
  starting transfers between devices: 60.9 us -> 154 us
  local copies, waits for them, and re-layouts: 262 us -> 210 us
    reduce_scatter x7 -> x0, waiting for transfers between devices: 797 us -> none  [the longest x1 443 us: local(): lax.psum_scatter(qkv_term, ('expert', 'shard'), scatter_dimension=0, tile...]
    all_to_all x8 -> x10, waiting for transfers between devices: 613 us -> 47.9 us  [swap(): return lax.all_to_all(value, axis, split_axis=0, concat_axis=0, tiled=True)]
    ppermute x0 -> x77, waiting for transfers between devices: none -> 487 us  [hop(): return lax.ppermute(value, axis, [(i, i ^ step) for i in range(size)])]
    unnamed x25 -> x2, waiting for transfers between devices: 235 us -> 0.03 us
    reduce_scatter x1, waiting for transfers between devices: 177 us -> 0.01 us  [local(): lax.psum_scatter(out_term, ('expert', 'shard'), scatter_dimension=0, tile...]
    all_gather x7 -> x1, waiting for transfers between devices: 128 us -> 0.01 us  [local(): grad_all = lax.all_gather(cotangent, 'expert', axis=1, tiled=True)]
    dot_general x48 -> x51, matrix products: 398 us -> 303 us  [the longest x35 221 us: ein(): return jnp.einsum(spec, a, b, preferred_element_type=F32)]
    ppermute x0 -> x77, starting transfers between devices: none -> 88.8 us  [hop(): return lax.ppermute(value, axis, [(i, i ^ step) for i in range(size)])]
  transfers between devices with their start and end apart: 28 -> 89, of which waited for: 21 -> 35; matrix products, arithmetic and copies ran while one was open for 20% -> 43% of each run, Pallas kernels for 0% -> 0%
where the time goes in v1:
time: 1410 us; the launch traced here: 1400 us
  waiting for transfers between devices  534 us (38%)
  matrix products  303 us (21%)
  local copies, waits for them, and re-layouts  210 us (15%)
  starting transfers between devices  154 us (11%)
  other arithmetic  131 us (9%)
  blocking collectives  55.8 us (4%)
  between operations  17.1 us (1%)
    ppermute x77, waiting for transfers between devices, hop(): return lax.ppermute(value, axis, [(i, i ^ step) for i in range(size)])  487 us
    dot_general x35, matrix products, ein(): return jnp.einsum(spec, a, b, preferred_element_type=F32)  221 us
    ppermute x77, starting transfers between devices, hop(): return lax.ppermute(value, axis, [(i, i ^ step) for i in range(size)])  88.8 us
    dot_general x16, matrix products, dot(): return jnp.dot(a, b, preferred_element_type=F32)  82 us
    all_to_all x10, starting transfers between devices, swap(): return lax.all_to_all(value, axis, split_axis=0, concat_axis=0, tiled=True)  64.7 us
    all_gather x1, blocking collectives, local(): routes_all = lax.all_gather(routes, 'expert', axis=0)  55.8 us
    unnamed x336, local copies, waits for them, and re-layouts  52.1 us
    all_to_all x10, waiting for transfers between devices, swap(): return lax.all_to_all(value, axis, split_axis=0, concat_axis=0, tiled=True)  47.9 us
  transfers between devices with their start and end apart: 89, of which 35 were waited for; matrix products, arithmetic and copies ran while one was open for 43% of the time, Pallas kernels for 0%

profile of v1, /device:TPU:8, one launch (start us, length us, event | category | flops | bytes accessed | tf_op | source)
XLA Modules:
  0.0 1404.6 jit_solution(13677553845408268791)
XLA Ops:
  24.3 55.8 %all-gather = s32[16,128,8]{1,2,0:T(8,128)S(1)} all-gather(s32[2,128,8]{1,2,0:T(8,128)S(1)} %copy-done.132), channel_id=2, replica_groups=mesh['expert'=8,'shard'=4] {'expert'}, dimensions={0}, use_global_device_ids=true | all-gather | bytes 73728 | tf_op jit(solution)/shard_map/all_gather | solution.py:159
  81.9 30.8 %copy.339 = bf16[2048,6144]{0,1:T(8,128)(2,1)} copy(bf16[2048,6144]{1,0:T(8,128)(2,1)} %param.16) | data formatting | bytes 50331648 | tf_op args[2]
  114.6 6.4 constant_dynamic-slice_fusion.26
  147.4 36.5 %collective-permute-done.3 = bf16[128,2048]{1,0:T(8,128)(2,1)S(1)} collective-permute-done((bf16[128,2048]{1,0:T(8,128)(2,1)}, bf16[128,2048]{1,0:T(8,128)(2,1)S(1)}, u32[]{:S(2)}, u32[]{:S(2)}) %collective-permute-start.3) | collective-permute-done | bytes 524320 | tf_op jit(solution)/shard_map/ppermute | solution.py:60
  185.4 10.7 collective-permute-done.5
  200.3 30.5 %collective-permute-done.33 = bf16[128,2048]{1,0:T(8,128)(2,1)S(1)} collective-permute-done((bf16[128,2048]{1,0:T(8,128)(2,1)}, bf16[128,2048]{1,0:T(8,128)(2,1)S(1)}, u32[]{:S(2)}, u32[]{:S(2)}) %collective-permute-start.33) | collective-permute-done | bytes 524320 | tf_op jit(solution)/shard_map/ppermute | solution.py:60
  256.9 6.6 collective-permute-done.36
  293.8 7.1 all-to-all-start.1
  326.4 7.3 all-to-all-done
  362.7 21.4 %collective-permute-done.18 = bf16[2,512,1024]{2,1,0:T(8,128)(2,1)S(1)} collective-permute-done((bf16[2,512,1024]{2,1,0:T(8,128)(2,1)}, bf16[2,512,1024]{2,1,0:T(8,128)(2,1)S(1)}, u32[]{:S(2)}, u32[]{:S(2)}) %collective-permute-start.18) | collective-permute-done | bytes 2097184 | tf_op jit(solution)/shard_map/ppermute | solution.py:60
  390.1 8.9 collective-permute-done.7
  412.2 9.3 collective-permute-done.41
  422.1 20.3 %collective-permute-done.10 = bf16[128,2048]{1,0:T(8,128)(2,1)S(1)} collective-permute-done((bf16[128,2048]{1,0:T(8,128)(2,1)S(1)}, bf16[128,2048]{1,0:T(8,128)(2,1)S(1)}, u32[]{:S(2)}, u32[]{:S(2)}) %collective-permute-start.10) | collective-permute-done | bytes 524320 | tf_op jit(solution)/shard_map/ppermute | solution.py:60
  444.8 12.5 collective-permute-done.11
  457.9 10.7 collective-permute-done.43
  470.6 5.7 collective-permute-done.13
  482.5 6.2 copy.407
  493.6 6.6 copy.406
  514.1 12.5 fusion.170
  526.6 10.6 multiply_convert_fusion.4
  537.2 6.0 convolution_convert_fusion.1
  543.2 6.0 fusion.168
  549.3 10.7 multiply_convert_fusion.5
  559.9 6.0 convolution_convert_fusion.2
  580.8 6.6 all-to-all-start.5
  604.7 12.5 fusion.28
  617.3 14.8 %fusion.18 = bf16[2,1024,2048]{2,1,0:T(8,128)(2,1)} fusion(bf16[2,512,2048]{2,1,0:T(8,128)(2,1)} %bitcast.378, bf16[2,512,2048]{2,1,0:T(8,128)(2,1)} %bitcast.380, bf16[2,512,1024]{2,1,0:T(8,128)(2,1)} %copy-done.150, bf16[2,512,1024]{2,1,0:T(8,128)(2,1)} %copy-done.151), kind=kOutput, calls=%fused_computation.44 | convolution fusion | flops 8619294720 | bytes 20971520 | tf_op jit(solution)/shard_map/erf,erd->efd/dot_general | solution.py:109
  632.1 15.0 %fusion.25 = (bf16[2,512,1024]{2,1,0:T(8,128)(2,1)}, bf16[2,512,1024]{2,1,0:T(8,128)(2,1)}) fusion(f32[2,512,1024]{2,1,0:T(8,128)} %fusion.168, f32[2,512,1024]{2,1,0:T(8,128)} %get-tuple-element.223, bf16[2,512,2048]{2,1,0:T(8,128)(2,1)} %bitcast.381, bf16[2,1024,2048]{2,1,0:T(8,128)(2,1)} %copy-done.44), kind=kOutput, calls=%fused_computation.49 | convolution fusion | flops 4309647360 | bytes 25165824 | tf_op jit(solution)/shard_map/erd,efd->erf/dot_general | solution.py:109
  653.6 10.6 fusion.171
  664.2 10.5 fusion.173
  674.8 11.9 fusion.22
  691.4 14.2 %fusion.21 = bf16[2,2048,1024]{2,1,0:T(8,128)(2,1)} fusion(bf16[2,512,2048]{1,2,0:T(8,128)(2,1)S(1)} %copy-done.57, bf16[2,512,2048]{1,2,0:T(8,128)(2,1)} %copy.406, bf16[2,512,1024]{2,1,0:T(8,128)(2,1)} %get-tuple-element.118, bf16[2,512,1024]{2,1,0:T(8,128)(2,1)} %get-tuple-element.116), kind=kOutput, calls=%fused_computation.45 | convolution fusion | flops 8619294720 | bytes 20971520 | tf_op jit(solution)/shard_map/erd,erf->edf/dot_general | solution.py:109
  705.6 11.4 add_convert_fusion.1
  717.0 12.9 add_convert_fusion
  744.9 6.2 all-to-all-start.2
  752.6 15.7 %all-to-all-done.2 = f32[8,2,128]{2,1,0:T(2,128)S(1)} async-done(((f32[8,2,128]{2,1,0:T(2,128)}), f32[8,2,128]{2,1,0:T(2,128)S(1)}, u32[]{:S(2)}, u32[]{:S(2)}) %all-to-all-start.2) | async-done | bytes 8224 | tf_op jit(solution)/shard_map/all_to_all | solution.py:101
  777.6 8.0 collective-permute-done.63
  787.1 9.8 collective-permute-done.61
  798.3 9.8 collective-permute-done.59
  812.7 6.6 collective-permute-done.45
  821.7 8.9 collective-permute-done.51
  837.0 7.7 collective-permute-done.53
  847.8 29.6 %collective-permute-done.55 = bf16[128,2048]{1,0:T(8,128)(2,1)S(1)} collective-permute-done((bf16[128,2048]{1,0:T(8,128)(2,1)S(1)}, bf16[128,2048]{1,0:T(8,128)(2,1)S(1)}, u32[]{:S(2)}, u32[]{:S(2)}) %collective-permute-start.55) | collective-permute-done | bytes 524320 | tf_op jit(solution)/shard_map/ppermute | solution.py:60
  878.9 17.2 %collective-permute-done.60 = bf16[128,2048]{1,0:T(8,128)(2,1)S(1)} collective-permute-done((bf16[128,2048]{1,0:T(8,128)(2,1)S(1)}, bf16[128,2048]{1,0:T(8,128)(2,1)S(1)}, u32[]{:S(2)}, u32[]{:S(2)}) %collective-permute-start.60) | collective-permute-done | bytes 524320 | tf_op jit(solution)/shard_map/ppermute | solution.py:60
  896.7 14.4 %collective-permute-done.62 = bf16[128,2048]{1,0:T(8,128)(2,1)S(1)} collective-permute-done((bf16[128,2048]{1,0:T(8,128)(2,1)S(1)}, bf16[128,2048]{1,0:T(8,128)(2,1)S(1)}, u32[]{:S(2)}, u32[]{:S(2)}) %collective-permute-start.62) | collective-permute-done | bytes 524320 | tf_op jit(solution)/shard_map/ppermute | solution.py:60
  918.7 11.0 collective-permute-done.46
  940.2 7.0 all-to-all-start.3
  948.6 6.3 convolution_convert_fusion.3
  955.7 6.0 all-to-all-start.6
  981.0 6.1 fusion.29
  1025.2 10.7 fusion.52
  1046.8 6.8 convolution_convert_fusion
  1056.8 6.3 all-to-all-start.7
  1090.3 21.1 %all-to-all-done.7 = bf16[8,128,768]{1,2,0:T(8,128)(2,1)} async-done(((bf16[8,128,768]{1,2,0:T(8,128)(2,1)}), bf16[8,128,768]{1,2,0:T(8,128)(2,1)}, u32[]{:S(2)}, u32[]{:S(2)}) %all-to-all-start.7) | async-done | bytes 1572896 | tf_op jit(solution)/shard_map/all_to_all | solution.py:101
  1111.4 6.6 all-to-all-start.4
  1118.0 109.5 %collective-permute-done.67 = bf16[1,8,49152]{2,0,1:T(2,128)(2,1)} collective-permute-done((bf16[1,8,49152]{2,0,1:T(2,128)(2,1)}, bf16[1,8,49152]{2,0,1:T(2,128)(2,1)}, u32[]{:S(2)}, u32[]{:S(2)}) %collective-permute-start.67) | collective-permute-done | bytes 786464 | tf_op jit(solution)/shard_map/ppermute | solution.py:60
  1233.9 8.1 fusion.61
  1252.5 27.9 %collective-permute-done.70 = bf16[2,512,1024]{2,1,0:T(8,128)(2,1)} collective-permute-done((bf16[2,512,1024]{2,1,0:T(8,128)(2,1)}, bf16[2,512,1024]{2,1,0:T(8,128)(2,1)}, u32[]{:S(2)}, u32[]{:S(2)}) %collective-permute-start.70) | collective-permute-done | bytes 2097184 | tf_op jit(solution)/shard_map/ppermute | solution.py:60
  1280.8 6.3 convert_add_fusion.2
  1290.6 34.1 %collective-permute-done.76 = bf16[2,256,2048]{2,1,0:T(8,128)(2,1)} collective-permute-done((bf16[2,256,2048]{2,1,0:T(8,128)(2,1)}, bf16[2,256,2048]{2,1,0:T(8,128)(2,1)}, u32[]{:S(2)}, u32[]{:S(2)}) %collective-permute-start.76) | collective-permute-done | bytes 2097184 | tf_op jit(solution)/shard_map/ppermute | solution.py:60
  1324.7 6.1 convert_add_fusion
  1332.3 8.8 all-to-all-start.8
  1343.8 14.3 %fusion.175 = f32[128,2048]{1,0:T(8,128)} fusion(bf16[128,6144]{0,1:T(8,128)(2,1)S(1)} %bitcast.354, bf16[2048,6144]{1,0:T(8,128)(2,1)} %param.16), kind=kOutput, calls=%fused_computation.442 | convolution fusion | flops 3221225472 | bytes 27787264 | tf_op jit(solution)/shard_map/dot_general | solution.py:105
  1358.2 14.8 %fusion.75 = (f32[2048]{0:T(1024)S(1)}, f32[128]{0:T(128)S(1)}, f32[128]{0:T(128)S(1)}, f32[2048]{0:T(1024)S(1)}, f32[128,2048]{1,0:T(8,128)}) fusion(f32[128]{0:T(128)S(1)} %copy-done.127, bf16[2,128,2048]{2,1,0:T(8,128)(2,1)S(1)} %copy-done.20, f32[2048]{0:T(1024)S(1)} %copy-done.105, f32[128,2048]{1,0:T(8,128)} %fusion.175, f32[128]{0:T(128)S(1)} %copy-done.125, ...), kind=kOutput, calls=%fused_computation.146 | convolution fusion | flops 3224891392 | bytes 29911040 | tf_op jit(solution)/shard_map/dot_general | solution.py:105
  (714 shorter events, 470.5 us)
Async XLA Ops:
  7.2 558.8 %all-gather.3.cloned.1.call-start = ((), (), s32[]{:S(2)}) async-start(), calls=%async_computation.11 | async-start | bytes 9437184 | tf_op jit(solution)/shard_map/all_gather | solution.py:158
  12.6 134.8 %collective-permute-start.31 = (bf16[128,2048]{1,0:T(8,128)(2,1)}, bf16[128,2048]{1,0:T(8,128)(2,1)S(1)}, u32[]{:S(2)}, u32[]{:S(2)}) collective-permute-start(bf16[128,2048]{1,0:T(8,128)(2,1)} %get-tuple-element.109), channel_id=1, source_target_pairs={{0,8},{4,12},{8,0},{12,4},{16,24},{20,28},{24,16},{28,20},{1,9},{5... | collective-permute-start | bytes 1572872 | tf_op jit(solution)/shard_map/ppermute | solution.py:60
  12.6 127.7 %collective-permute-start.30 = (bf16[128,2048]{1,0:T(8,128)(2,1)}, bf16[128,2048]{1,0:T(8,128)(2,1)S(1)}, u32[]{:S(2)}, u32[]{:S(2)}) collective-permute-start(bf16[128,2048]{1,0:T(8,128)(2,1)} %get-tuple-element.109), channel_id=1, source_target_pairs={{0,4},{4,0},{8,12},{12,8},{16,20},{20,16},{24,28},{28,24},{1,5},{5... | collective-permute-start | bytes 1572872 | tf_op jit(solution)/shard_map/ppermute | solution.py:60
  18.3 125.2 %collective-permute-start.1 = (bf16[128,2048]{1,0:T(8,128)(2,1)}, bf16[128,2048]{1,0:T(8,128)(2,1)S(1)}, u32[]{:S(2)}, u32[]{:S(2)}) collective-permute-start(bf16[128,2048]{1,0:T(8,128)(2,1)} %get-tuple-element.103), channel_id=1, source_target_pairs={{0,8},{4,12},{8,0},{12,4},{16,24},{20,28},{24,16},{28,20},{1,9},{5... | collective-permute-start | bytes 1572872 | tf_op jit(solution)/shard_map/ppermute | solution.py:60
  19.9 125.9 %collective-permute-start = (bf16[128,2048]{1,0:T(8,128)(2,1)}, bf16[128,2048]{1,0:T(8,128)(2,1)S(1)}, u32[]{:S(2)}, u32[]{:S(2)}) collective-permute-start(bf16[128,2048]{1,0:T(8,128)(2,1)} %get-tuple-element.103), channel_id=1, source_target_pairs={{0,4},{4,0},{8,12},{12,8},{16,20},{20,16},{24,28},{28,24},{1,5},{5... | collective-permute-start | bytes 1572872 | tf_op jit(solution)/shard_map/ppermute | solution.py:60
  20.4 333.6 %collective-permute-start.15 = (bf16[2,512,1024]{2,1,0:T(8,128)(2,1)}, bf16[2,512,1024]{2,1,0:T(8,128)(2,1)}, u32[]{:S(2)}, u32[]{:S(2)}) collective-permute-start(bf16[2,512,1024]{2,1,0:T(8,128)(2,1)} %param.22), channel_id=1, source_target_pairs={{0,2},{1,3},{2,0},{3,1},{4,6},{5,7},{6,4},{7,5},{8,10},{9,11},{10,... | collective-permute-start | bytes 6291464 | tf_op jit(solution)/shard_map/ppermute | solution.py:60
  140.4 43.5 %collective-permute-start.3 = (bf16[128,2048]{1,0:T(8,128)(2,1)}, bf16[128,2048]{1,0:T(8,128)(2,1)S(1)}, u32[]{:S(2)}, u32[]{:S(2)}) collective-permute-start(bf16[128,2048]{1,0:T(8,128)(2,1)} %get-tuple-element.103), channel_id=1, source_target_pairs={{0,16},{4,20},{8,24},{12,28},{16,0},{20,4},{24,8},{28,12},{1,17},{... | collective-permute-start | bytes 1572872 | tf_op jit(solution)/shard_map/ppermute | solution.py:60
  143.5 52.5 %collective-permute-start.5 = (bf16[128,2048]{1,0:T(8,128)(2,1)}, bf16[128,2048]{1,0:T(8,128)(2,1)S(1)}, u32[]{:S(2)}, u32[]{:S(2)}) collective-permute-start(bf16[128,2048]{1,0:T(8,128)(2,1)} %get-tuple-element.103), channel_id=1, source_target_pairs={{0,24},{4,28},{8,16},{12,20},{16,8},{20,12},{24,0},{28,4},{1,25},{... | collective-permute-start | bytes 1572872 | tf_op jit(solution)/shard_map/ppermute | solution.py:60
  145.8 50.3 %collective-permute-start.2 = (bf16[128,2048]{1,0:T(8,128)(2,1)S(1)}, bf16[128,2048]{1,0:T(8,128)(2,1)S(1)}, u32[]{:S(2)}, u32[]{:S(2)}) collective-permute-start(bf16[128,2048]{1,0:T(8,128)(2,1)S(1)} %collective-permute-done.1), channel_id=1, source_target_pairs={{0,4},{4,0},{8,12},{12,8},{16,20},{20,16},{24,28},{28,24},{1,5},{5... | collective-permute-start | bytes 1572872 | tf_op jit(solution)/shard_map/ppermute | solution.py:60
  147.4 191.2 %collective-permute-start.14 = (bf16[2,512,1024]{2,1,0:T(8,128)(2,1)}, bf16[2,512,1024]{2,1,0:T(8,128)(2,1)}, u32[]{:S(2)}, u32[]{:S(2)}) collective-permute-start(bf16[2,512,1024]{2,1,0:T(8,128)(2,1)} %param.22), channel_id=1, source_target_pairs={{0,1},{1,0},{2,3},{3,2},{4,5},{5,4},{6,7},{7,6},{8,9},{9,8},{10,11... | collective-permute-start | bytes 6291464 | tf_op jit(solution)/shard_map/ppermute | solution.py:60
  196.0 34.8 %collective-permute-start.33 = (bf16[128,2048]{1,0:T(8,128)(2,1)}, bf16[128,2048]{1,0:T(8,128)(2,1)S(1)}, u32[]{:S(2)}, u32[]{:S(2)}) collective-permute-start(bf16[128,2048]{1,0:T(8,128)(2,1)} %get-tuple-element.109), channel_id=1, source_target_pairs={{0,16},{4,20},{8,24},{12,28},{16,0},{20,4},{24,8},{28,12},{1,17},{... | collective-permute-start | bytes 1572872 | tf_op jit(solution)/shard_map/ppermute | solution.py:60
  196.0 35.0 %collective-permute-start.6 = (bf16[128,2048]{1,0:T(8,128)(2,1)S(1)}, bf16[128,2048]{1,0:T(8,128)(2,1)S(1)}, u32[]{:S(2)}, u32[]{:S(2)}) collective-permute-start(bf16[128,2048]{1,0:T(8,128)(2,1)S(1)} %collective-permute-done.5), channel_id=1, source_target_pairs={{0,4},{4,0},{8,12},{12,8},{16,20},{20,16},{24,28},{28,24},{1,5},{5... | collective-permute-start | bytes 1572872 | tf_op jit(solution)/shard_map/ppermute | solution.py:60
  198.2 49.1 %collective-permute-start.35 = (bf16[128,2048]{1,0:T(8,128)(2,1)}, bf16[128,2048]{1,0:T(8,128)(2,1)S(1)}, u32[]{:S(2)}, u32[]{:S(2)}) collective-permute-start(bf16[128,2048]{1,0:T(8,128)(2,1)} %get-tuple-element.109), channel_id=1, source_target_pairs={{0,24},{4,28},{8,16},{12,20},{16,8},{20,12},{24,0},{28,4},{1,25},{... | collective-permute-start | bytes 1572872 | tf_op jit(solution)/shard_map/ppermute | solution.py:60
  245.7 99.3 %collective-permute-start.17 = (bf16[2,512,1024]{2,1,0:T(8,128)(2,1)}, bf16[2,512,1024]{2,1,0:T(8,128)(2,1)}, u32[]{:S(2)}, u32[]{:S(2)}) collective-permute-start(bf16[2,512,1024]{2,1,0:T(8,128)(2,1)} %param.23), channel_id=1, source_target_pairs={{0,1},{1,0},{2,3},{3,2},{4,5},{5,4},{6,7},{7,6},{8,9},{9,8},{10,11... | collective-permute-start | bytes 6291464 | tf_op jit(solution)/shard_map/ppermute | solution.py:60
  247.3 111.3 %collective-permute-start.21 = (bf16[2,256,2048]{2,1,0:T(8,128)(2,1)}, bf16[2,256,2048]{2,1,0:T(8,128)(2,1)}, u32[]{:S(2)}, u32[]{:S(2)}) collective-permute-start(bf16[2,256,2048]{2,1,0:T(8,128)(2,1)} %param.24), channel_id=1, source_target_pairs={{0,2},{1,3},{2,0},{3,1},{4,6},{5,7},{6,4},{7,5},{8,10},{9,11},{10,... | collective-permute-start | bytes 6291464 | tf_op jit(solution)/shard_map/ppermute | solution.py:60
  263.5 84.6 %collective-permute-start.20 = (bf16[2,256,2048]{2,1,0:T(8,128)(2,1)}, bf16[2,256,2048]{2,1,0:T(8,128)(2,1)}, u32[]{:S(2)}, u32[]{:S(2)}) collective-permute-start(bf16[2,256,2048]{2,1,0:T(8,128)(2,1)} %param.24), channel_id=1, source_target_pairs={{0,1},{1,0},{2,3},{3,2},{4,5},{5,4},{6,7},{7,6},{8,9},{9,8},{10,11... | collective-permute-start | bytes 6291464 | tf_op jit(solution)/shard_map/ppermute | solution.py:60
  338.7 45.4 %collective-permute-start.18 = (bf16[2,512,1024]{2,1,0:T(8,128)(2,1)}, bf16[2,512,1024]{2,1,0:T(8,128)(2,1)S(1)}, u32[]{:S(2)}, u32[]{:S(2)}) collective-permute-start(bf16[2,512,1024]{2,1,0:T(8,128)(2,1)} %param.23), channel_id=1, source_target_pairs={{0,2},{1,3},{2,0},{3,1},{4,6},{5,7},{6,4},{7,5},{8,10},{9,11},{10,... | collective-permute-start | bytes 6291464 | tf_op jit(solution)/shard_map/ppermute | solution.py:60
  345.0 76.6 %collective-permute-start.42 = (bf16[128,2048]{1,0:T(8,128)(2,1)S(1)}, bf16[128,2048]{1,0:T(8,128)(2,1)S(1)}, u32[]{:S(2)}, u32[]{:S(2)}) collective-permute-start(bf16[128,2048]{1,0:T(8,128)(2,1)S(1)} %get-tuple-element.107), channel_id=1, source_target_pairs={{0,24},{4,28},{8,16},{12,20},{16,8},{20,12},{24,0},{28,4},{1,25},{... | collective-permute-start | bytes 1572872 | tf_op jit(solution)/shard_map/ppermute | solution.py:60
  348.1 39.4 %collective-permute-start.38 = (bf16[128,2048]{1,0:T(8,128)(2,1)S(1)}, bf16[128,2048]{1,0:T(8,128)(2,1)S(1)}, u32[]{:S(2)}, u32[]{:S(2)}) collective-permute-start(bf16[128,2048]{1,0:T(8,128)(2,1)S(1)} %get-tuple-element.107), channel_id=1, source_target_pairs={{0,8},{4,12},{8,0},{12,4},{16,24},{20,28},{24,16},{28,20},{1,9},{5... | collective-permute-start | bytes 1572872 | tf_op jit(solution)/shard_map/ppermute | solution.py:60
  354.0 35.9 %collective-permute-start.37 = (bf16[128,2048]{1,0:T(8,128)(2,1)S(1)}, bf16[128,2048]{1,0:T(8,128)(2,1)S(1)}, u32[]{:S(2)}, u32[]{:S(2)}) collective-permute-start(bf16[128,2048]{1,0:T(8,128)(2,1)S(1)} %get-tuple-element.107), channel_id=1, source_target_pairs={{0,4},{4,0},{8,12},{12,8},{16,20},{20,16},{24,28},{28,24},{1,5},{5... | collective-permute-start | bytes 1572872 | tf_op jit(solution)/shard_map/ppermute | solution.py:60
  358.6 42.7 %collective-permute-start.40 = (bf16[128,2048]{1,0:T(8,128)(2,1)S(1)}, bf16[128,2048]{1,0:T(8,128)(2,1)S(1)}, u32[]{:S(2)}, u32[]{:S(2)}) collective-permute-start(bf16[128,2048]{1,0:T(8,128)(2,1)S(1)} %get-tuple-element.107), channel_id=1, source_target_pairs={{0,16},{4,20},{8,24},{12,28},{16,0},{20,4},{24,8},{28,12},{1,17},{... | collective-permute-start | bytes 1572872 | tf_op jit(solution)/shard_map/ppermute | solution.py:60
  399.0 45.7 %collective-permute-start.12 = (bf16[128,2048]{1,0:T(8,128)(2,1)S(1)}, bf16[128,2048]{1,0:T(8,128)(2,1)S(1)}, u32[]{:S(2)}, u32[]{:S(2)}) collective-permute-start(bf16[128,2048]{1,0:T(8,128)(2,1)S(1)} %get-tuple-element.101), channel_id=1, source_target_pairs={{0,24},{4,28},{8,16},{12,20},{16,8},{20,12},{24,0},{28,4},{1,25},{... | collective-permute-start | bytes 1572872 | tf_op jit(solution)/shard_map/ppermute | solution.py:60
  401.3 41.1 %collective-permute-start.10 = (bf16[128,2048]{1,0:T(8,128)(2,1)S(1)}, bf16[128,2048]{1,0:T(8,128)(2,1)S(1)}, u32[]{:S(2)}, u32[]{:S(2)}) collective-permute-start(bf16[128,2048]{1,0:T(8,128)(2,1)S(1)} %get-tuple-element.101), channel_id=1, source_target_pairs={{0,16},{4,20},{8,24},{12,28},{16,0},{20,4},{24,8},{28,12},{1,17},{... | collective-permute-start | bytes 1572872 | tf_op jit(solution)/shard_map/ppermute | solution.py:60
  410.2 32.7 %collective-permute-start.9 = (bf16[128,2048]{1,0:T(8,128)(2,1)S(1)}, bf16[128,2048]{1,0:T(8,128)(2,1)S(1)}, u32[]{:S(2)}, u32[]{:S(2)}) collective-permute-start(bf16[128,2048]{1,0:T(8,128)(2,1)S(1)} %collective-permute-done.8), channel_id=1, source_target_pairs={{0,4},{4,0},{8,12},{12,8},{16,20},{20,16},{24,28},{28,24},{1,5},{5... | collective-permute-start | bytes 1572872 | tf_op jit(solution)/shard_map/ppermute | solution.py:60
  421.5 84.3 %collective-permute-start.16 = (bf16[2,512,1024]{2,1,0:T(8,128)(2,1)}, bf16[2,512,1024]{2,1,0:T(8,128)(2,1)}, u32[]{:S(2)}, u32[]{:S(2)}) collective-permute-start(bf16[2,512,1024]{2,1,0:T(8,128)(2,1)} %collective-permute-done.15), channel_id=1, source_target_pairs={{0,1},{1,0},{2,3},{3,2},{4,5},{5,4},{6,7},{7,6},{8,9},{9,8},{10,11... | collective-permute-start | bytes 6291464 | tf_op jit(solution)/shard_map/ppermute | solution.py:60
  421.5 87.4 %collective-permute-start.19 = (bf16[2,512,1024]{2,1,0:T(8,128)(2,1)S(1)}, bf16[2,512,1024]{2,1,0:T(8,128)(2,1)}, u32[]{:S(2)}, u32[]{:S(2)}) collective-permute-start(bf16[2,512,1024]{2,1,0:T(8,128)(2,1)S(1)} %collective-permute-done.18), channel_id=1, source_target_pairs={{0,1},{1,0},{2,3},{3,2},{4,5},{5,4},{6,7},{7,6},{8,9},{9,8},{10,11... | collective-permute-start | bytes 6291464 | tf_op jit(solution)/shard_map/ppermute | solution.py:60
  444.7 67.5 %collective-permute-start.22 = (bf16[2,256,2048]{2,1,0:T(8,128)(2,1)}, bf16[2,256,2048]{2,1,0:T(8,128)(2,1)}, u32[]{:S(2)}, u32[]{:S(2)}) collective-permute-start(bf16[2,256,2048]{2,1,0:T(8,128)(2,1)} %collective-permute-done.21), channel_id=1, source_target_pairs={{0,1},{1,0},{2,3},{3,2},{4,5},{5,4},{6,7},{7,6},{8,9},{9,8},{10,11... | collective-permute-start | bytes 6291464 | tf_op jit(solution)/shard_map/ppermute | solution.py:60
  580.8 164.1 %all-to-all-start.5 = ((f32[8,2,128]{2,1,0:T(2,128)}), f32[8,2,128]{2,1,0:T(2,128)}, u32[]{:S(2)}, u32[]{:S(2)}) async-start(f32[8,2,128]{2,1,0:T(2,128)} %bitcast.92), calls=%async_computation.5 | async-start | bytes 16384 | tf_op jit(solution)/shard_map/all_to_all | solution.py:101
  590.4 186.3 %collective-permute-start.49 = (bf16[128,2048]{1,0:T(8,128)(2,1)}, bf16[128,2048]{1,0:T(8,128)(2,1)}, u32[]{:S(2)}, u32[]{:S(2)}) collective-permute-start(bf16[128,2048]{1,0:T(8,128)(2,1)} %get-tuple-element.144), channel_id=1, source_target_pairs={{0,4},{4,0},{8,12},{12,8},{16,20},{20,16},{24,28},{28,24},{1,5},{5... | collective-permute-start | bytes 1572872 | tf_op jit(solution)/shard_map/ppermute | solution.py:60
  591.9 218.4 %collective-permute-start.47 = (bf16[128,2048]{1,0:T(8,128)(2,1)}, bf16[128,2048]{1,0:T(8,128)(2,1)}, u32[]{:S(2)}, u32[]{:S(2)}) collective-permute-start(bf16[128,2048]{1,0:T(8,128)(2,1)} %get-tuple-element.145), channel_id=1, source_target_pairs={{0,4},{4,0},{8,12},{12,8},{16,20},{20,16},{24,28},{28,24},{1,5},{5... | collective-permute-start | bytes 1572872 | tf_op jit(solution)/shard_map/ppermute | solution.py:60
  736.0 36.3 %collective-permute-start.54 = (bf16[128,2048]{1,0:T(8,128)(2,1)}, bf16[128,2048]{1,0:T(8,128)(2,1)}, u32[]{:S(2)}, u32[]{:S(2)}) collective-permute-start(bf16[128,2048]{1,0:T(8,128)(2,1)} %get-tuple-element.124), channel_id=1, source_target_pairs={{0,4},{4,0},{8,12},{12,8},{16,20},{20,16},{24,28},{28,24},{1,5},{5... | collective-permute-start | bytes 1572872 | tf_op jit(solution)/shard_map/ppermute | solution.py:60
  742.9 27.8 %collective-permute-start.56 = (bf16[128,2048]{1,0:T(8,128)(2,1)}, bf16[128,2048]{1,0:T(8,128)(2,1)}, u32[]{:S(2)}, u32[]{:S(2)}) collective-permute-start(bf16[128,2048]{1,0:T(8,128)(2,1)} %get-tuple-element.123), channel_id=1, source_target_pairs={{0,4},{4,0},{8,12},{12,8},{16,20},{20,16},{24,28},{28,24},{1,5},{5... | collective-permute-start | bytes 1572872 | tf_op jit(solution)/shard_map/ppermute | solution.py:60
  744.3 28.5 %collective-permute-start.52 = (bf16[128,2048]{1,0:T(8,128)(2,1)}, bf16[128,2048]{1,0:T(8,128)(2,1)}, u32[]{:S(2)}, u32[]{:S(2)}) collective-permute-start(bf16[128,2048]{1,0:T(8,128)(2,1)} %get-tuple-element.125), channel_id=1, source_target_pairs={{0,4},{4,0},{8,12},{12,8},{16,20},{20,16},{24,28},{28,24},{1,5},{5... | collective-permute-start | bytes 1572872 | tf_op jit(solution)/shard_map/ppermute | solution.py:60
  772.8 35.3 %collective-permute-start.59 = (bf16[128,2048]{1,0:T(8,128)(2,1)S(1)}, bf16[128,2048]{1,0:T(8,128)(2,1)S(1)}, u32[]{:S(2)}, u32[]{:S(2)}) collective-permute-start(bf16[128,2048]{1,0:T(8,128)(2,1)S(1)} %get-tuple-element.132), channel_id=1, source_target_pairs={{0,4},{4,0},{8,12},{12,8},{16,20},{20,16},{24,28},{28,24},{1,5},{5... | collective-permute-start | bytes 1572872 | tf_op jit(solution)/shard_map/ppermute | solution.py:60
  776.7 42.6 %collective-permute-start.45 = (bf16[128,2048]{1,0:T(8,128)(2,1)S(1)}, bf16[128,2048]{1,0:T(8,128)(2,1)S(1)}, u32[]{:S(2)}, u32[]{:S(2)}) collective-permute-start(bf16[128,2048]{1,0:T(8,128)(2,1)S(1)} %copy-done.99), channel_id=1, source_target_pairs={{0,4},{4,0},{8,12},{12,8},{16,20},{20,16},{24,28},{28,24},{1,5},{5... | collective-permute-start | bytes 1572872 | tf_op jit(solution)/shard_map/ppermute | solution.py:60
  785.6 44.9 %collective-permute-start.51 = (bf16[128,2048]{1,0:T(8,128)(2,1)S(1)}, bf16[128,2048]{1,0:T(8,128)(2,1)S(1)}, u32[]{:S(2)}, u32[]{:S(2)}) collective-permute-start(bf16[128,2048]{1,0:T(8,128)(2,1)S(1)} %get-tuple-element.122), channel_id=1, source_target_pairs={{0,4},{4,0},{8,12},{12,8},{16,20},{20,16},{24,28},{28,24},{1,5},{5... | collective-permute-start | bytes 1572872 | tf_op jit(solution)/shard_map/ppermute | solution.py:60
  796.8 39.8 %collective-permute-start.58 = (bf16[128,2048]{1,0:T(8,128)(2,1)S(1)}, bf16[128,2048]{1,0:T(8,128)(2,1)S(1)}, u32[]{:S(2)}, u32[]{:S(2)}) collective-permute-start(bf16[128,2048]{1,0:T(8,128)(2,1)S(1)} %get-tuple-element.129), channel_id=1, source_target_pairs={{0,4},{4,0},{8,12},{12,8},{16,20},{20,16},{24,28},{28,24},{1,5},{5... | collective-permute-start | bytes 1572872 | tf_op jit(solution)/shard_map/ppermute | solution.py:60
  808.1 36.6 %collective-permute-start.53 = (bf16[128,2048]{1,0:T(8,128)(2,1)S(1)}, bf16[128,2048]{1,0:T(8,128)(2,1)S(1)}, u32[]{:S(2)}, u32[]{:S(2)}) collective-permute-start(bf16[128,2048]{1,0:T(8,128)(2,1)S(1)} %get-tuple-element.126), channel_id=1, source_target_pairs={{0,24},{4,28},{8,16},{12,20},{16,8},{20,12},{24,0},{28,4},{1,25},{... | collective-permute-start | bytes 1572872 | tf_op jit(solution)/shard_map/ppermute | solution.py:60
  810.3 36.3 %collective-permute-start.57 = (bf16[128,2048]{1,0:T(8,128)(2,1)S(1)}, bf16[128,2048]{1,0:T(8,128)(2,1)S(1)}, u32[]{:S(2)}, u32[]{:S(2)}) collective-permute-start(bf16[128,2048]{1,0:T(8,128)(2,1)S(1)} %get-tuple-element.127), channel_id=1, source_target_pairs={{0,8},{4,12},{8,0},{12,4},{16,24},{20,28},{24,16},{28,20},{1,9},{5... | collective-permute-start | bytes 1572872 | tf_op jit(solution)/shard_map/ppermute | solution.py:60
  819.3 58.1 %collective-permute-start.55 = (bf16[128,2048]{1,0:T(8,128)(2,1)S(1)}, bf16[128,2048]{1,0:T(8,128)(2,1)S(1)}, u32[]{:S(2)}, u32[]{:S(2)}) collective-permute-start(bf16[128,2048]{1,0:T(8,128)(2,1)S(1)} %get-tuple-element.128), channel_id=1, source_target_pairs={{0,16},{4,20},{8,24},{12,28},{16,0},{20,4},{24,8},{28,12},{1,17},{... | collective-permute-start | bytes 1572872 | tf_op jit(solution)/shard_map/ppermute | solution.py:60
  830.6 65.5 %collective-permute-start.60 = (bf16[128,2048]{1,0:T(8,128)(2,1)S(1)}, bf16[128,2048]{1,0:T(8,128)(2,1)S(1)}, u32[]{:S(2)}, u32[]{:S(2)}) collective-permute-start(bf16[128,2048]{1,0:T(8,128)(2,1)S(1)} %get-tuple-element.133), channel_id=1, source_target_pairs={{0,24},{4,28},{8,16},{12,20},{16,8},{20,12},{24,0},{28,4},{1,25},{... | collective-permute-start | bytes 1572872 | tf_op jit(solution)/shard_map/ppermute | solution.py:60
  836.6 60.1 %collective-permute-start.64 = (bf16[128,2048]{1,0:T(8,128)(2,1)S(1)}, bf16[128,2048]{1,0:T(8,128)(2,1)S(1)}, u32[]{:S(2)}, u32[]{:S(2)}) collective-permute-start(bf16[128,2048]{1,0:T(8,128)(2,1)S(1)} %get-tuple-element.134), channel_id=1, source_target_pairs={{0,8},{4,12},{8,0},{12,4},{16,24},{20,28},{24,16},{28,20},{1,9},{5... | collective-permute-start | bytes 1572872 | tf_op jit(solution)/shard_map/ppermute | solution.py:60
  844.7 66.4 %collective-permute-start.62 = (bf16[128,2048]{1,0:T(8,128)(2,1)S(1)}, bf16[128,2048]{1,0:T(8,128)(2,1)S(1)}, u32[]{:S(2)}, u32[]{:S(2)}) collective-permute-start(bf16[128,2048]{1,0:T(8,128)(2,1)S(1)} %get-tuple-element.135), channel_id=1, source_target_pairs={{0,16},{4,20},{8,24},{12,28},{16,0},{20,4},{24,8},{28,12},{1,17},{... | collective-permute-start | bytes 1572872 | tf_op jit(solution)/shard_map/ppermute | solution.py:60
  846.5 70.6 %collective-permute-start.44 = (bf16[128,2048]{1,0:T(8,128)(2,1)S(1)}, bf16[128,2048]{1,0:T(8,128)(2,1)S(1)}, u32[]{:S(2)}, u32[]{:S(2)}) collective-permute-start(bf16[128,2048]{1,0:T(8,128)(2,1)S(1)} %copy-done.98), channel_id=1, source_target_pairs={{0,4},{4,0},{8,12},{12,8},{16,20},{20,16},{24,28},{28,24},{1,5},{5... | collective-permute-start | bytes 1572872 | tf_op jit(solution)/shard_map/ppermute | solution.py:60
  877.4 193.9 %collective-permute-start.28 = (bf16[128,2048]{1,0:T(8,128)(2,1)}, bf16[128,2048]{1,0:T(8,128)(2,1)}, u32[]{:S(2)}, u32[]{:S(2)}) collective-permute-start(bf16[128,2048]{1,0:T(8,128)(2,1)} %get-tuple-element.137), channel_id=1, source_target_pairs={{0,4},{4,0},{8,12},{12,8},{16,20},{20,16},{24,28},{28,24},{1,5},{5... | collective-permute-start | bytes 1572872 | tf_op jit(solution)/shard_map/ppermute | solution.py:60
  896.1 33.6 %collective-permute-start.46 = (bf16[128,2048]{1,0:T(8,128)(2,1)S(1)}, bf16[128,2048]{1,0:T(8,128)(2,1)S(1)}, u32[]{:S(2)}, u32[]{:S(2)}) collective-permute-start(bf16[128,2048]{1,0:T(8,128)(2,1)S(1)} %get-tuple-element.147), channel_id=1, source_target_pairs={{0,24},{4,28},{8,16},{12,20},{16,8},{20,12},{24,0},{28,4},{1,25},{... | collective-permute-start | bytes 1572872 | tf_op jit(solution)/shard_map/ppermute | solution.py:60
  896.7 34.5 %collective-permute-start.50 = (bf16[128,2048]{1,0:T(8,128)(2,1)S(1)}, bf16[128,2048]{1,0:T(8,128)(2,1)S(1)}, u32[]{:S(2)}, u32[]{:S(2)}) collective-permute-start(bf16[128,2048]{1,0:T(8,128)(2,1)S(1)} %get-tuple-element.148), channel_id=1, source_target_pairs={{0,8},{4,12},{8,0},{12,4},{16,24},{20,28},{24,16},{28,20},{1,9},{5... | collective-permute-start | bytes 1572872 | tf_op jit(solution)/shard_map/ppermute | solution.py:60
  917.2 159.8 %collective-permute-start.26 = (bf16[128,2048]{1,0:T(8,128)(2,1)}, bf16[128,2048]{1,0:T(8,128)(2,1)}, u32[]{:S(2)}, u32[]{:S(2)}) collective-permute-start(bf16[128,2048]{1,0:T(8,128)(2,1)} %get-tuple-element.138), channel_id=1, source_target_pairs={{0,4},{4,0},{8,12},{12,8},{16,20},{20,16},{24,28},{28,24},{1,5},{5... | collective-permute-start | bytes 1572872 | tf_op jit(solution)/shard_map/ppermute | solution.py:60
  929.7 147.7 %collective-permute-start.24 = (bf16[128,2048]{1,0:T(8,128)(2,1)}, bf16[128,2048]{1,0:T(8,128)(2,1)}, u32[]{:S(2)}, u32[]{:S(2)}) collective-permute-start(bf16[128,2048]{1,0:T(8,128)(2,1)} %get-tuple-element.139), channel_id=1, source_target_pairs={{0,4},{4,0},{8,12},{12,8},{16,20},{20,16},{24,28},{28,24},{1,5},{5... | collective-permute-start | bytes 1572872 | tf_op jit(solution)/shard_map/ppermute | solution.py:60
  931.2 135.3 %collective-permute-start.72 = (bf16[2,512,1024]{2,1,0:T(8,128)(2,1)}, bf16[2,512,1024]{2,1,0:T(8,128)(2,1)}, u32[]{:S(2)}, u32[]{:S(2)}) collective-permute-start(bf16[2,512,1024]{2,1,0:T(8,128)(2,1)} %get-tuple-element.113), channel_id=1, source_target_pairs={{0,1},{1,0},{2,3},{3,2},{4,5},{5,4},{6,7},{7,6},{8,9},{9,8},{10,11... | collective-permute-start | bytes 6291464 | tf_op jit(solution)/shard_map/ppermute | solution.py:60
  961.7 434.1 %reduce-scatter.2.cloned.1.call-start = ((), (), s32[]{:S(2)}) async-start(), calls=%async_computation.12 | async-start | bytes 8650752 | tf_op jit(solution)/shard_map/reduce_scatter | solution.py:323
  1056.8 54.6 %all-to-all-start.7 = ((bf16[8,128,768]{1,2,0:T(8,128)(2,1)}), bf16[8,128,768]{1,2,0:T(8,128)(2,1)}, u32[]{:S(2)}, u32[]{:S(2)}) async-start(bf16[8,128,768]{1,2,0:T(8,128)(2,1)} %copy_bitcast_fusion), calls=%async_computation.7 | async-start | bytes 3145728 | tf_op jit(solution)/shard_map/all_to_all | solution.py:101
  1077.4 165.6 %collective-permute-start.73 = (bf16[2,512,1024]{2,1,0:T(8,128)(2,1)}, bf16[2,512,1024]{2,1,0:T(8,128)(2,1)}, u32[]{:S(2)}, u32[]{:S(2)}) collective-permute-start(bf16[2,512,1024]{2,1,0:T(8,128)(2,1)} %add_convert_fusion.3), channel_id=1, source_target_pairs={{0,2},{1,3},{2,0},{3,1},{4,6},{5,7},{6,4},{7,5},{8,10},{9,11},{10,... | collective-permute-start | bytes 6291464 | tf_op jit(solution)/shard_map/ppermute | solution.py:60
  1079.0 148.5 %collective-permute-start.67 = (bf16[1,8,49152]{2,0,1:T(2,128)(2,1)}, bf16[1,8,49152]{2,0,1:T(2,128)(2,1)}, u32[]{:S(2)}, u32[]{:S(2)}) collective-permute-start(bf16[1,8,49152]{2,0,1:T(2,128)(2,1)} %fusion.58), channel_id=1, source_target_pairs={{0,2},{1,3},{2,0},{3,1},{4,6},{5,7},{6,4},{7,5},{8,10},{9,11},{10,... | collective-permute-start | bytes 2359304 | tf_op jit(solution)/shard_map/ppermute | solution.py:60
  1084.2 165.1 %collective-permute-start.68 = (bf16[2,512,1024]{2,1,0:T(8,128)(2,1)}, bf16[2,512,1024]{2,1,0:T(8,128)(2,1)}, u32[]{:S(2)}, u32[]{:S(2)}) collective-permute-start(bf16[2,512,1024]{2,1,0:T(8,128)(2,1)} %get-tuple-element.114), channel_id=1, source_target_pairs={{0,1},{1,0},{2,3},{3,2},{4,5},{5,4},{6,7},{7,6},{8,9},{9,8},{10,11... | collective-permute-start | bytes 6291464 | tf_op jit(solution)/shard_map/ppermute | solution.py:60
  1084.3 196.2 %collective-permute-start.70 = (bf16[2,512,1024]{2,1,0:T(8,128)(2,1)}, bf16[2,512,1024]{2,1,0:T(8,128)(2,1)}, u32[]{:S(2)}, u32[]{:S(2)}) collective-permute-start(bf16[2,512,1024]{2,1,0:T(8,128)(2,1)} %add_convert_fusion.4), channel_id=1, source_target_pairs={{0,2},{1,3},{2,0},{3,1},{4,6},{5,7},{6,4},{7,5},{8,10},{9,11},{10,... | collective-permute-start | bytes 6291464 | tf_op jit(solution)/shard_map/ppermute | solution.py:60
  1089.9 197.2 %collective-permute-start.74 = (bf16[2,256,2048]{2,1,0:T(8,128)(2,1)}, bf16[2,256,2048]{2,1,0:T(8,128)(2,1)}, u32[]{:S(2)}, u32[]{:S(2)}) collective-permute-start(bf16[2,256,2048]{2,1,0:T(8,128)(2,1)} %get-tuple-element.110), channel_id=1, source_target_pairs={{0,1},{1,0},{2,3},{3,2},{4,5},{5,4},{6,7},{7,6},{8,9},{9,8},{10,11... | collective-permute-start | bytes 6291464 | tf_op jit(solution)/shard_map/ppermute | solution.py:60
  1111.4 220.9 %all-to-all-start.4 = ((bf16[8,128,768]{1,2,0:T(8,128)(2,1)}), bf16[8,128,768]{1,2,0:T(8,128)(2,1)}, u32[]{:S(2)}, u32[]{:S(2)}) async-start(bf16[8,128,768]{1,2,0:T(8,128)(2,1)} %copy_bitcast_fusion.1), calls=%async_computation.4 | async-start | bytes 3145728 | tf_op jit(solution)/shard_map/all_to_all | solution.py:101
  1227.5 97.2 %collective-permute-start.76 = (bf16[2,256,2048]{2,1,0:T(8,128)(2,1)}, bf16[2,256,2048]{2,1,0:T(8,128)(2,1)}, u32[]{:S(2)}, u32[]{:S(2)}) collective-permute-start(bf16[2,256,2048]{2,1,0:T(8,128)(2,1)} %add_convert_fusion.2), channel_id=1, source_target_pairs={{0,2},{1,3},{2,0},{3,1},{4,6},{5,7},{6,4},{7,5},{8,10},{9,11},{10,... | collective-permute-start | bytes 6291464 | tf_op jit(solution)/shard_map/ppermute | solution.py:60
  1243.0 130.9 %collective-permute-start.23 = (bf16[128,2048]{1,0:T(8,128)(2,1)}, bf16[128,2048]{1,0:T(8,128)(2,1)S(1)}, u32[]{:S(2)}, u32[]{:S(2)}) collective-permute-start(bf16[128,2048]{1,0:T(8,128)(2,1)} %get-tuple-element.136), channel_id=1, source_target_pairs={{0,4},{4,0},{8,12},{12,8},{16,20},{20,16},{24,28},{28,24},{1,5},{5... | collective-permute-start | bytes 1572872 | tf_op jit(solution)/shard_map/ppermute | solution.py:60
  1249.3 124.6 %collective-permute-start.25 = (bf16[128,2048]{1,0:T(8,128)(2,1)}, bf16[128,2048]{1,0:T(8,128)(2,1)}, u32[]{:S(2)}, u32[]{:S(2)}) collective-permute-start(bf16[128,2048]{1,0:T(8,128)(2,1)} %get-tuple-element.140), channel_id=1, source_target_pairs={{0,24},{4,28},{8,16},{12,20},{16,8},{20,12},{24,0},{28,4},{1,25},{... | collective-permute-start | bytes 1572872 | tf_op jit(solution)/shard_map/ppermute | solution.py:60
  1280.4 93.5 %collective-permute-start.29 = (bf16[128,2048]{1,0:T(8,128)(2,1)}, bf16[128,2048]{1,0:T(8,128)(2,1)}, u32[]{:S(2)}, u32[]{:S(2)}) collective-permute-start(bf16[128,2048]{1,0:T(8,128)(2,1)} %get-tuple-element.141), channel_id=1, source_target_pairs={{0,8},{4,12},{8,0},{12,4},{16,24},{20,28},{24,16},{28,20},{1,9},{5... | collective-permute-start | bytes 1572872 | tf_op jit(solution)/shard_map/ppermute | solution.py:60
  1287.1 86.9 %collective-permute-start.27 = (bf16[128,2048]{1,0:T(8,128)(2,1)}, bf16[128,2048]{1,0:T(8,128)(2,1)}, u32[]{:S(2)}, u32[]{:S(2)}) collective-permute-start(bf16[128,2048]{1,0:T(8,128)(2,1)} %get-tuple-element.142), channel_id=1, source_target_pairs={{0,16},{4,20},{8,24},{12,28},{16,0},{20,4},{24,8},{28,12},{1,17},{... | collective-permute-start | bytes 1572872 | tf_op jit(solution)/shard_map/ppermute | solution.py:60
  1332.3 47.0 %all-to-all-start.8 = ((bf16[8,64,768]{2,1,0:T(8,128)(2,1)}), bf16[8,64,768]{2,1,0:T(8,128)(2,1)}, u32[]{:S(2)}, u32[]{:S(2)}) async-start(bf16[8,64,768]{2,1,0:T(8,128)(2,1)} %bitcast.314), calls=%async_computation.8 | async-start | bytes 1572864 | tf_op jit(solution)/shard_map/all_to_all | solution.py:101
  (189 other events, 3293.6 us)
Sparse Core Ops, SparseCore 0:
  20.5 158.7 all-gather.2
  1053.7 185.5 reduce-scatter.1

commit v2 on v1

v2 whole, which is shorter than its diff:
```python
import functools

import jax
import jax.numpy as jnp
from jax import lax
from jax.experimental import pallas as pl
from jax.experimental.pallas import tpu as pltpu
from jax.sharding import PartitionSpec as P

HEAD = 128
EPS = 1e-06
ROPE_BASE = 10000.0
NEGATIVE = -1e30
LOW = jnp.bfloat16
F32 = jnp.float32


def rms_scale(values, gain_vec):
    return values * lax.rsqrt(jnp.mean(values * values, axis=-1, keepdims=True) + EPS) * gain_vec


def places(perm_row, length_row):
    seq_ends = jnp.cumsum(length_row)
    seg_ids = jnp.sum((perm_row[:, None] >= seq_ends[None, :]).astype(jnp.int32), axis=1)
    starts = seq_ends - length_row
    pick_mask = seg_ids[:, None] == jnp.arange(length_row.shape[0], dtype=jnp.int32)[None, :]
    seq_begin = jnp.sum(jnp.where(pick_mask, starts[None, :], 0), axis=1)
    return (seg_ids, perm_row - seq_begin)


def angles(positions):
    half_size = HEAD // 2
    frequency = jnp.power(ROPE_BASE, -2.0 * jnp.arange(half_size, dtype=F32) / HEAD)
    turned = positions.astype(F32)[..., None] * frequency
    cosine, sine = jnp.cos(turned), jnp.sin(turned)
    return (
        jnp.concatenate([cosine, cosine], axis=-1),
        jnp.concatenate([-sine, sine], axis=-1),
    )


def hop(value, axis, step):
    size = lax.axis_size(axis)
    return lax.ppermute(value, axis, [(i, i ^ step) for i in range(size)])


def gather_first(value, axis):
    size = lax.axis_size(axis)
    blocks = [None] * size
    blocks[0] = value
    for k in range(2, size, 2):
        blocks[k] = hop(value, axis, k)
    return blocks


def gather_second(blocks, axis):
    blocks = list(blocks)
    for k in range(0, len(blocks), 2):
        blocks[k + 1] = hop(blocks[k], axis, 1)
    return blocks


def gather_blocks(value, axis):
    return gather_second(gather_first(value, axis), axis)


def scatter_first(blocks, axis):
    return {
        k: (blocks[k].astype(F32) + hop(blocks[k + 1], axis, 1).astype(F32)).astype(LOW)
        for k in range(len(blocks) - 2, -1, -2)
    }


def scatter_second(half, axis):
    total = half[0].astype(F32)
    for k in sorted(half):
        if k:
            total = total + hop(half[k], axis, k).astype(F32)
    return total


def scatter_blocks(blocks, axis):
    return scatter_second(scatter_first(blocks, axis), axis)


def place_blocks(blocks, own, dim):
    size = blocks[0].shape[dim]
    shape = list(blocks[0].shape)
    shape[dim] = size * len(blocks)
    whole = jnp.zeros(shape, blocks[0].dtype)
    for k, block in enumerate(blocks):
        whole = lax.dynamic_update_slice_in_dim(whole, block, (own ^ k) * size, dim)
    return whole


def take_blocks(whole, own, count, dim):
    size = whole.shape[dim] // count
    return [lax.dynamic_slice_in_dim(whole, (own ^ k) * size, size, dim) for k in range(count)]


def swap(value, axis):
    return lax.all_to_all(value, axis, split_axis=0, concat_axis=0, tiled=True)


def dot(a, b):
    return jnp.dot(a, b, preferred_element_type=F32)


def ein(spec, a, b):
    return jnp.einsum(spec, a, b, preferred_element_type=F32)


def tie(value, *others):
    return lax.optimization_barrier((value, others))[0]


def mm(a, b, dims=((1,), (0,))):
    return lax.dot_general(a, b, (dims, ((), ())), preferred_element_type=F32)


def mm_nt(a, b):
    return mm(a, b, ((1,), (1,)))


def expert_kernel(n, tile, shared, own_ref, *refs):
    xs, cs = refs[:n], refs[n : 2 * n]
    pick_ref, turned_ref, router_ref, gate_ref, up_ref, down_ref = refs[2 * n : 2 * n + 6]
    outs = refs[2 * n + 6 + shared :]
    moe, dsum = outs[:n], outs[n : 2 * n]
    buffer_ref, d_result_ref, hidden_ref, dg_ref, du_ref, d_gate_ref = outs[2 * n : 2 * n + 6]
    acc_res, acc_db, grad_rows, gate_cols = outs[2 * n + 6 :]
    own = own_ref[0]
    expert, step, steps = pl.program_id(0), pl.program_id(1), pl.num_programs(1)
    cap = pick_ref.shape[3]
    index = own * pl.num_programs(0) + expert

    @pl.when(step == 0)
    def _():
        for k in range(n):
            span = pl.ds(k * cap, cap)
            block = xs[k][...]
            pick = pick_ref[0, 0, own ^ k]
            buffer_ref[0, span, :] = mm(pick, block).astype(LOW)
            logits = mm_nt(router_ref[...], block)
            terms = jnp.exp(logits - jnp.max(logits, axis=0, keepdims=True))
            router = terms / jnp.sum(terms, axis=0, keepdims=True)
            lines = lax.broadcasted_iota(jnp.int32, router.shape, 0)
            row = jnp.sum(jnp.where(lines == index, router, 0.0), axis=0, keepdims=True)
            col = jnp.sum(pick.astype(F32) * row, axis=1, keepdims=True)
            grads = mm(pick, cs[k][...])
            grad_rows[span, :] = grads.astype(LOW)
            d_result_ref[0, span, :] = (col * grads).astype(LOW)
            gate_cols[span, :] = jnp.broadcast_to(col, (cap, gate_cols.shape[1]))

    slots = n * cap
    for r in range(0, slots, tile):
        span = pl.ds(r, tile)
        rows_in = buffer_ref[0, span, :]
        gate_act = mm(rows_in, gate_ref[0])
        up_act = mm(rows_in, up_ref[0])
        d_hidden = mm_nt(d_result_ref[0, span, :], down_ref[0])
        sig = 1.0 / (1.0 + jnp.exp(-gate_act))
        silu = gate_act * sig
        hidden = (silu * up_act).astype(LOW)
        dg = (d_hidden * up_act * (sig * (1.0 + gate_act * (1.0 - sig)))).astype(LOW)
        du = (d_hidden * silu).astype(LOW)
        hidden_ref[0, span, :] = hidden
        dg_ref[0, span, :] = dg
        du_ref[0, span, :] = du

        @pl.when(step == 0)
        def _():
            acc_res[span, :] = mm(hidden_ref[0, span, :], down_ref[0])
            acc_db[span, :] = mm_nt(dg_ref[0, span, :], gate_ref[0]) + mm_nt(
                du_ref[0, span, :], up_ref[0]
            )

        @pl.when(step > 0)
        def _():
            acc_res[span, :] += mm(hidden_ref[0, span, :], down_ref[0])
            acc_db[span, :] += mm_nt(dg_ref[0, span, :], gate_ref[0]) + mm_nt(
                du_ref[0, span, :], up_ref[0]
            )

    @pl.when(step == steps - 1)
    def _():
        lines = lax.broadcasted_iota(jnp.int32, d_gate_ref.shape[1:], 0)
        d_gate = jnp.zeros(d_gate_ref.shape[1:], F32)
        for k in range(n):
            span = pl.ds(k * cap, cap)
            pick = pick_ref[0, 0, own ^ k]
            turned = turned_ref[0, 0, own ^ k]
            result = acc_res[span, :].astype(LOW).astype(F32)
            col = jnp.sum(result * grad_rows[span, :].astype(F32), axis=1, keepdims=True)
            row = jnp.sum(pick.astype(F32) * col, axis=0, keepdims=True)
            d_gate = jnp.where(lines == (own ^ k), row, d_gate)
            scaled = (gate_cols[span, :1] * result).astype(LOW)
            part = mm(turned, scaled)
            d_part = mm(turned, acc_db[span, :].astype(LOW))

            @pl.when(expert == 0)
            def _():
                moe[k][...] = part.astype(LOW)
                dsum[k][...] = d_part.astype(LOW)

            @pl.when(expert > 0)
            def _():
                moe[k][...] = (moe[k][...].astype(F32) + part).astype(LOW)
                dsum[k][...] = (dsum[k][...].astype(F32) + d_part).astype(LOW)

        d_gate_ref[0] = d_gate


def expert_layer(own, blocks, grads, pick, turned, router_turned, gate, up, down, at, micro, kept, tile=512):
    n = len(blocks)
    rows, width = blocks[0].shape
    count, _, ff = gate.shape
    cap = pick.shape[3]
    slots = n * cap
    split = 2 if n <= 8 else 4
    ft = ff // split
    one = dict(pipeline_mode=pl.Buffered(1))
    some = one if n > 8 else {}
    block = pl.BlockSpec((rows, width), lambda e, f, o: (0, 0), **one)
    row_block = pl.BlockSpec((1, slots, width), lambda e, f, o: (e, at, 0), **some)
    ff_block = pl.BlockSpec((1, slots, ft), lambda e, f, o: (e, at, f))
    tokens_shape = jax.ShapeDtypeStruct((rows, width), LOW)
    rows_shape = jax.ShapeDtypeStruct((count, micro * slots, width), LOW)
    ff_shape = jax.ShapeDtypeStruct((count, micro * slots, ff), LOW)
    kept = [] if kept is None else list(kept)
    before = 1 + 2 * n + 6
    outs = pl.pallas_call(
        functools.partial(expert_kernel, n, tile, len(kept)),
        out_shape=[tokens_shape] * (2 * n)
        + [rows_shape, rows_shape, ff_shape, ff_shape, ff_shape]
        + [jax.ShapeDtypeStruct((count, n, rows), F32)],
        grid_spec=pltpu.PrefetchScalarGridSpec(
            num_scalar_prefetch=1,
            grid=(count, split),
            in_specs=[block] * (2 * n)
            + [
                pl.BlockSpec((1, 1, n, cap, rows), lambda e, f, o: (e, at, 0, 0, 0), **some),
                pl.BlockSpec((1, 1, n, rows, cap), lambda e, f, o: (e, at, 0, 0, 0), **some),
                pl.BlockSpec(router_turned.shape, lambda e, f, o: (0, 0)),
                pl.BlockSpec((1, width, ft), lambda e, f, o: (e, 0, f)),
                pl.BlockSpec((1, width, ft), lambda e, f, o: (e, 0, f)),
                pl.BlockSpec((1, ft, width), lambda e, f, o: (e, f, 0)),
            ]
            + [pl.BlockSpec(memory_space=pl.ANY)] * len(kept),
            out_specs=[block] * (2 * n)
            + [row_block, row_block, ff_block, ff_block, ff_block]
            + [pl.BlockSpec((1, n, rows), lambda e, f, o: (e, 0, 0))],
            scratch_shapes=[
                pltpu.VMEM((slots, width), F32),
                pltpu.VMEM((slots, width), F32),
                pltpu.VMEM((slots, width), LOW),
                pltpu.VMEM((slots, 128), F32),
            ],
        ),
        input_output_aliases={before + i: 2 * n + i for i in range(len(kept))},
        compiler_params=pltpu.CompilerParams(vmem_limit_bytes=60 << 20),
        cost_estimate=pl.CostEstimate(
            flops=24 * count * slots * width * ff,
            transcendentals=count * slots * ff,
            bytes_accessed=4 * n * rows * width * 2 + 3 * count * width * ff * 2,
        ),
        name="experts",
    )(own.reshape(1), *blocks, *grads, pick, turned, router_turned, gate, up, down, *kept)
    return outs[:n], outs[n : 2 * n], outs[2 * n : 2 * n + 5], outs[2 * n + 5]


def turn(x):
    return pltpu.roll(x, HEAD // 2, 1)


def attend_kernel(n, tile, own_ref, *refs):
    xs = refs[:n]
    wq, wk, wv, gains_ref, cos_ref, sin_ref, seg_col, seg_row = refs[n : n + 8]
    attended_ref, normed_ref, raw_ref, low_ref = refs[n + 8 :]
    own = own_ref[0]
    rows, width = xs[0].shape
    part = wq.shape[1]
    group = n * rows
    for k in range(n):
        normed_ref[own ^ k] = xs[k][...]
    for r in range(0, group, tile):
        span = pl.ds(r, tile)
        block = normed_ref[r // rows : (r + tile) // rows].reshape(tile, width)
        cos, sin = cos_ref[span, :], sin_ref[span, :]
        for which, weight in enumerate((wq, wk, wv)):
            out = mm(block, weight[...])
            if which == 2:
                low_ref[span, 2 * part :] = out.astype(LOW)
                continue
            raw_ref[span, which * part : (which + 1) * part] = out
            for h in range(part // HEAD):
                x = out[:, h * HEAD : (h + 1) * HEAD]
                x = x * lax.rsqrt(jnp.mean(x * x, axis=1, keepdims=True) + EPS)
                x = x * gains_ref[which : which + 1, :]
                x = x * cos + turn(x) * sin
                at = which * part + h * HEAD
                low_ref[span, at : at + HEAD] = x.astype(LOW)
    for h in range(part // HEAD):
        keys = low_ref[:, part + h * HEAD : part + (h + 1) * HEAD]
        values = low_ref[:, 2 * part + h * HEAD : 2 * part + (h + 1) * HEAD]
        for r in range(0, group, tile):
            query = low_ref[r : r + tile, h * HEAD : (h + 1) * HEAD]
            scores = mm_nt(query, keys) * HEAD**-0.5
            same = seg_col[r : r + tile, :] == seg_row[...]
            scores = jnp.where(same, scores, NEGATIVE)
            terms = jnp.exp(scores - jnp.max(scores, axis=1, keepdims=True))
            probs = terms * (1.0 / jnp.sum(terms, axis=1, keepdims=True))
            out = mm(probs.astype(LOW), values).astype(LOW)
            for i in range(0, tile, rows):
                attended_ref[(r + i) // rows, :, h * HEAD : (h + 1) * HEAD] = out[i : i + rows]


def attend(own, blocks, qkv_weight, gains, cos, sin, seg, tile=512):
    n = len(blocks)
    rows, width = blocks[0].shape
    part = width // n
    group = n * rows

    def columns(which):
        return pl.BlockSpec((width, part), lambda i, o: (0, which * n + o[0]))

    def whole(*shape):
        return pl.BlockSpec(shape, lambda i, o: (0,) * len(shape))

    return pl.pallas_call(
        functools.partial(attend_kernel, n, tile),
        out_shape=[
            jax.ShapeDtypeStruct((n, rows, part), LOW),
            jax.ShapeDtypeStruct((n, rows, width), LOW),
            jax.ShapeDtypeStruct((group, 2 * part), F32),
            jax.ShapeDtypeStruct((group, 3 * part), LOW),
        ],
        grid_spec=pltpu.PrefetchScalarGridSpec(
            num_scalar_prefetch=1,
            grid=(1,),
            in_specs=[whole(rows, width)] * n
            + [columns(0), columns(1), columns(2)]
            + [
                whole(2, HEAD),
                whole(group, HEAD),
                whole(group, HEAD),
                whole(group, 1),
                whole(1, group),
            ],
            out_specs=[
                whole(n, rows, part),
                whole(n, rows, width),
                whole(group, 2 * part),
                whole(group, 3 * part),
            ],
        ),
        compiler_params=pltpu.CompilerParams(vmem_limit_bytes=56 << 20),
        cost_estimate=pl.CostEstimate(
            flops=2 * group * (3 * width * part + 2 * group * part),
            transcendentals=group * group * (part // HEAD),
            bytes_accessed=group * (4 * width + 18 * part) + 6 * width * part,
        ),
        name="attend",
    )(
        own.reshape(1),
        *blocks,
        qkv_weight,
        qkv_weight,
        qkv_weight,
        gains,
        cos,
        sin,
        seg[:, None],
        seg[None, :],
    )


def attend_back_kernel(
    n,
    tile,
    d_ref,
    low_ref,
    raw_ref,
    gains_ref,
    cos_ref,
    sin_ref,
    seg_col,
    seg_row,
    out_ref,
    gain_ref,
    dq_ref,
    dk_ref,
    dv_ref,
):
    rows, part = d_ref.shape[1:]
    group = n * rows
    scale = HEAD**-0.5
    gain_terms = [jnp.zeros((1, HEAD), F32), jnp.zeros((1, HEAD), F32)]
    for h in range(part // HEAD):
        cols = slice(h * HEAD, (h + 1) * HEAD)
        keys = low_ref[:, part + h * HEAD : part + (h + 1) * HEAD]
        values = low_ref[:, 2 * part + h * HEAD : 2 * part + (h + 1) * HEAD]
        for r in range(0, group, tile):
            query = low_ref[r : r + tile, cols]
            d_out = d_ref[r // rows : (r + tile) // rows, :, cols].reshape(tile, HEAD)
            scores = mm_nt(keys, query) * scale
            same = seg_col[...] == seg_row[:, r : r + tile]
            scores = jnp.where(same, scores, NEGATIVE)
            terms = jnp.exp(scores - jnp.max(scores, axis=0, keepdims=True))
            probs = terms * (1.0 / jnp.sum(terms, axis=0, keepdims=True))
            d_probs = mm_nt(values, d_out)
            delta = jnp.sum(probs * d_probs, axis=0, keepdims=True)
            d_scores = (probs * (d_probs - delta)).astype(LOW)
            dv = mm(probs.astype(LOW), d_out)
            dk = mm(d_scores, query)
            dq_ref[r : r + tile, :] = mm(d_scores, keys, ((0,), (0,))) * scale
            if r == 0:
                dv_ref[...] = dv
                dk_ref[...] = dk * scale
            else:
                dv_ref[...] += dv
                dk_ref[...] += dk * scale
        for r in range(0, group, rows):
            span = pl.ds(r, rows)
            cos, sin = cos_ref[span, :], sin_ref[span, :]
            at = 2 * part + h * HEAD
            out_ref[r // rows, :, at : at + HEAD] = dv_ref[span, :].astype(LOW)
            for which, grad_ref in enumerate((dq_ref, dk_ref)):
                at = which * part + h * HEAD
                raw = raw_ref[span, at : at + HEAD]
                inv = lax.rsqrt(jnp.mean(raw * raw, axis=1, keepdims=True) + EPS)
                unit = raw * inv
                grad = grad_ref[span, :]
                grad = grad * cos + turn(grad * sin)
                gain_terms[which] += jnp.sum(grad * unit, axis=0, keepdims=True)
                grad = grad * gains_ref[which : which + 1, :]
                grad = inv * (grad - unit * jnp.mean(grad * unit, axis=1, keepdims=True))
                out_ref[r // rows, :, at : at + HEAD] = grad.astype(LOW)
    for which in range(2):
        gain_ref[which : which + 1, :] = gain_terms[which]


def attend_back(d_attended, low, raw, gains, cos, sin, seg, tile=512):
    n, rows, part = d_attended.shape
    group = n * rows
    return pl.pallas_call(
        functools.partial(attend_back_kernel, n, tile),
        out_shape=[
            jax.ShapeDtypeStruct((n, rows, 3 * part), LOW),
            jax.ShapeDtypeStruct((2, HEAD), F32),
        ],
        scratch_shapes=[pltpu.VMEM((group, HEAD), F32)] * 3,
        compiler_params=pltpu.CompilerParams(vmem_limit_bytes=56 << 20),
        cost_estimate=pl.CostEstimate(
            flops=10 * group * group * part,
            transcendentals=group * group * (part // HEAD),
            bytes_accessed=group * part * 22,
        ),
        name="attend_back",
    )(d_attended, low, raw, gains, cos, sin, seg[:, None], seg[None, :])


def local(
    tokens,
    cotangent,
    qkv_weight,
    out_weight,
    router_weight,
    attn_gain,
    moe_gain,
    head_gains,
    gate_weight,
    up_weight,
    down_weight,
    permutation,
    lengths,
    routes,
):
    micro, rows, width = tokens.shape
    n = lax.axis_size("expert")
    m = lax.axis_size("shard")
    own = lax.axis_index("expert")
    own_shard = lax.axis_index("shard")
    local_count = gate_weight.shape[0]
    expert_count = local_count * n
    top_count = routes.shape[2]
    capacity = rows * top_count // expert_count
    part = width // n
    piece = width // (n * m)

    full_gate = lax.all_gather(gate_weight, "shard", axis=1, tiled=True)
    full_up = lax.all_gather(up_weight, "shard", axis=1, tiled=True)
    full_down = lax.all_gather(down_weight, "shard", axis=1, tiled=True)

    each = range(micro)
    routes_all = swap(jnp.broadcast_to(routes[None], (n,) + routes.shape), "expert")
    inputs = [tokens[i].astype(F32) for i in each]
    normed_attn = [rms_scale(x, attn_gain).astype(LOW) for x in inputs]
    normed_attn[0], routes_all = lax.optimization_barrier((normed_attn[0], routes_all))

    own_experts = own * local_count + jnp.arange(local_count, dtype=jnp.int32)
    by_micro = jnp.swapaxes(routes_all, 0, 1)
    hit = jnp.any(by_micro[None] == own_experts[:, None, None, None, None], axis=-1)
    hot = hit.astype(jnp.int32)
    slot = jnp.cumsum(hot, axis=-1) - hot
    slot_iota = jnp.arange(capacity, dtype=jnp.int32)
    pick = (hit[:, :, :, None, :] & (slot[:, :, :, None, :] == slot_iota[:, None])).astype(LOW)
    turned = (hit[..., None] & (slot[..., None] == slot_iota)).astype(LOW)

    gains = head_gains.reshape(2, HEAD)
    spots = [places(permutation[i, 0], lengths[i, 0]) for i in each]
    turns = [angles(pos) for _, pos in spots]
    near = [gather_first(x, "expert") for x in normed_attn]
    normed_blocks = [gather_second(x, "expert") for x in near]
    grad_near = [gather_first(tie(cotangent[i], near[-1][-2]), "expert") for i in each]
    attended, normed_all, qkv_raw, qkv_low, mixed, normed_moe = ([None] * micro for _ in range(6))
    for i in each:
        attended[i], normed_all[i], qkv_raw[i], qkv_low[i] = attend(
            own, normed_blocks[i], qkv_weight, gains, *turns[i], spots[i][0]
        )
        attended[i] = swap(attended[i], "expert")
        mixed[i] = inputs[i] + ein("hrp,hpd->rd", attended[i], out_weight.reshape(n, part, width))
        normed_moe[i] = rms_scale(mixed[i], moe_gain).astype(LOW)

    moe_sum, d_sum, d_gate = ([None] * micro for _ in range(3))
    kept = None
    for i in each:
        grad_blocks = gather_second(grad_near[i], "expert")
        moe_blocks = gather_blocks(normed_moe[i], "expert")
        moe_sum[i], d_sum[i], kept, d_gate[i] = expert_layer(
            own,
            moe_blocks,
            grad_blocks,
            pick,
            turned,
            router_weight.T,
            full_gate,
            full_up,
            full_down,
            i,
            micro,
            kept,
        )
    buffer, d_result, hidden, dg, du = kept
    gate_term = ein("erd,erf->edf", buffer, dg).astype(LOW)
    up_term = ein("erd,erf->edf", buffer, du).astype(LOW)
    down_term = ein("erf,erd->efd", hidden, d_result).astype(LOW)
    gate_grad, up_grad, down_grad = (
        lax.psum_scatter(term, "shard", scatter_dimension=1, tiled=True).astype(F32)
        for term in (gate_term, up_term, down_term)
    )

    output, input_grad, d_attn, d_qkv = ([None] * micro for _ in range(4))
    router_term, moe_gain_term, head_term, attn_gain_term = 0.0, 0.0, 0.0, 0.0
    for i in each:
        d_gates = swap(d_gate[i].transpose(1, 0, 2), "expert")
        d_router = d_gates.reshape(expert_count, rows).T
        d_normed = scatter_blocks(d_sum[i], "expert")
        grad_out = cotangent[i].astype(F32)
        logits = dot(normed_moe[i], router_weight)
        exp_logits = jnp.exp(logits - jnp.max(logits, axis=-1, keepdims=True))
        router = exp_logits / jnp.sum(exp_logits, axis=-1, keepdims=True)
        d_logits = (
            router * (d_router - jnp.sum(router * d_router, axis=-1, keepdims=True))
        ).astype(LOW)
        d_normed = d_normed + dot(d_logits, router_weight.T)
        router_term = router_term + dot(normed_moe[i].T, d_logits)
        _, norm_pull = jax.vjp(rms_scale, mixed[i], moe_gain)
        d_mixed_norm, term = norm_pull(d_normed)
        moe_gain_term = moe_gain_term + term
        d_mixed = grad_out + d_mixed_norm
        d_attn[i] = d_mixed.astype(LOW)
        d_attended = dot(d_attn[i], out_weight.T).astype(LOW)
        d_attended = swap(jnp.swapaxes(d_attended.reshape(rows, n, part), 0, 1), "expert")
        d_qkv[i], terms = attend_back(
            d_attended, qkv_low[i], qkv_raw[i], gains, *turns[i], spots[i][0]
        )
        head_term = head_term + terms.reshape(2 * HEAD)
        d_qkv_rows = swap(d_qkv[i], "expert").reshape(n, rows, 3, part).transpose(1, 2, 0, 3)
        d_normed_attn = dot(d_qkv_rows.reshape(rows, 3 * width), qkv_weight.T)
        _, attn_pull = jax.vjp(rms_scale, inputs[i], attn_gain)
        d_inputs_norm, term = attn_pull(d_normed_attn)
        attn_gain_term = attn_gain_term + term
        input_grad[i] = (d_mixed + d_inputs_norm).astype(LOW)
        moe_part = scatter_blocks([tie(x, d_normed) for x in moe_sum[i]], "expert")
        output[i] = (mixed[i] + moe_part).astype(LOW)

    attended_cols = jnp.stack([x.reshape(n, rows, m, piece) for x in attended])
    attended_cols = swap(attended_cols.transpose(3, 0, 2, 1, 4), "shard")
    attended_cols = attended_cols.reshape(m * micro * rows, n * piece)
    d_attn_all = place_blocks(
        gather_blocks(jnp.concatenate(d_attn, axis=0), "shard"), own_shard, 0
    )
    out_term = dot(attended_cols.T, d_attn_all).astype(LOW).reshape(n, piece, width)
    out_grad = scatter_blocks(
        [x[0] for x in take_blocks(out_term, own, n, 0)], "expert"
    )

    qkv_term = sum(
        dot(normed_all[i].reshape(n * rows, width).T, d_qkv[i].reshape(n * rows, 3 * part))
        for i in each
    ).astype(LOW)
    qkv_term = jnp.swapaxes(qkv_term.reshape(n, m, piece, 3 * part), 0, 1)
    qkv_sum = scatter_blocks(take_blocks(qkv_term, own_shard, m, 0), "shard").astype(LOW)
    qkv_rows = swap(qkv_sum.reshape(n, piece, 3 * part), "expert")
    qkv_grad = (
        qkv_rows.reshape(n, piece, 3, part).transpose(1, 2, 0, 3).reshape(piece, 3 * width)
    ).astype(F32)
    output, input_grad = jnp.stack(output), jnp.stack(input_grad)

    world = n * m
    head_piece = 2 * HEAD // world
    small = jnp.concatenate(
        [
            router_term.reshape(world, piece * expert_count),
            attn_gain_term.reshape(world, piece),
            moe_gain_term.reshape(world, piece),
            head_term.reshape(world, head_piece),
        ],
        axis=1,
    )
    used = small.shape[1]
    padded = -(-used // 1024) * 1024
    small = jnp.pad(small, ((0, 0), (0, padded - used))).reshape(world, padded // 128, 128)
    small = jnp.sum(swap(small, ("expert", "shard")), axis=0).reshape(padded)
    a = piece * expert_count
    return (
        output,
        input_grad,
        qkv_grad,
        out_grad,
        small[:a].reshape(piece, expert_count),
        small[a : a + piece],
        small[a + piece : a + 2 * piece],
        small[a + 2 * piece : a + 2 * piece + head_piece],
        gate_grad,
        up_grad,
        down_grad,
    )


def solution(mesh):
    return jax.shard_map(
        local,
        mesh=mesh,
        in_specs=(
            P(None, ("expert", "shard"), None),
            P(None, ("expert", "shard"), None),
            P(),
            P(),
            P(),
            P(),
            P(),
            P(),
            P("expert", "shard", None),
            P("expert", "shard", None),
            P("expert", "shard", None),
            P(None, "shard", None),
            P(None, "shard", None),
            P(None, ("expert", "shard"), None),
        ),
        out_specs=(
            P(None, ("expert", "shard"), None),
            P(None, ("expert", "shard"), None),
            P(("expert", "shard"), None),
            P(("expert", "shard"), None),
            P(("expert", "shard"), None),
            P(("expert", "shard")),
            P(("expert", "shard")),
            P(("expert", "shard")),
            P("expert", "shard", None),
            P("expert", "shard", None),
            P("expert", "shard", None),
        ),
        check_vma=False,
    )
```

time: 1410 us -> 975 us (0.69)
  matrix products: 303 us -> 116 us
  Pallas kernels: 0 us -> 174 us
  waiting for transfers between devices: 534 us -> 362 us
  local copies, waits for them, and re-layouts: 210 us -> 52.4 us
  blocking collectives: 55.8 us -> 0 us
  other arithmetic: 131 us -> 80.2 us
    pallas_call x0 -> x6, Pallas kernels: none -> 174 us  [the longest x2 120 us: expert_layer(): pl.pallas_call(functools.partial(expert_kernel, n, tile, len(kept)), out_...]
    dot_general x35 -> x5, matrix products: 221 us -> 54.1 us  [ein(): return jnp.einsum(spec, a, b, preferred_element_type=F32)]
    ppermute x77 -> x83, waiting for transfers between devices: 487 us -> 341 us  [hop(): return lax.ppermute(value, axis, [(i, i ^ step) for i in range(size)])]
    all_gather x1 -> x0, blocking collectives: 55.8 us -> none  [local(): routes_all = lax.all_gather(routes, 'expert', axis=0)]
    unnamed x336 -> x148, local copies, waits for them, and re-layouts: 52.1 us -> 4.93 us
    dynamic_update_slice x40 -> x3, local copies, waits for them, and re-layouts: 43.3 us -> 4.42 us  [place_blocks(): whole = lax.dynamic_update_slice_in_dim(whole, block, (own ^ k) * size, dim)]
    all_to_all x10 -> x12, waiting for transfers between devices: 47.9 us -> 18.7 us  [swap(): return lax.all_to_all(value, axis, split_axis=0, concat_axis=0, tiled=True)]
    reshape x14 -> x1, local copies, waits for them, and re-layouts: 30.5 us -> 2.6 us  [local(): attended_cols = attended_cols.reshape(m * micro * rows, n * piece)]
  transfers between devices with their start and end apart: 89 -> 101, of which waited for: 35 -> 44; matrix products, arithmetic and copies ran while one was open for 43% -> 24% of each run, Pallas kernels for 0% -> 12%
where the time goes in v2:
time: 975 us; the launch traced here: 967 us
  waiting for transfers between devices  362 us (37%)
  Pallas kernels  174 us (18%)
  starting transfers between devices  168 us (17%)
  matrix products  116 us (12%)
  other arithmetic  80.2 us (8%)
  local copies, waits for them, and re-layouts  52.4 us (5%)
  between operations  15.3 us (2%)
    ppermute x83, waiting for transfers between devices, hop(): return lax.ppermute(value, axis, [(i, i ^ step) for i in range(size)])  341 us
    pallas_call x2, Pallas kernels, expert_layer(): pl.pallas_call(functools.partial(expert_kernel, n, tile, len(kept)), out_...  120 us
    ppermute x83, starting transfers between devices, hop(): return lax.ppermute(value, axis, [(i, i ^ step) for i in range(size)])  104 us
    all_to_all x12, starting transfers between devices, swap(): return lax.all_to_all(value, axis, split_axis=0, concat_axis=0, tiled=True)  63.6 us
    dot_general x13, matrix products, dot(): return jnp.dot(a, b, preferred_element_type=F32)  61.7 us
    dot_general x5, matrix products, ein(): return jnp.einsum(spec, a, b, preferred_element_type=F32)  54.1 us
    pallas_call x2, Pallas kernels, attend_back(): pl.pallas_call(functools.partial(attend_back_kernel, n, tile), out_shape=...  28.3 us
    pallas_call x2, Pallas kernels, attend(): pl.pallas_call(functools.partial(attend_kernel, n, tile), out_shape=[jax....  25.6 us
  transfers between devices with their start and end apart: 101, of which 44 were waited for; matrix products, arithmetic and copies ran while one was open for 24% of the time, Pallas kernels for 12%

profile of v2, /device:TPU:8, one launch (start us, length us, event | category | flops | bytes accessed | tf_op | source)
XLA Modules:
  0.0 967.3 jit_solution(1696877686791514503)
XLA Ops:
  20.5 18.6 %all-to-all-done = s32[8,2,128,8]{2,3,1,0:T(8,128)S(1)} async-done(((s32[8,2,128,8]{2,3,1,0:T(8,128)}), s32[8,2,128,8]{2,3,1,0:T(8,128)S(1)}, u32[]{:S(2)}, u32[]{:S(2)}) %all-to-all-start) | async-done | bytes 65568 | tf_op jit(solution)/shard_map/all_to_all | solution.py:102
  42.6 5.0 fusion.36
  52.2 8.4 collective-permute-done.1.refs_2_
  61.2 26.6 %collective-permute-done.3.refs_4_ = bf16[128,2048]{1,0:T(8,128)(2,1)} collective-permute-done((bf16[128,2048]{1,0:T(8,128)(2,1)S(1)}, bf16[128,2048]{1,0:T(8,128)(2,1)}, u32[]{:S(2)}, u32[]{:S(2)}) %collective-permute-start.3) | collective-permute-done | bytes 524320 | tf_op jit(solution)/shard_map/ppermute | solution.py:44
  88.8 11.7 %collective-permute-done.5.refs_6_ = bf16[128,2048]{1,0:T(8,128)(2,1)} collective-permute-done((bf16[128,2048]{1,0:T(8,128)(2,1)S(1)}, bf16[128,2048]{1,0:T(8,128)(2,1)}, u32[]{:S(2)}, u32[]{:S(2)}) %collective-permute-start.5) | collective-permute-done | bytes 524320 | tf_op jit(solution)/shard_map/ppermute | solution.py:44
  114.2 12.9 %attend.2 = (bf16[8,128,256]{2,1,0:T(8,128)(2,1)}, bf16[8,128,2048]{2,1,0:T(8,128)(2,1)}, f32[1024,512]{1,0:T(8,128)}, bf16[1024,768]{1,0:T(8,128)(2,1)}) custom-call(s32[1]{0:T(128)} %bitcast.1.own_ref, bf16[128,2048]{1,0:T(8,128)(2,1)} %copy-done.14, bf16[128,2048]{1,0:T(8,128)(2,1)} %collective-permute-done.refs_1_, ...), custom_call_target="tpu_custom_call" | custom-call | flops 4294967296 | bytes 16252928 | tf_op jit(solution)/shard_map/attend/pallas_call | solution.py:330
  127.1 5.7 all-to-all-start.1
  142.1 10.0 %collective-permute-done.40.refs_5_ = bf16[128,2048]{1,0:T(8,128)(2,1)} collective-permute-done((bf16[128,2048]{1,0:T(8,128)(2,1)}, bf16[128,2048]{1,0:T(8,128)(2,1)}, u32[]{:S(2)}, u32[]{:S(2)}) %collective-permute-start.40) | collective-permute-done | bytes 524320 | tf_op jit(solution)/shard_map/ppermute | solution.py:44
  154.1 12.7 %attend.3 = (bf16[8,128,256]{2,1,0:T(8,128)(2,1)}, bf16[8,128,2048]{2,1,0:T(8,128)(2,1)}, f32[1024,512]{1,0:T(8,128)}, bf16[1024,768]{1,0:T(8,128)(2,1)}) custom-call(s32[1]{0:T(128)} %bitcast.1.own_ref, bf16[128,2048]{1,0:T(8,128)(2,1)} %copy-done.13, bf16[128,2048]{1,0:T(8,128)(2,1)} %collective-permute-done.36.refs_1_, ...), custom_call_target="tpu_custom_call" | custom-call | flops 4294967296 | bytes 16252928 | tf_op jit(solution)/shard_map/attend/pallas_call | solution.py:330
  166.8 5.5 all-to-all-start.3
  172.3 4.8 multiply_reduce_fusion.5
  186.5 5.7 collective-permute-done.19.refs_13_
  198.1 17.6 %collective-permute-done.10.refs_4_ = bf16[128,2048]{1,0:T(8,128)(2,1)} collective-permute-done((bf16[128,2048]{1,0:T(8,128)(2,1)}, bf16[128,2048]{1,0:T(8,128)(2,1)}, u32[]{:S(2)}, u32[]{:S(2)}) %collective-permute-start.10) | collective-permute-done | bytes 524320 | tf_op jit(solution)/shard_map/ppermute | solution.py:44
  217.4 6.5 collective-permute-done.12.refs_6_
  225.4 5.0 multiply_reduce_fusion.4
  233.4 5.2 collective-permute-done.11.refs_5_
  238.5 7.3 collective-permute-done.13.refs_7_
  245.8 65.3 %experts.2 = (bf16[128,2048]{1,0:T(8,128)(2,1)}, bf16[128,2048]{1,0:T(8,128)(2,1)}, bf16[128,2048]{1,0:T(8,128)(2,1)}, bf16[128,2048]{1,0:T(8,128)(2,1)}, bf16[1...) custom-call(s32[1]{0:T(128)} %bitcast.1.own_ref, ...), custom_call_target="tpu_custom_call" | custom-call | flops 51539607552 | bytes 41943040 | tf_op jit(solution)/shard_map/experts/pallas_call | solution.py:232
  315.9 5.3 all-to-all-start.2
  329.0 8.5 collective-permute-done.25
  340.0 8.8 collective-permute-done.23
  354.4 5.8 collective-permute-done.22
  361.6 12.1 %collective-permute-done.28 = bf16[128,2048]{1,0:T(8,128)(2,1)} collective-permute-done((bf16[128,2048]{1,0:T(8,128)(2,1)S(1)}, bf16[128,2048]{1,0:T(8,128)(2,1)}, u32[]{:S(2)}, u32[]{:S(2)}) %collective-permute-start.28) | collective-permute-done | bytes 524320 | tf_op jit(solution)/shard_map/ppermute | solution.py:44
  374.6 27.0 %collective-permute-done.26 = bf16[128,2048]{1,0:T(8,128)(2,1)} collective-permute-done((bf16[128,2048]{1,0:T(8,128)(2,1)S(1)}, bf16[128,2048]{1,0:T(8,128)(2,1)}, u32[]{:S(2)}, u32[]{:S(2)}) %collective-permute-start.26) | collective-permute-done | bytes 524320 | tf_op jit(solution)/shard_map/ppermute | solution.py:44
  409.8 4.2 collective-permute-done.54.refs_14_
  420.7 14.6 %collective-permute-done.45.refs_4_ = bf16[128,2048]{1,0:T(8,128)(2,1)S(1)} collective-permute-done((bf16[128,2048]{1,0:T(8,128)(2,1)S(1)}, bf16[128,2048]{1,0:T(8,128)(2,1)S(1)}, u32[]{:S(2)}, u32[]{:S(2)}) %collective-permute-start.45) | collective-permute-done | bytes 524320 | tf_op jit(solution)/shard_map/ppermute | solution.py:44
  436.2 6.6 collective-permute-done.47.refs_6_
  444.7 7.9 collective-permute-done.44.refs_3_
  452.7 8.9 collective-permute-done.46.refs_5_
  461.5 5.6 collective-permute-done.48.refs_7_
  468.0 54.7 %experts.3 = (bf16[128,2048]{1,0:T(8,128)(2,1)}, bf16[128,2048]{1,0:T(8,128)(2,1)}, bf16[128,2048]{1,0:T(8,128)(2,1)}, bf16[128,2048]{1,0:T(8,128)(2,1)}, bf16[1...) custom-call(s32[1]{0:T(128)} %bitcast.1.own_ref, ...), custom_call_target="tpu_custom_call", output_to_operand_aliasing={{16}: (23, {}), {17}: (24, {}), {18}: (25, {}), {19}: (26, ... | custom-call | flops 51539607552 | bytes 41943040 | tf_op jit(solution)/shard_map/experts/pallas_call | solution.py:232
  522.6 14.7 %convolution_convert_fusion.2 = bf16[2,2048,1024]{2,1,0:T(8,128)(2,1)} fusion(bf16[2,1024,2048]{2,1,0:T(8,128)(2,1)} %get-tuple-element.158, bf16[2,1024,1024]{2,1,0:T(8,128)(2,1)} %get-tuple-element.159), kind=kOutput, calls=%fused_computation.4 | convolution fusion | flops 8594128896 | bytes 20971520 | tf_op jit(solution)/shard_map/erd,erf->edf/dot_general | solution.py:110
  537.4 14.7 %convolution_convert_fusion.1 = bf16[2,2048,1024]{2,1,0:T(8,128)(2,1)} fusion(bf16[2,1024,2048]{2,1,0:T(8,128)(2,1)} %get-tuple-element.158, bf16[2,1024,1024]{2,1,0:T(8,128)(2,1)} %get-tuple-element.160), kind=kOutput, calls=%fused_computation.3 | convolution fusion | flops 8594128896 | bytes 20971520 | tf_op jit(solution)/shard_map/erd,erf->edf/dot_general | solution.py:110
  558.2 4.6 all-to-all-start.4
  570.4 8.2 collective-permute-done.59
  580.7 5.8 collective-permute-done.57
  595.2 9.2 collective-permute-done.60
  611.6 15.1 %convolution_convert_fusion = bf16[2,1024,2048]{2,1,0:T(8,128)(2,1)} fusion(bf16[2,1024,1024]{2,1,0:T(8,128)(2,1)S(1)} %copy-done.71, bf16[2,1024,2048]{2,1,0:T(8,128)(2,1)} %get-tuple-element.162), kind=kOutput, calls=%fused_computation.2 | convolution fusion | flops 8594128896 | bytes 20971520 | tf_op jit(solution)/shard_map/erf,erd->efd/dot_general | solution.py:110
  640.7 6.3 collective-permute-done.64
  652.8 4.3 all-to-all-start.10
  657.1 9.3 collective-permute-done.69
  666.4 6.4 collective-permute-done.67
  672.9 4.4 fusion.47
  678.0 6.3 convolution_convert_fusion.4
  687.4 7.0 all-to-all-start.7
  705.0 8.1 convolution_convert_fusion.5
  716.3 5.4 all-to-all-start.5
  729.4 14.1 %attend_back.3 = (bf16[8,128,768]{2,1,0:T(8,128)(2,1)}, f32[2,128]{1,0:T(2,128)}) custom-call(bf16[8,128,256]{2,1,0:T(8,128)(2,1)} %all-to-all-done.7.d_ref, bf16[1024,768]{1,0:T(8,128)(2,1)} %get-tuple-element.151.low_ref, f32[1024,512]{1,0:T(8,128)} %get-tuple-element.152.raw_ref, f32[2,128]{1,0:T(2,128)} %bitcast.230, ...), custom_call_target="tpu_custom_call" | custom-call | flops 2684354560 | bytes 5767168 | tf_op jit(solution)/shard_map/attend_back/pallas_call | solution.py:446
  743.5 6.2 all-to-all-start.8
  749.8 14.2 %attend_back.2 = (bf16[8,128,768]{2,1,0:T(8,128)(2,1)}, f32[2,128]{1,0:T(2,128)}) custom-call(bf16[8,128,256]{2,1,0:T(8,128)(2,1)} %all-to-all-done.5.d_ref, bf16[1024,768]{1,0:T(8,128)(2,1)} %get-tuple-element.148.low_ref, f32[1024,512]{1,0:T(8,128)} %get-tuple-element.149.raw_ref, f32[2,128]{1,0:T(2,128)} %bitcast.231, ...), custom_call_target="tpu_custom_call" | custom-call | flops 2684354560 | bytes 5767168 | tf_op jit(solution)/shard_map/attend_back/pallas_call | solution.py:446
  764.0 5.7 fusion.55
  785.9 6.0 all-to-all-start.6
  791.9 5.0 convolution_convert_fusion.3
  804.8 8.9 collective-permute-done.77
  816.7 4.3 collective-permute-done.81
  823.4 5.4 collective-permute-done.79
  838.4 5.8 collective-permute-done.76
  845.6 20.7 %collective-permute-done.82 = bf16[64,2048]{1,0:T(8,128)(2,1)S(1)} collective-permute-done((bf16[64,2048]{1,0:T(8,128)(2,1)S(1)}, bf16[64,2048]{1,0:T(8,128)(2,1)S(1)}, u32[]{:S(2)}, u32[]{:S(2)}) %collective-permute-start.82) | collective-permute-done | bytes 262176 | tf_op jit(solution)/shard_map/ppermute | solution.py:44
  866.3 10.4 %collective-permute-done.80 = bf16[64,2048]{1,0:T(8,128)(2,1)S(1)} collective-permute-done((bf16[64,2048]{1,0:T(8,128)(2,1)S(1)}, bf16[64,2048]{1,0:T(8,128)(2,1)S(1)}, u32[]{:S(2)}, u32[]{:S(2)}) %collective-permute-start.80) | collective-permute-done | bytes 262176 | tf_op jit(solution)/shard_map/ppermute | solution.py:44
  886.2 5.2 all-to-all-start.9
  896.7 14.3 %fusion.54 = f32[128,2048]{1,0:T(8,128)} fusion(bf16[128,6144]{0,1:T(8,128)(2,1)} %bitcast.190, bf16[2048,6144]{1,0:T(8,128)(2,1)} %refs_10_.3), kind=kOutput, calls=%fused_computation.169 | convolution fusion | flops 3221225472 | bytes 27787264 | tf_op jit(solution)/shard_map/dot_general | solution.py:106
  911.0 14.7 %fusion.14 = (f32[2048]{0:T(1024)S(1)}, f32[128]{0:T(128)S(1)}, f32[128]{0:T(128)S(1)}, f32[2048]{0:T(1024)S(1)}, f32[128,2048]{1,0:T(8,128)}) fusion(f32[128]{0:T(128)S(1)} %copy-done.46, bf16[2,128,2048]{2,1,0:T(8,128)(2,1)S(1)} %copy-done.1, f32[2048]{0:T(1024)S(1)} %copy-done.36, f32[128,2048]{1,0:T(8,128)} %fusion.54, f32[128]{0:T(128)S(1)} %copy-done.44, ...), kind=kOutput, calls=%fused_computation.40 | convolution fusion | flops 3224891392 | bytes 29911040 | tf_op jit(solution)/shard_map/dot_general | solution.py:106
  926.8 4.5 fusion.31
  931.3 5.2 all-to-all-start.11
  (424 shorter events, 267.4 us)
Async XLA Ops:
  7.2 238.6 %all-gather.4.cloned.1.call-start = ((), (), s32[]{:S(2)}) async-start(), calls=%async_computation.15 | async-start | bytes 10485760 | tf_op jit(solution)/shard_map/all_gather | solution.py:491
  8.0 237.9 %all-gather.6.cloned.1.call-start = ((), (), s32[]{:S(2)}) async-start(), calls=%async_computation.16 | async-start | bytes 10485760 | tf_op jit(solution)/shard_map/all_gather | solution.py:492
  8.7 237.1 %all-gather.8.cloned.1.call-start = ((), (), s32[]{:S(2)}) async-start(), calls=%async_computation.17 | async-start | bytes 10485760 | tf_op jit(solution)/shard_map/all_gather | solution.py:493
  10.2 31.5 %collective-permute-start.14 = (bf16[128,2048]{1,0:T(8,128)(2,1)S(1)}, bf16[128,2048]{1,0:T(8,128)(2,1)}, u32[]{:S(2)}, u32[]{:S(2)}) collective-permute-start(bf16[128,2048]{1,0:T(8,128)(2,1)S(1)} %get-tuple-element.233.refs_0_), channel_id=1, source_target_pairs={{0,24},{4,28},{8,16},{12,20},{16,8},{20,12},{24,0},{28,4},{1,25},{... | collective-permute-start | bytes 1572872 | tf_op jit(solution)/shard_map/ppermute | solution.py:44
  11.8 36.9 %collective-permute-start.36 = (bf16[128,2048]{1,0:T(8,128)(2,1)S(1)}, bf16[128,2048]{1,0:T(8,128)(2,1)}, u32[]{:S(2)}, u32[]{:S(2)}) collective-permute-start(bf16[128,2048]{1,0:T(8,128)(2,1)S(1)} %get-tuple-element.233.refs_0_), channel_id=1, source_target_pairs={{0,4},{4,0},{8,12},{12,8},{16,20},{20,16},{24,28},{28,24},{1,5},{5... | collective-permute-start | bytes 1572872 | tf_op jit(solution)/shard_map/ppermute | solution.py:44
  13.3 38.5 %collective-permute-start.37 = (bf16[128,2048]{1,0:T(8,128)(2,1)S(1)}, bf16[128,2048]{1,0:T(8,128)(2,1)}, u32[]{:S(2)}, u32[]{:S(2)}) collective-permute-start(bf16[128,2048]{1,0:T(8,128)(2,1)S(1)} %get-tuple-element.233.refs_0_), channel_id=1, source_target_pairs={{0,8},{4,12},{8,0},{12,4},{16,24},{20,28},{24,16},{28,20},{1,9},{5... | collective-permute-start | bytes 1572872 | tf_op jit(solution)/shard_map/ppermute | solution.py:44
  39.5 48.2 %collective-permute-start.3 = (bf16[128,2048]{1,0:T(8,128)(2,1)S(1)}, bf16[128,2048]{1,0:T(8,128)(2,1)}, u32[]{:S(2)}, u32[]{:S(2)}) collective-permute-start(bf16[128,2048]{1,0:T(8,128)(2,1)S(1)} %get-tuple-element.87.refs_0_), channel_id=1, source_target_pairs={{0,16},{4,20},{8,24},{12,28},{16,0},{20,4},{24,8},{28,12},{1,17},{... | collective-permute-start | bytes 1572872 | tf_op jit(solution)/shard_map/ppermute | solution.py:44
  41.7 58.8 %collective-permute-start.5 = (bf16[128,2048]{1,0:T(8,128)(2,1)S(1)}, bf16[128,2048]{1,0:T(8,128)(2,1)}, u32[]{:S(2)}, u32[]{:S(2)}) collective-permute-start(bf16[128,2048]{1,0:T(8,128)(2,1)S(1)} %get-tuple-element.87.refs_0_), channel_id=1, source_target_pairs={{0,24},{4,28},{8,16},{12,20},{16,8},{20,12},{24,0},{28,4},{1,25},{... | collective-permute-start | bytes 1572872 | tf_op jit(solution)/shard_map/ppermute | solution.py:44
  48.7 58.8 %collective-permute-start.39 = (bf16[128,2048]{1,0:T(8,128)(2,1)S(1)}, bf16[128,2048]{1,0:T(8,128)(2,1)}, u32[]{:S(2)}, u32[]{:S(2)}) collective-permute-start(bf16[128,2048]{1,0:T(8,128)(2,1)S(1)} %get-tuple-element.233.refs_0_), channel_id=1, source_target_pairs={{0,16},{4,20},{8,24},{12,28},{16,0},{20,4},{24,8},{28,12},{1,17},{... | collective-permute-start | bytes 1572872 | tf_op jit(solution)/shard_map/ppermute | solution.py:44
  51.8 58.7 %collective-permute-start = (bf16[128,2048]{1,0:T(8,128)(2,1)S(1)}, bf16[128,2048]{1,0:T(8,128)(2,1)}, u32[]{:S(2)}, u32[]{:S(2)}) collective-permute-start(bf16[128,2048]{1,0:T(8,128)(2,1)S(1)} %get-tuple-element.87.refs_0_), channel_id=1, source_target_pairs={{0,4},{4,0},{8,12},{12,8},{16,20},{20,16},{24,28},{28,24},{1,5},{5... | collective-permute-start | bytes 1572872 | tf_op jit(solution)/shard_map/ppermute | solution.py:44
  60.7 50.3 %collective-permute-start.2 = (bf16[128,2048]{1,0:T(8,128)(2,1)}, bf16[128,2048]{1,0:T(8,128)(2,1)}, u32[]{:S(2)}, u32[]{:S(2)}) collective-permute-start(bf16[128,2048]{1,0:T(8,128)(2,1)} %collective-permute-done.1.refs_2_), channel_id=1, source_target_pairs={{0,4},{4,0},{8,12},{12,8},{16,20},{20,16},{24,28},{28,24},{1,5},{5... | collective-permute-start | bytes 1572872 | tf_op jit(solution)/shard_map/ppermute | solution.py:44
  107.5 29.7 %collective-permute-start.16 = (bf16[128,2048]{1,0:T(8,128)(2,1)}, bf16[128,2048]{1,0:T(8,128)(2,1)}, u32[]{:S(2)}, u32[]{:S(2)}) collective-permute-start(bf16[128,2048]{1,0:T(8,128)(2,1)} %get-tuple-element.89.refs_8_), channel_id=1, source_target_pairs={{0,8},{4,12},{8,0},{12,4},{16,24},{20,28},{24,16},{28,20},{1,9},{5... | collective-permute-start | bytes 1572872 | tf_op jit(solution)/shard_map/ppermute | solution.py:44
  111.0 43.1 %collective-permute-start.41 = (bf16[128,2048]{1,0:T(8,128)(2,1)}, bf16[128,2048]{1,0:T(8,128)(2,1)}, u32[]{:S(2)}, u32[]{:S(2)}) collective-permute-start(bf16[128,2048]{1,0:T(8,128)(2,1)} %collective-permute-done.14.refs_6_), channel_id=1, source_target_pairs={{0,4},{4,0},{8,12},{12,8},{16,20},{20,16},{24,28},{28,24},{1,5},{5... | collective-permute-start | bytes 1572872 | tf_op jit(solution)/shard_map/ppermute | solution.py:44
  113.0 39.1 %collective-permute-start.40 = (bf16[128,2048]{1,0:T(8,128)(2,1)}, bf16[128,2048]{1,0:T(8,128)(2,1)}, u32[]{:S(2)}, u32[]{:S(2)}) collective-permute-start(bf16[128,2048]{1,0:T(8,128)(2,1)} %collective-permute-done.39.refs_4_), channel_id=1, source_target_pairs={{0,4},{4,0},{8,12},{12,8},{16,20},{20,16},{24,28},{28,24},{1,5},{5... | collective-permute-start | bytes 1572872 | tf_op jit(solution)/shard_map/ppermute | solution.py:44
  127.1 39.7 %all-to-all-start.1 = ((bf16[8,128,256]{2,1,0:T(8,128)(2,1)}), bf16[8,128,256]{2,1,0:T(8,128)(2,1)S(1)}, u32[]{:S(2)}, u32[]{:S(2)}) async-start(bf16[8,128,256]{2,1,0:T(8,128)(2,1)} %get-tuple-element.88), calls=%async_computation.1 | async-start | bytes 1048576 | tf_op jit(solution)/shard_map/all_to_all | solution.py:102
  137.2 40.9 %collective-permute-start.15 = (bf16[128,2048]{1,0:T(8,128)(2,1)}, bf16[128,2048]{1,0:T(8,128)(2,1)S(1)}, u32[]{:S(2)}, u32[]{:S(2)}) collective-permute-start(bf16[128,2048]{1,0:T(8,128)(2,1)} %get-tuple-element.89.refs_8_), channel_id=1, source_target_pairs={{0,4},{4,0},{8,12},{12,8},{16,20},{20,16},{24,28},{28,24},{1,5},{5... | collective-permute-start | bytes 1572872 | tf_op jit(solution)/shard_map/ppermute | solution.py:44
  138.7 42.3 %collective-permute-start.20 = (bf16[128,2048]{1,0:T(8,128)(2,1)}, bf16[128,2048]{1,0:T(8,128)(2,1)}, u32[]{:S(2)}, u32[]{:S(2)}) collective-permute-start(bf16[128,2048]{1,0:T(8,128)(2,1)} %get-tuple-element.89.refs_8_), channel_id=1, source_target_pairs={{0,24},{4,28},{8,16},{12,20},{16,8},{20,12},{24,0},{28,4},{1,25},{... | collective-permute-start | bytes 1572872 | tf_op jit(solution)/shard_map/ppermute | solution.py:44
  140.8 44.2 %collective-permute-start.17 = (bf16[128,2048]{1,0:T(8,128)(2,1)}, bf16[128,2048]{1,0:T(8,128)(2,1)}, u32[]{:S(2)}, u32[]{:S(2)}) collective-permute-start(bf16[128,2048]{1,0:T(8,128)(2,1)} %collective-permute-done.16.refs_10_), channel_id=1, source_target_pairs={{0,4},{4,0},{8,12},{12,8},{16,20},{20,16},{24,28},{28,24},{1,5},{5... | collective-permute-start | bytes 1572872 | tf_op jit(solution)/shard_map/ppermute | solution.py:44
  152.2 40.0 %collective-permute-start.19 = (bf16[128,2048]{1,0:T(8,128)(2,1)}, bf16[128,2048]{1,0:T(8,128)(2,1)}, u32[]{:S(2)}, u32[]{:S(2)}) collective-permute-start(bf16[128,2048]{1,0:T(8,128)(2,1)} %collective-permute-done.18.refs_12_), channel_id=1, source_target_pairs={{0,4},{4,0},{8,12},{12,8},{16,20},{20,16},{24,28},{28,24},{1,5},{5... | collective-permute-start | bytes 1572872 | tf_op jit(solution)/shard_map/ppermute | solution.py:44
  166.8 58.6 %all-to-all-start.3 = ((bf16[8,128,256]{2,1,0:T(8,128)(2,1)}), bf16[8,128,256]{2,1,0:T(8,128)(2,1)}, u32[]{:S(2)}, u32[]{:S(2)}) async-start(bf16[8,128,256]{2,1,0:T(8,128)(2,1)} %get-tuple-element.116), calls=%async_computation.3 | async-start | bytes 1048576 | tf_op jit(solution)/shard_map/all_to_all | solution.py:102
  178.1 37.5 %collective-permute-start.10 = (bf16[128,2048]{1,0:T(8,128)(2,1)}, bf16[128,2048]{1,0:T(8,128)(2,1)}, u32[]{:S(2)}, u32[]{:S(2)}) collective-permute-start(bf16[128,2048]{1,0:T(8,128)(2,1)} %multiply_convert_fusion.1.refs_0_), channel_id=1, source_target_pairs={{0,16},{4,20},{8,24},{12,28},{16,0},{20,4},{24,8},{28,12},{1,17},{... | collective-permute-start | bytes 1572872 | tf_op jit(solution)/shard_map/ppermute | solution.py:44
  181.0 42.9 %collective-permute-start.12 = (bf16[128,2048]{1,0:T(8,128)(2,1)}, bf16[128,2048]{1,0:T(8,128)(2,1)}, u32[]{:S(2)}, u32[]{:S(2)}) collective-permute-start(bf16[128,2048]{1,0:T(8,128)(2,1)} %multiply_convert_fusion.1.refs_0_), channel_id=1, source_target_pairs={{0,24},{4,28},{8,16},{12,20},{16,8},{20,12},{24,0},{28,4},{1,25},{... | collective-permute-start | bytes 1572872 | tf_op jit(solution)/shard_map/ppermute | solution.py:44
  185.1 45.3 %collective-permute-start.21 = (bf16[128,2048]{1,0:T(8,128)(2,1)}, bf16[128,2048]{1,0:T(8,128)(2,1)}, u32[]{:S(2)}, u32[]{:S(2)}) collective-permute-start(bf16[128,2048]{1,0:T(8,128)(2,1)} %collective-permute-done.20.refs_14_), channel_id=1, source_target_pairs={{0,4},{4,0},{8,12},{12,8},{16,20},{20,16},{24,28},{28,24},{1,5},{5... | collective-permute-start | bytes 1572872 | tf_op jit(solution)/shard_map/ppermute | solution.py:44
  192.2 38.3 %collective-permute-start.7 = (bf16[128,2048]{1,0:T(8,128)(2,1)}, bf16[128,2048]{1,0:T(8,128)(2,1)}, u32[]{:S(2)}, u32[]{:S(2)}) collective-permute-start(bf16[128,2048]{1,0:T(8,128)(2,1)} %multiply_convert_fusion.1.refs_0_), channel_id=1, source_target_pairs={{0,4},{4,0},{8,12},{12,8},{16,20},{20,16},{24,28},{28,24},{1,5},{5... | collective-permute-start | bytes 1572872 | tf_op jit(solution)/shard_map/ppermute | solution.py:44
  197.6 35.8 %collective-permute-start.9 = (bf16[128,2048]{1,0:T(8,128)(2,1)}, bf16[128,2048]{1,0:T(8,128)(2,1)}, u32[]{:S(2)}, u32[]{:S(2)}) collective-permute-start(bf16[128,2048]{1,0:T(8,128)(2,1)} %collective-permute-done.8.refs_2_), channel_id=1, source_target_pairs={{0,4},{4,0},{8,12},{12,8},{16,20},{20,16},{24,28},{28,24},{1,5},{5... | collective-permute-start | bytes 1572872 | tf_op jit(solution)/shard_map/ppermute | solution.py:44
  230.4 122.7 %collective-permute-start.50 = (bf16[128,2048]{1,0:T(8,128)(2,1)}, bf16[128,2048]{1,0:T(8,128)(2,1)}, u32[]{:S(2)}, u32[]{:S(2)}) collective-permute-start(bf16[128,2048]{1,0:T(8,128)(2,1)} %get-tuple-element.117.refs_8_), channel_id=1, source_target_pairs={{0,8},{4,12},{8,0},{12,4},{16,24},{20,28},{24,16},{28,20},{1,9},{5... | collective-permute-start | bytes 1572872 | tf_op jit(solution)/shard_map/ppermute | solution.py:44
  230.4 122.9 %collective-permute-start.52 = (bf16[128,2048]{1,0:T(8,128)(2,1)}, bf16[128,2048]{1,0:T(8,128)(2,1)}, u32[]{:S(2)}, u32[]{:S(2)}) collective-permute-start(bf16[128,2048]{1,0:T(8,128)(2,1)} %get-tuple-element.117.refs_8_), channel_id=1, source_target_pairs={{0,16},{4,20},{8,24},{12,28},{16,0},{20,4},{24,8},{28,12},{1,17},{... | collective-permute-start | bytes 1572872 | tf_op jit(solution)/shard_map/ppermute | solution.py:44
  315.9 37.4 %all-to-all-start.2 = ((f32[8,2,128]{2,1,0:T(2,128)}), f32[8,2,128]{2,1,0:T(2,128)S(1)}, u32[]{:S(2)}, u32[]{:S(2)}) async-start(f32[8,2,128]{2,1,0:T(2,128)} %copy.127), calls=%async_computation.2 | async-start | bytes 16384 | tf_op jit(solution)/shard_map/all_to_all | solution.py:102
  321.2 626.8 %reduce-scatter.4.cloned.1.call-start = ((), (), s32[]{:S(2)}) async-start(), calls=%async_computation.18 | async-start | bytes 10485760 | tf_op jit(solution)/shard_map/reduce_scatter | solution.py:549
  326.3 33.8 %collective-permute-start.22 = (bf16[128,2048]{1,0:T(8,128)(2,1)}, bf16[128,2048]{1,0:T(8,128)(2,1)}, u32[]{:S(2)}, u32[]{:S(2)}) collective-permute-start(bf16[128,2048]{1,0:T(8,128)(2,1)} %get-tuple-element.93), channel_id=1, source_target_pairs={{0,4},{4,0},{8,12},{12,8},{16,20},{20,16},{24,28},{28,24},{1,5},{5... | collective-permute-start | bytes 1572872 | tf_op jit(solution)/shard_map/ppermute | solution.py:44
  337.5 36.1 %collective-permute-start.28 = (bf16[128,2048]{1,0:T(8,128)(2,1)S(1)}, bf16[128,2048]{1,0:T(8,128)(2,1)}, u32[]{:S(2)}, u32[]{:S(2)}) collective-permute-start(bf16[128,2048]{1,0:T(8,128)(2,1)S(1)} %add_convert_fusion.15), channel_id=1, source_target_pairs={{0,24},{4,28},{8,16},{12,20},{16,8},{20,12},{24,0},{28,4},{1,25},{... | collective-permute-start | bytes 1572872 | tf_op jit(solution)/shard_map/ppermute | solution.py:44
  348.8 52.8 %collective-permute-start.26 = (bf16[128,2048]{1,0:T(8,128)(2,1)S(1)}, bf16[128,2048]{1,0:T(8,128)(2,1)}, u32[]{:S(2)}, u32[]{:S(2)}) collective-permute-start(bf16[128,2048]{1,0:T(8,128)(2,1)S(1)} %add_convert_fusion.16), channel_id=1, source_target_pairs={{0,16},{4,20},{8,24},{12,28},{16,0},{20,4},{24,8},{28,12},{1,17},{... | collective-permute-start | bytes 1572872 | tf_op jit(solution)/shard_map/ppermute | solution.py:44
  353.1 49.4 %collective-permute-start.24 = (bf16[128,2048]{1,0:T(8,128)(2,1)}, bf16[128,2048]{1,0:T(8,128)(2,1)}, u32[]{:S(2)}, u32[]{:S(2)}) collective-permute-start(bf16[128,2048]{1,0:T(8,128)(2,1)} %add_convert_fusion.17), channel_id=1, source_target_pairs={{0,8},{4,12},{8,0},{12,4},{16,24},{20,28},{24,16},{28,20},{1,9},{5... | collective-permute-start | bytes 1572872 | tf_op jit(solution)/shard_map/ppermute | solution.py:44
  353.4 56.2 %collective-permute-start.49 = (bf16[128,2048]{1,0:T(8,128)(2,1)}, bf16[128,2048]{1,0:T(8,128)(2,1)S(1)}, u32[]{:S(2)}, u32[]{:S(2)}) collective-permute-start(bf16[128,2048]{1,0:T(8,128)(2,1)} %get-tuple-element.117.refs_8_), channel_id=1, source_target_pairs={{0,4},{4,0},{8,12},{12,8},{16,20},{20,16},{24,28},{28,24},{1,5},{5... | collective-permute-start | bytes 1572872 | tf_op jit(solution)/shard_map/ppermute | solution.py:44
  360.1 53.9 %collective-permute-start.54 = (bf16[128,2048]{1,0:T(8,128)(2,1)}, bf16[128,2048]{1,0:T(8,128)(2,1)S(1)}, u32[]{:S(2)}, u32[]{:S(2)}) collective-permute-start(bf16[128,2048]{1,0:T(8,128)(2,1)} %get-tuple-element.117.refs_8_), channel_id=1, source_target_pairs={{0,24},{4,28},{8,16},{12,20},{16,8},{20,12},{24,0},{28,4},{1,25},{... | collective-permute-start | bytes 1572872 | tf_op jit(solution)/shard_map/ppermute | solution.py:44
  373.6 41.7 %collective-permute-start.51 = (bf16[128,2048]{1,0:T(8,128)(2,1)}, bf16[128,2048]{1,0:T(8,128)(2,1)S(1)}, u32[]{:S(2)}, u32[]{:S(2)}) collective-permute-start(bf16[128,2048]{1,0:T(8,128)(2,1)} %collective-permute-done.50.refs_10_), channel_id=1, source_target_pairs={{0,4},{4,0},{8,12},{12,8},{16,20},{20,16},{24,28},{28,24},{1,5},{5... | collective-permute-start | bytes 1572872 | tf_op jit(solution)/shard_map/ppermute | solution.py:44
  414.0 28.8 %collective-permute-start.47 = (bf16[128,2048]{1,0:T(8,128)(2,1)S(1)}, bf16[128,2048]{1,0:T(8,128)(2,1)S(1)}, u32[]{:S(2)}, u32[]{:S(2)}) collective-permute-start(bf16[128,2048]{1,0:T(8,128)(2,1)S(1)} %get-tuple-element.243.refs_0_), channel_id=1, source_target_pairs={{0,24},{4,28},{8,16},{12,20},{16,8},{20,12},{24,0},{28,4},{1,25},{... | collective-permute-start | bytes 1572872 | tf_op jit(solution)/shard_map/ppermute | solution.py:44
  415.3 29.4 %collective-permute-start.55 = (bf16[128,2048]{1,0:T(8,128)(2,1)S(1)}, bf16[128,2048]{1,0:T(8,128)(2,1)S(1)}, u32[]{:S(2)}, u32[]{:S(2)}) collective-permute-start(bf16[128,2048]{1,0:T(8,128)(2,1)S(1)} %collective-permute-done.54.refs_14_), channel_id=1, source_target_pairs={{0,4},{4,0},{8,12},{12,8},{16,20},{20,16},{24,28},{28,24},{1,5},{5... | collective-permute-start | bytes 1572872 | tf_op jit(solution)/shard_map/ppermute | solution.py:44
  419.6 33.0 %collective-permute-start.44 = (bf16[128,2048]{1,0:T(8,128)(2,1)S(1)}, bf16[128,2048]{1,0:T(8,128)(2,1)S(1)}, u32[]{:S(2)}, u32[]{:S(2)}) collective-permute-start(bf16[128,2048]{1,0:T(8,128)(2,1)S(1)} %collective-permute-done.43.refs_2_), channel_id=1, source_target_pairs={{0,4},{4,0},{8,12},{12,8},{16,20},{20,16},{24,28},{28,24},{1,5},{5... | collective-permute-start | bytes 1572872 | tf_op jit(solution)/shard_map/ppermute | solution.py:44
  537.3 414.7 %reduce-scatter.6.cloned.1.call-start = ((), (), s32[]{:S(2)}) async-start(), calls=%async_computation.19 | async-start | bytes 10485760 | tf_op jit(solution)/shard_map/reduce_scatter | solution.py:549
  558.2 30.3 %all-to-all-start.4 = ((f32[8,2,128]{2,1,0:T(2,128)}), f32[8,2,128]{2,1,0:T(2,128)S(1)}, u32[]{:S(2)}, u32[]{:S(2)}) async-start(f32[8,2,128]{2,1,0:T(2,128)} %copy.129), calls=%async_computation.4 | async-start | bytes 16384 | tf_op jit(solution)/shard_map/all_to_all | solution.py:102
  562.9 393.2 %reduce-scatter.8.cloned.1.call-start = ((), (), s32[]{:S(2)}) async-start(), calls=%async_computation.20 | async-start | bytes 10485760 | tf_op jit(solution)/shard_map/reduce_scatter | solution.py:549
  627.7 29.4 %collective-permute-start.63 = (bf16[128,2048]{1,0:T(8,128)(2,1)}, bf16[128,2048]{1,0:T(8,128)(2,1)}, u32[]{:S(2)}, u32[]{:S(2)}) collective-permute-start(bf16[128,2048]{1,0:T(8,128)(2,1)} %get-tuple-element.135), channel_id=1, source_target_pairs={{0,4},{4,0},{8,12},{12,8},{16,20},{20,16},{24,28},{28,24},{1,5},{5... | collective-permute-start | bytes 1572872 | tf_op jit(solution)/shard_map/ppermute | solution.py:44
  630.7 35.7 %collective-permute-start.69 = (bf16[128,2048]{1,0:T(8,128)(2,1)}, bf16[128,2048]{1,0:T(8,128)(2,1)}, u32[]{:S(2)}, u32[]{:S(2)}) collective-permute-start(bf16[128,2048]{1,0:T(8,128)(2,1)} %add_convert_fusion.2), channel_id=1, source_target_pairs={{0,24},{4,28},{8,16},{12,20},{16,8},{20,12},{24,0},{28,4},{1,25},{... | collective-permute-start | bytes 1572872 | tf_op jit(solution)/shard_map/ppermute | solution.py:44
  637.9 35.0 %collective-permute-start.67 = (bf16[128,2048]{1,0:T(8,128)(2,1)}, bf16[128,2048]{1,0:T(8,128)(2,1)}, u32[]{:S(2)}, u32[]{:S(2)}) collective-permute-start(bf16[128,2048]{1,0:T(8,128)(2,1)} %add_convert_fusion.3), channel_id=1, source_target_pairs={{0,16},{4,20},{8,24},{12,28},{16,0},{20,4},{24,8},{28,12},{1,17},{... | collective-permute-start | bytes 1572872 | tf_op jit(solution)/shard_map/ppermute | solution.py:44
  652.8 34.7 %all-to-all-start.10 = ((bf16[4,2,128,8,64]{2,4,3,1,0:T(8,128)(2,1)}), bf16[4,2,128,8,64]{2,4,3,1,0:T(8,128)(2,1)}, u32[]{:S(2)}, u32[]{:S(2)}) async-start(bf16[4,2,128,8,64]{2,4,3,1,0:T(8,128)(2,1)} %copy.147), calls=%async_computation.10 | async-start | bytes 2097152 | tf_op jit(solution)/shard_map/all_to_all | solution.py:102
  687.4 28.8 %all-to-all-start.7 = ((bf16[8,128,256]{2,1,0:T(8,128)(2,1)}), bf16[8,128,256]{2,1,0:T(8,128)(2,1)}, u32[]{:S(2)}, u32[]{:S(2)}) async-start(bf16[8,128,256]{2,1,0:T(8,128)(2,1)} %bitcast.42), calls=%async_computation.7 | async-start | bytes 1048576 | tf_op jit(solution)/shard_map/all_to_all | solution.py:102
  703.0 73.4 %collective-permute-start.32 = (bf16[128,2048]{1,0:T(8,128)(2,1)}, bf16[128,2048]{1,0:T(8,128)(2,1)}, u32[]{:S(2)}, u32[]{:S(2)}) collective-permute-start(bf16[128,2048]{1,0:T(8,128)(2,1)} %get-tuple-element.111), channel_id=1, source_target_pairs={{0,4},{4,0},{8,12},{12,8},{16,20},{20,16},{24,28},{28,24},{1,5},{5... | collective-permute-start | bytes 1572872 | tf_op jit(solution)/shard_map/ppermute | solution.py:44
  703.6 96.5 %collective-permute-start.30 = (bf16[128,2048]{1,0:T(8,128)(2,1)}, bf16[128,2048]{1,0:T(8,128)(2,1)}, u32[]{:S(2)}, u32[]{:S(2)}) collective-permute-start(bf16[128,2048]{1,0:T(8,128)(2,1)} %get-tuple-element.107), channel_id=1, source_target_pairs={{0,4},{4,0},{8,12},{12,8},{16,20},{20,16},{24,28},{28,24},{1,5},{5... | collective-permute-start | bytes 1572872 | tf_op jit(solution)/shard_map/ppermute | solution.py:44
  727.9 51.0 %collective-permute-start.73 = (bf16[256,2048]{1,0:T(8,128)(2,1)}, bf16[256,2048]{1,0:T(8,128)(2,1)}, u32[]{:S(2)}, u32[]{:S(2)}) collective-permute-start(bf16[256,2048]{1,0:T(8,128)(2,1)} %get-tuple-element.235), channel_id=1, source_target_pairs={{0,1},{1,0},{2,3},{3,2},{4,5},{5,4},{6,7},{7,6},{8,9},{9,8},{10,11... | collective-permute-start | bytes 3145736 | tf_op jit(solution)/shard_map/ppermute | solution.py:44
  727.9 48.5 %collective-permute-start.74 = (bf16[256,2048]{1,0:T(8,128)(2,1)}, bf16[256,2048]{1,0:T(8,128)(2,1)S(1)}, u32[]{:S(2)}, u32[]{:S(2)}) collective-permute-start(bf16[256,2048]{1,0:T(8,128)(2,1)} %get-tuple-element.235), channel_id=1, source_target_pairs={{0,2},{1,3},{2,0},{3,1},{4,6},{5,7},{6,4},{7,5},{8,10},{9,11},{10,... | collective-permute-start | bytes 3145736 | tf_op jit(solution)/shard_map/ppermute | solution.py:44
  743.5 42.4 %all-to-all-start.8 = ((bf16[8,128,768]{2,1,0:T(8,128)(2,1)}), bf16[8,128,768]{2,1,0:T(8,128)(2,1)}, u32[]{:S(2)}, u32[]{:S(2)}) async-start(bf16[8,128,768]{2,1,0:T(8,128)(2,1)} %get-tuple-element.153), calls=%async_computation.8 | async-start | bytes 3145728 | tf_op jit(solution)/shard_map/all_to_all | solution.py:102
  778.4 52.3 %collective-permute-start.70 = (bf16[1,8,64,768]{3,2,1,0:T(8,128)(2,1)}, bf16[1,8,64,768]{3,2,1,0:T(8,128)(2,1)}, u32[]{:S(2)}, u32[]{:S(2)}) collective-permute-start(bf16[1,8,64,768]{3,2,1,0:T(8,128)(2,1)} %get-tuple-element.221), channel_id=1, source_target_pairs={{0,1},{1,0},{2,3},{3,2},{4,5},{5,4},{6,7},{7,6},{8,9},{9,8},{10,11... | collective-permute-start | bytes 2359304 | tf_op jit(solution)/shard_map/ppermute | solution.py:44
  783.4 50.8 %collective-permute-start.72 = (bf16[1,8,64,768]{3,2,1,0:T(8,128)(2,1)}, bf16[1,8,64,768]{3,2,1,0:T(8,128)(2,1)}, u32[]{:S(2)}, u32[]{:S(2)}) collective-permute-start(bf16[1,8,64,768]{3,2,1,0:T(8,128)(2,1)} %fusion.5), channel_id=1, source_target_pairs={{0,2},{1,3},{2,0},{3,1},{4,6},{5,7},{6,4},{7,5},{8,10},{9,11},{10,... | collective-permute-start | bytes 2359304 | tf_op jit(solution)/shard_map/ppermute | solution.py:44
  785.9 100.3 %all-to-all-start.6 = ((bf16[8,128,768]{2,1,0:T(8,128)(2,1)}), bf16[8,128,768]{2,1,0:T(8,128)(2,1)}, u32[]{:S(2)}, u32[]{:S(2)}) async-start(bf16[8,128,768]{2,1,0:T(8,128)(2,1)} %get-tuple-element.150), calls=%async_computation.6 | async-start | bytes 3145728 | tf_op jit(solution)/shard_map/all_to_all | solution.py:102
  800.0 28.8 %collective-permute-start.79 = (bf16[64,2048]{1,0:T(8,128)(2,1)}, bf16[64,2048]{1,0:T(8,128)(2,1)}, u32[]{:S(2)}, u32[]{:S(2)}) collective-permute-start(bf16[64,2048]{1,0:T(8,128)(2,1)} %get-tuple-element.225), channel_id=1, source_target_pairs={{0,4},{4,0},{8,12},{12,8},{16,20},{20,16},{24,28},{28,24},{1,5},{5... | collective-permute-start | bytes 786440 | tf_op jit(solution)/shard_map/ppermute | solution.py:44
  813.7 113.0 %collective-permute-start.29 = (bf16[128,2048]{1,0:T(8,128)(2,1)}, bf16[128,2048]{1,0:T(8,128)(2,1)}, u32[]{:S(2)}, u32[]{:S(2)}) collective-permute-start(bf16[128,2048]{1,0:T(8,128)(2,1)} %get-tuple-element.103), channel_id=1, source_target_pairs={{0,4},{4,0},{8,12},{12,8},{16,20},{20,16},{24,28},{28,24},{1,5},{5... | collective-permute-start | bytes 1572872 | tf_op jit(solution)/shard_map/ppermute | solution.py:44
  830.4 35.9 %collective-permute-start.82 = (bf16[64,2048]{1,0:T(8,128)(2,1)S(1)}, bf16[64,2048]{1,0:T(8,128)(2,1)S(1)}, u32[]{:S(2)}, u32[]{:S(2)}) collective-permute-start(bf16[64,2048]{1,0:T(8,128)(2,1)S(1)} %get-tuple-element.228), channel_id=1, source_target_pairs={{0,24},{4,28},{8,16},{12,20},{16,8},{20,12},{24,0},{28,4},{1,25},{... | collective-permute-start | bytes 786440 | tf_op jit(solution)/shard_map/ppermute | solution.py:44
  830.7 46.0 %collective-permute-start.80 = (bf16[64,2048]{1,0:T(8,128)(2,1)S(1)}, bf16[64,2048]{1,0:T(8,128)(2,1)S(1)}, u32[]{:S(2)}, u32[]{:S(2)}) collective-permute-start(bf16[64,2048]{1,0:T(8,128)(2,1)S(1)} %get-tuple-element.229), channel_id=1, source_target_pairs={{0,16},{4,20},{8,24},{12,28},{16,0},{20,4},{24,8},{28,12},{1,17},{... | collective-permute-start | bytes 786440 | tf_op jit(solution)/shard_map/ppermute | solution.py:44
  834.1 44.9 %collective-permute-start.78 = (bf16[64,2048]{1,0:T(8,128)(2,1)S(1)}, bf16[64,2048]{1,0:T(8,128)(2,1)S(1)}, u32[]{:S(2)}, u32[]{:S(2)}) collective-permute-start(bf16[64,2048]{1,0:T(8,128)(2,1)S(1)} %get-tuple-element.227), channel_id=1, source_target_pairs={{0,8},{4,12},{8,0},{12,4},{16,24},{20,28},{24,16},{28,20},{1,9},{5... | collective-permute-start | bytes 786440 | tf_op jit(solution)/shard_map/ppermute | solution.py:44
  844.2 82.6 %collective-permute-start.35 = (bf16[128,2048]{1,0:T(8,128)(2,1)}, bf16[128,2048]{1,0:T(8,128)(2,1)}, u32[]{:S(2)}, u32[]{:S(2)}) collective-permute-start(bf16[128,2048]{1,0:T(8,128)(2,1)} %add_convert_fusion.11), channel_id=1, source_target_pairs={{0,24},{4,28},{8,16},{12,20},{16,8},{20,12},{24,0},{28,4},{1,25},{... | collective-permute-start | bytes 1572872 | tf_op jit(solution)/shard_map/ppermute | solution.py:44
  866.3 60.5 %collective-permute-start.33 = (bf16[128,2048]{1,0:T(8,128)(2,1)}, bf16[128,2048]{1,0:T(8,128)(2,1)}, u32[]{:S(2)}, u32[]{:S(2)}) collective-permute-start(bf16[128,2048]{1,0:T(8,128)(2,1)} %add_convert_fusion.12), channel_id=1, source_target_pairs={{0,16},{4,20},{8,24},{12,28},{16,0},{20,4},{24,8},{28,12},{1,17},{... | collective-permute-start | bytes 1572872 | tf_op jit(solution)/shard_map/ppermute | solution.py:44
  876.7 50.0 %collective-permute-start.31 = (bf16[128,2048]{1,0:T(8,128)(2,1)}, bf16[128,2048]{1,0:T(8,128)(2,1)}, u32[]{:S(2)}, u32[]{:S(2)}) collective-permute-start(bf16[128,2048]{1,0:T(8,128)(2,1)} %add_convert_fusion.13), channel_id=1, source_target_pairs={{0,8},{4,12},{8,0},{12,4},{16,24},{20,28},{24,16},{28,20},{1,9},{5... | collective-permute-start | bytes 1572872 | tf_op jit(solution)/shard_map/ppermute | solution.py:44
  886.2 45.1 %all-to-all-start.9 = ((bf16[8,64,768]{2,1,0:T(8,128)(2,1)}), bf16[8,64,768]{2,1,0:T(8,128)(2,1)}, u32[]{:S(2)}, u32[]{:S(2)}) async-start(bf16[8,64,768]{2,1,0:T(8,128)(2,1)} %fusion.27), calls=%async_computation.9 | async-start | bytes 1572864 | tf_op jit(solution)/shard_map/all_to_all | solution.py:102
  (109 other events, 2365.1 us)
Sparse Core Ops, SparseCore 0:
  9.6 59.4 all-gather.3
  70.6 58.2 all-gather.5
  130.5 58.2 all-gather.7
  537.4 71.0 reduce-scatter.3
  611.2 82.9 reduce-scatter.5
  696.6 97.3 reduce-scatter.7

commit v3 on v2

--- a/solution.py
+++ b/solution.py
@@ -64,23 +64,24 @@
     return gather_second(gather_first(value, axis), axis)
 
 
-def scatter_first(blocks, axis):
-    return {
-        k: (blocks[k].astype(F32) + hop(blocks[k + 1], axis, 1).astype(F32)).astype(LOW)
-        for k in range(len(blocks) - 2, -1, -2)
-    }
-
-
-def scatter_second(half, axis):
-    total = half[0].astype(F32)
-    for k in sorted(half):
-        if k:
-            total = total + hop(half[k], axis, k).astype(F32)
-    return total
+def far_sum(half, received):
+    return half[0].astype(F32) + sum(x.astype(F32) for x in received)
+
+
+def near_sums(keep, received):
+    return [(k.astype(F32) + r.astype(F32)).astype(LOW) for k, r in zip(keep, received)]
+
+
+def far_sends(half, after):
+    return [hop(tie(half[j], *after), "expert", 2 * j) for j in range(1, len(half))]
 
 
 def scatter_blocks(blocks, axis):
-    return scatter_second(scatter_first(blocks, axis), axis)
+    half = [
+        (blocks[k].astype(F32) + hop(blocks[k + 1], axis, 1).astype(F32)).astype(LOW)
+        for k in range(0, len(blocks), 2)
+    ]
+    return far_sum(half, [hop(half[j], axis, 2 * j) for j in range(1, len(half))])
 
 
 def place_blocks(blocks, own, dim):
@@ -122,23 +123,33 @@
     return mm(a, b, ((1,), (1,)))
 
 
-def expert_kernel(n, tile, shared, own_ref, *refs):
-    xs, cs = refs[:n], refs[n : 2 * n]
-    pick_ref, turned_ref, router_ref, gate_ref, up_ref, down_ref = refs[2 * n : 2 * n + 6]
-    outs = refs[2 * n + 6 + shared :]
-    moe, dsum = outs[:n], outs[n : 2 * n]
-    buffer_ref, d_result_ref, hidden_ref, dg_ref, du_ref, d_gate_ref = outs[2 * n : 2 * n + 6]
-    acc_res, acc_db, grad_rows, gate_cols = outs[2 * n + 6 :]
+def expert_kernel(n, tile, grads_near, shared, own_ref, *refs):
+    refs = list(refs)
+
+    def take(count):
+        out = refs[:count]
+        del refs[:count]
+        return out
+
+    near, (far_ref,) = take(n // 2), take(1)
+    grads = take(n // 2 + 1) if grads_near else take(1)
+    pick_ref, turned_ref, router_ref, gate_ref, up_ref, down_ref = take(6)
+    take(shared)
+    buffer_ref, d_result_ref, hidden_ref, dg_ref, du_ref, moe_ref = take(6)
+    d_keep, d_send = take(2)
+    acc_res, acc_db, grad_rows, gate_cols = take(4)
     own = own_ref[0]
     expert, step, steps = pl.program_id(0), pl.program_id(1), pl.num_programs(1)
-    cap = pick_ref.shape[3]
-    index = own * pl.num_programs(0) + expert
+    count = pl.num_programs(0)
+    cap, rows = pick_ref.shape[3:]
+    width = acc_res.shape[1]
+    index = own * count + expert
 
     @pl.when(step == 0)
     def _():
         for k in range(n):
             span = pl.ds(k * cap, cap)
-            block = xs[k][...]
+            block = far_ref[k // 2] if k % 2 else near[k // 2][...]
             pick = pick_ref[0, 0, own ^ k]
             buffer_ref[0, span, :] = mm(pick, block).astype(LOW)
             logits = mm_nt(router_ref[...], block)
@@ -147,9 +158,13 @@
             lines = lax.broadcasted_iota(jnp.int32, router.shape, 0)
             row = jnp.sum(jnp.where(lines == index, router, 0.0), axis=0, keepdims=True)
             col = jnp.sum(pick.astype(F32) * row, axis=1, keepdims=True)
-            grads = mm(pick, cs[k][...])
-            grad_rows[span, :] = grads.astype(LOW)
-            d_result_ref[0, span, :] = (col * grads).astype(LOW)
+            if grads_near:
+                block = grads[-1][k // 2] if k % 2 else grads[k // 2][...]
+            else:
+                block = grads[0][own ^ k]
+            block = mm(pick, block)
+            grad_rows[span, :] = block.astype(LOW)
+            d_result_ref[0, span, :] = (col * block).astype(LOW)
             gate_cols[span, :] = jnp.broadcast_to(col, (cap, gate_cols.shape[1]))
 
     slots = n * cap
@@ -161,12 +176,10 @@
         d_hidden = mm_nt(d_result_ref[0, span, :], down_ref[0])
         sig = 1.0 / (1.0 + jnp.exp(-gate_act))
         silu = gate_act * sig
-        hidden = (silu * up_act).astype(LOW)
-        dg = (d_hidden * up_act * (sig * (1.0 + gate_act * (1.0 - sig)))).astype(LOW)
-        du = (d_hidden * silu).astype(LOW)
-        hidden_ref[0, span, :] = hidden
-        dg_ref[0, span, :] = dg
-        du_ref[0, span, :] = du
+        hidden_ref[0, span, :] = (silu * up_act).astype(LOW)
+        slope = sig * (1.0 + gate_act * (1.0 - sig))
+        dg_ref[0, span, :] = (d_hidden * up_act * slope).astype(LOW)
+        du_ref[0, span, :] = (d_hidden * silu).astype(LOW)
 
         @pl.when(step == 0)
         def _():
@@ -184,60 +197,78 @@
 
     @pl.when(step == steps - 1)
     def _():
-        lines = lax.broadcasted_iota(jnp.int32, d_gate_ref.shape[1:], 0)
-        d_gate = jnp.zeros(d_gate_ref.shape[1:], F32)
+        lines = count * n * rows // width
+        place = index * rows
+        line, column = place // width, place % width
+        shape = (d_keep.shape[1] - rows, width)
+        at_line = lax.broadcasted_iota(jnp.int32, shape, 0)
+        at_column = lax.broadcasted_iota(jnp.int32, shape, 1)
+        here = (at_column >= column) & (at_column < column + rows)
         for k in range(n):
             span = pl.ds(k * cap, cap)
+            out = d_send if k % 2 else d_keep
             pick = pick_ref[0, 0, own ^ k]
             turned = turned_ref[0, 0, own ^ k]
             result = acc_res[span, :].astype(LOW).astype(F32)
             col = jnp.sum(result * grad_rows[span, :].astype(F32), axis=1, keepdims=True)
             row = jnp.sum(pick.astype(F32) * col, axis=0, keepdims=True)
-            d_gate = jnp.where(lines == (own ^ k), row, d_gate)
-            scaled = (gate_cols[span, :1] * result).astype(LOW)
-            part = mm(turned, scaled)
+            high = row.astype(LOW).astype(F32)
+            high, rest = (
+                jnp.concatenate([x] * (width // rows), axis=1) for x in (high, row - high)
+            )
+            extra = jnp.where(here & (at_line == line), high, 0.0) + jnp.where(
+                here & (at_line == line + lines), rest, 0.0
+            )
+            part = mm(turned, (gate_cols[span, :1] * result).astype(LOW))
             d_part = mm(turned, acc_db[span, :].astype(LOW))
 
             @pl.when(expert == 0)
             def _():
-                moe[k][...] = part.astype(LOW)
-                dsum[k][...] = d_part.astype(LOW)
+                moe_ref[own ^ k, 0] = part.astype(LOW)
+                out[k // 2, :rows] = d_part.astype(LOW)
+                out[k // 2, rows:] = extra.astype(LOW)
 
             @pl.when(expert > 0)
             def _():
-                moe[k][...] = (moe[k][...].astype(F32) + part).astype(LOW)
-                dsum[k][...] = (dsum[k][...].astype(F32) + d_part).astype(LOW)
-
-        d_gate_ref[0] = d_gate
-
-
-def expert_layer(own, blocks, grads, pick, turned, router_turned, gate, up, down, at, micro, kept, tile=512):
-    n = len(blocks)
+                moe_ref[own ^ k, 0] = (moe_ref[own ^ k, 0].astype(F32) + part).astype(LOW)
+                out[k // 2, :rows] = (out[k // 2, :rows].astype(F32) + d_part).astype(LOW)
+                out[k // 2, rows:] = (out[k // 2, rows:].astype(F32) + extra).astype(LOW)
+
+
+def expert_layer(own, blocks, far, grads, pick, turned, router_turned, weights, at, micro, kept):
+    n = 2 * len(blocks)
     rows, width = blocks[0].shape
-    count, _, ff = gate.shape
+    count, _, ff = weights[0].shape
     cap = pick.shape[3]
     slots = n * cap
     split = 2 if n <= 8 else 4
     ft = ff // split
+    extra = 8
     one = dict(pipeline_mode=pl.Buffered(1))
     some = one if n > 8 else {}
     block = pl.BlockSpec((rows, width), lambda e, f, o: (0, 0), **one)
+
+    def stack(size, height):
+        return pl.BlockSpec((size, height, width), lambda e, f, o: (0, 0, 0), **one)
+
     row_block = pl.BlockSpec((1, slots, width), lambda e, f, o: (e, at, 0), **some)
     ff_block = pl.BlockSpec((1, slots, ft), lambda e, f, o: (e, at, f))
-    tokens_shape = jax.ShapeDtypeStruct((rows, width), LOW)
     rows_shape = jax.ShapeDtypeStruct((count, micro * slots, width), LOW)
     ff_shape = jax.ShapeDtypeStruct((count, micro * slots, ff), LOW)
+    grads_near = len(grads) > 1
     kept = [] if kept is None else list(kept)
-    before = 1 + 2 * n + 6
+    args = [*blocks, far, *grads, pick, turned, router_turned, *weights]
     outs = pl.pallas_call(
-        functools.partial(expert_kernel, n, tile, len(kept)),
-        out_shape=[tokens_shape] * (2 * n)
-        + [rows_shape, rows_shape, ff_shape, ff_shape, ff_shape]
-        + [jax.ShapeDtypeStruct((count, n, rows), F32)],
+        functools.partial(expert_kernel, n, 512, grads_near, len(kept)),
+        out_shape=[rows_shape, rows_shape, ff_shape, ff_shape, ff_shape]
+        + [jax.ShapeDtypeStruct((n, micro, rows, width), LOW)]
+        + [jax.ShapeDtypeStruct((n // 2, rows + extra, width), LOW)] * 2,
         grid_spec=pltpu.PrefetchScalarGridSpec(
             num_scalar_prefetch=1,
             grid=(count, split),
-            in_specs=[block] * (2 * n)
+            in_specs=[block] * (n // 2)
+            + [stack(n // 2, rows)]
+            + ([block] * (n // 2) + [stack(n // 2, rows)] if grads_near else [stack(n, rows)])
             + [
                 pl.BlockSpec((1, 1, n, cap, rows), lambda e, f, o: (e, at, 0, 0, 0), **some),
                 pl.BlockSpec((1, 1, n, rows, cap), lambda e, f, o: (e, at, 0, 0, 0), **some),
@@ -247,9 +278,9 @@
                 pl.BlockSpec((1, ft, width), lambda e, f, o: (e, f, 0)),
             ]
             + [pl.BlockSpec(memory_space=pl.ANY)] * len(kept),
-            out_specs=[block] * (2 * n)
-            + [row_block, row_block, ff_block, ff_block, ff_block]
-            + [pl.BlockSpec((1, n, rows), lambda e, f, o: (e, 0, 0))],
+            out_specs=[row_block, row_block, ff_block, ff_block, ff_block]
+            + [pl.BlockSpec((n, 1, rows, width), lambda e, f, o: (0, at, 0, 0), **one)]
+            + [stack(n // 2, rows + extra)] * 2,
             scratch_shapes=[
                 pltpu.VMEM((slots, width), F32),
                 pltpu.VMEM((slots, width), F32),
@@ -257,7 +288,7 @@
                 pltpu.VMEM((slots, 128), F32),
             ],
         ),
-        input_output_aliases={before + i: 2 * n + i for i in range(len(kept))},
+        input_output_aliases={1 + len(args) + i: i for i in range(len(kept))},
         compiler_params=pltpu.CompilerParams(vmem_limit_bytes=60 << 20),
         cost_estimate=pl.CostEstimate(
             flops=24 * count * slots * width * ff,
@@ -265,8 +296,8 @@
             bytes_accessed=4 * n * rows * width * 2 + 3 * count * width * ff * 2,
         ),
         name="experts",
-    )(own.reshape(1), *blocks, *grads, pick, turned, router_turned, gate, up, down, *kept)
-    return outs[:n], outs[n : 2 * n], outs[2 * n : 2 * n + 5], outs[2 * n + 5]
+    )(own.reshape(1), *args, *kept)
+    return outs[:6], outs[6], outs[7]
 
 
 def turn(x):
@@ -276,7 +307,7 @@
 def attend_kernel(n, tile, own_ref, *refs):
     xs = refs[:n]
     wq, wk, wv, gains_ref, cos_ref, sin_ref, seg_col, seg_row = refs[n : n + 8]
-    attended_ref, normed_ref, raw_ref, low_ref = refs[n + 8 :]
+    attended_ref, normed_ref, raw_ref, low_ref = refs[-4:]
     own = own_ref[0]
     rows, width = xs[0].shape
     part = wq.shape[1]
@@ -312,14 +343,20 @@
             probs = terms * (1.0 / jnp.sum(terms, axis=1, keepdims=True))
             out = mm(probs.astype(LOW), values).astype(LOW)
             for i in range(0, tile, rows):
-                attended_ref[(r + i) // rows, :, h * HEAD : (h + 1) * HEAD] = out[i : i + rows]
-
-
-def attend(own, blocks, qkv_weight, gains, cos, sin, seg, tile=512):
+                attended_ref[(r + i) // rows, :rows, h * HEAD : (h + 1) * HEAD] = out[
+                    i : i + rows
+                ]
+    if len(refs) > n + 12:
+        for k in range(n):
+            attended_ref[k, rows:, :] = refs[n + 8][...]
+
+
+def attend(own, blocks, qkv_weight, gains, cos, sin, seg, riders, tile=512):
     n = len(blocks)
     rows, width = blocks[0].shape
     part = width // n
     group = n * rows
+    more = sum(x.shape[0] for x in riders)
 
     def columns(which):
         return pl.BlockSpec((width, part), lambda i, o: (0, which * n + o[0]))
@@ -330,7 +367,7 @@
     return pl.pallas_call(
         functools.partial(attend_kernel, n, tile),
         out_shape=[
-            jax.ShapeDtypeStruct((n, rows, part), LOW),
+            jax.ShapeDtypeStruct((n, rows + more, part), LOW),
             jax.ShapeDtypeStruct((n, rows, width), LOW),
             jax.ShapeDtypeStruct((group, 2 * part), F32),
             jax.ShapeDtypeStruct((group, 3 * part), LOW),
@@ -346,9 +383,10 @@
                 whole(group, HEAD),
                 whole(group, 1),
                 whole(1, group),
-            ],
+            ]
+            + [whole(*x.shape) for x in riders],
             out_specs=[
-                whole(n, rows, part),
+                whole(n, rows + more, part),
                 whole(n, rows, width),
                 whole(group, 2 * part),
                 whole(group, 3 * part),
@@ -372,6 +410,7 @@
         sin,
         seg[:, None],
         seg[None, :],
+        *riders,
     )
 
 
@@ -493,69 +532,106 @@
     full_down = lax.all_gather(down_weight, "shard", axis=1, tiled=True)
 
     each = range(micro)
-    routes_all = swap(jnp.broadcast_to(routes[None], (n,) + routes.shape), "expert")
     inputs = [tokens[i].astype(F32) for i in each]
     normed_attn = [rms_scale(x, attn_gain).astype(LOW) for x in inputs]
-    normed_attn[0], routes_all = lax.optimization_barrier((normed_attn[0], routes_all))
+    near = [gather_first(normed_attn[0], "expert")]
+    for i in range(1, micro):
+        near.append(gather_first(tie(normed_attn[i], near[i - 1][2]), "expert"))
+    gains = head_gains.reshape(2, HEAD)
+    spots = [places(permutation[i, 0], lengths[i, 0]) for i in each]
+    turns = [angles(pos) for _, pos in spots]
+    normed_blocks = [gather_second(x, "expert") for x in near]
+    grad_near = gather_first(tie(cotangent[0], *near[-1][2::2]), "expert")[::2]
+    grad_far = hop(jnp.stack(grad_near), "expert", 1)
+    grad_rest = [
+        lax.all_gather(tie(cotangent[i], near[-1][-2]), "expert", axis=0) for i in range(1, micro)
+    ]
+    attended, normed_all, qkv_raw, qkv_low, mixed, normed_moe = ([None] * micro for _ in range(6))
+    for i in each:
+        riders = ()
+        if i == 0:
+            riders = (routes.astype(LOW).transpose(0, 2, 1).reshape(-1, part),)
+        attended[i], normed_all[i], qkv_raw[i], qkv_low[i] = attend(
+            own, normed_blocks[i], qkv_weight, gains, *turns[i], spots[i][0], riders
+        )
+        attended[i] = swap(attended[i], "expert")
+        if i == 0:
+            routes_all = attended[i][:, rows:]
+            attended[i] = attended[i][:, :rows]
+        elif i == 1:
+            attended[i] = tie(attended[i], *grad_near[1:])
+        mixed[i] = inputs[i] + ein("hrp,hpd->rd", attended[i], out_weight.reshape(n, part, width))
+        normed_moe[i] = rms_scale(mixed[i], moe_gain).astype(LOW)
+    attended_cols = jnp.stack([x.reshape(n, rows, m, piece) for x in attended])
+    attended_cols = swap(attended_cols.transpose(3, 0, 2, 1, 4), "shard")
+    attended_cols = attended_cols.reshape(m * micro * rows, n * piece)
 
     own_experts = own * local_count + jnp.arange(local_count, dtype=jnp.int32)
-    by_micro = jnp.swapaxes(routes_all, 0, 1)
-    hit = jnp.any(by_micro[None] == own_experts[:, None, None, None, None], axis=-1)
+    by_micro = routes_all.reshape(n, micro, top_count, rows).swapaxes(0, 1).astype(jnp.int32)
+    hit = jnp.any(by_micro[None] == own_experts[:, None, None, None, None], axis=3)
     hot = hit.astype(jnp.int32)
     slot = jnp.cumsum(hot, axis=-1) - hot
     slot_iota = jnp.arange(capacity, dtype=jnp.int32)
     pick = (hit[:, :, :, None, :] & (slot[:, :, :, None, :] == slot_iota[:, None])).astype(LOW)
     turned = (hit[..., None] & (slot[..., None] == slot_iota)).astype(LOW)
 
-    gains = head_gains.reshape(2, HEAD)
-    spots = [places(permutation[i, 0], lengths[i, 0]) for i in each]
-    turns = [angles(pos) for _, pos in spots]
-    near = [gather_first(x, "expert") for x in normed_attn]
-    normed_blocks = [gather_second(x, "expert") for x in near]
-    grad_near = [gather_first(tie(cotangent[i], near[-1][-2]), "expert") for i in each]
-    attended, normed_all, qkv_raw, qkv_low, mixed, normed_moe = ([None] * micro for _ in range(6))
+    weights = (full_gate, full_up, full_down)
+    moe_near, moe_far = ([None] * micro for _ in range(2))
     for i in each:
-        attended[i], normed_all[i], qkv_raw[i], qkv_low[i] = attend(
-            own, normed_blocks[i], qkv_weight, gains, *turns[i], spots[i][0]
-        )
-        attended[i] = swap(attended[i], "expert")
-        mixed[i] = inputs[i] + ein("hrp,hpd->rd", attended[i], out_weight.reshape(n, part, width))
-        normed_moe[i] = rms_scale(mixed[i], moe_gain).astype(LOW)
-
-    moe_sum, d_sum, d_gate = ([None] * micro for _ in range(3))
-    kept = None
+        ready = tie(normed_moe[i], grad_far, *moe_near[i - 1][1:]) if i else normed_moe[i]
+        moe_near[i] = gather_first(ready, "expert")[::2]
+    moe_far[0] = jnp.stack([hop(x, "expert", 1) for x in moe_near[0]])
+    grads = [(*grad_near, grad_far)] + [(x,) for x in grad_rest]
+    kept, wait = None, (attended_cols, *moe_near[-1][1:])
+    keep, received = ([None] * micro for _ in range(2))
     for i in each:
-        grad_blocks = gather_second(grad_near[i], "expert")
-        moe_blocks = gather_blocks(normed_moe[i], "expert")
-        moe_sum[i], d_sum[i], kept, d_gate[i] = expert_layer(
+        if i:
+            moe_far[i] = hop(jnp.stack(moe_near[i]), "expert", 1)
+        kept, keep[i], send = expert_layer(
             own,
-            moe_blocks,
-            grad_blocks,
+            [tie(moe_near[i][0], *wait)] + moe_near[i][1:],
+            moe_far[i],
+            grads[i],
             pick,
             turned,
             router_weight.T,
-            full_gate,
-            full_up,
-            full_down,
+            weights,
             i,
             micro,
             kept,
         )
-    buffer, d_result, hidden, dg, du = kept
+        received[i] = hop(send, "expert", 1)
+        wait = ()
+    buffer, d_result, hidden, dg, du, moe_sum = kept
+    def grad_rows(term):
+        return lax.psum_scatter(term, "shard", scatter_dimension=1, tiled=True)
+
     gate_term = ein("erd,erf->edf", buffer, dg).astype(LOW)
-    up_term = ein("erd,erf->edf", buffer, du).astype(LOW)
-    down_term = ein("erf,erd->efd", hidden, d_result).astype(LOW)
-    gate_grad, up_grad, down_grad = (
-        lax.psum_scatter(term, "shard", scatter_dimension=1, tiled=True).astype(F32)
-        for term in (gate_term, up_term, down_term)
-    )
-
-    output, input_grad, d_attn, d_qkv = ([None] * micro for _ in range(4))
-    router_term, moe_gain_term, head_term, attn_gain_term = 0.0, 0.0, 0.0, 0.0
+    up_term = ein("erd,erf->edf", buffer, tie(du, gate_term)).astype(LOW)
+    half, far = [None] * micro, [None] * micro
+
+    d_attn, d_attended, d_mixed, d_qkv, d_qkv_sent = ([None] * micro for _ in range(5))
+    head_terms = [None] * micro
+    router_term, moe_gain_term = 0.0, 0.0
     for i in each:
-        d_gates = swap(d_gate[i].transpose(1, 0, 2), "expert")
-        d_router = d_gates.reshape(expert_count, rows).T
-        d_normed = scatter_blocks(d_sum[i], "expert")
+        half[i] = near_sums(
+            keep[i], tie(received[i], *(d_attended[i - 1], up_term) if i else (buffer,))
+        )
+        far[i] = far_sends(half[i], ())
+        if i:
+            gate_grad = lax.psum_scatter(
+                tie(gate_term, half[i][0]), "shard", scatter_dimension=1, tiled=True
+            )
+        total = far_sum(half[i], far[i])
+        if i == 0:
+            total = tie(total, gate_term)
+        if i:
+            down_term = ein("erf,erd->efd", tie(hidden, half[i][0]), d_result).astype(LOW)
+            total = tie(total, d_qkv[i - 1], down_term)
+        d_normed = total[:rows]
+        lines = expert_count * rows // width
+        d_router = total[rows : rows + lines] + total[rows + lines : rows + 2 * lines]
+        d_router = d_router.reshape(expert_count, rows).T
         grad_out = cotangent[i].astype(F32)
         logits = dot(normed_moe[i], router_weight)
         exp_logits = jnp.exp(logits - jnp.max(logits, axis=-1, keepdims=True))
@@ -568,52 +644,79 @@
         _, norm_pull = jax.vjp(rms_scale, mixed[i], moe_gain)
         d_mixed_norm, term = norm_pull(d_normed)
         moe_gain_term = moe_gain_term + term
-        d_mixed = grad_out + d_mixed_norm
-        d_attn[i] = d_mixed.astype(LOW)
-        d_attended = dot(d_attn[i], out_weight.T).astype(LOW)
-        d_attended = swap(jnp.swapaxes(d_attended.reshape(rows, n, part), 0, 1), "expert")
-        d_qkv[i], terms = attend_back(
-            d_attended, qkv_low[i], qkv_raw[i], gains, *turns[i], spots[i][0]
+        d_mixed[i] = grad_out + d_mixed_norm
+        d_attn[i] = d_mixed[i].astype(LOW)
+        back = dot(d_attn[i], out_weight.T).astype(LOW)
+        back = jnp.swapaxes(back.reshape(rows, n, part), 0, 1)
+        d_attended[i] = swap(tie(back, d_qkv_sent[i - 1]) if i else back, "expert")
+        d_qkv[i], head_terms[i] = attend_back(
+            d_attended[i], qkv_low[i], qkv_raw[i], gains, *turns[i], spots[i][0]
         )
-        head_term = head_term + terms.reshape(2 * HEAD)
-        d_qkv_rows = swap(d_qkv[i], "expert").reshape(n, rows, 3, part).transpose(1, 2, 0, 3)
-        d_normed_attn = dot(d_qkv_rows.reshape(rows, 3 * width), qkv_weight.T)
-        _, attn_pull = jax.vjp(rms_scale, inputs[i], attn_gain)
-        d_inputs_norm, term = attn_pull(d_normed_attn)
-        attn_gain_term = attn_gain_term + term
-        input_grad[i] = (d_mixed + d_inputs_norm).astype(LOW)
-        moe_part = scatter_blocks([tie(x, d_normed) for x in moe_sum[i]], "expert")
-        output[i] = (mixed[i] + moe_part).astype(LOW)
-
-    attended_cols = jnp.stack([x.reshape(n, rows, m, piece) for x in attended])
-    attended_cols = swap(attended_cols.transpose(3, 0, 2, 1, 4), "shard")
-    attended_cols = attended_cols.reshape(m * micro * rows, n * piece)
+        d_qkv_sent[i] = swap(d_qkv[i], "expert")
+
+    moe_part = lax.psum_scatter(
+        tie(moe_sum, d_attended[-1]).reshape(n * micro * rows, width),
+        "expert",
+        scatter_dimension=0,
+        tiled=True,
+    ).reshape(micro, rows, width)
+
+    up_grad = scatter_blocks(take_blocks(tie(up_term, d_qkv[-1]), own_shard, m, 1), "shard")
+
+    down_grad = scatter_blocks(
+        take_blocks(tie(down_term, d_qkv[-1]), own_shard, m, 1), "shard"
+    )
+
     d_attn_all = place_blocks(
-        gather_blocks(jnp.concatenate(d_attn, axis=0), "shard"), own_shard, 0
+        gather_blocks(tie(jnp.concatenate(d_attn, axis=0), d_qkv[-1]), "shard"), own_shard, 0
     )
-    out_term = dot(attended_cols.T, d_attn_all).astype(LOW).reshape(n, piece, width)
-    out_grad = scatter_blocks(
-        [x[0] for x in take_blocks(out_term, own, n, 0)], "expert"
-    )
+    out_term = dot(tie(attended_cols, d_qkv[-1]).T, d_attn_all)
+    out_term = out_term.astype(LOW)
+    parts = take_blocks(out_term, own, n, 0)
+    out_near = hop(jnp.stack(parts[1::2]), "expert", 1)
+    out_half = near_sums(parts[::2], out_near)
+    out_grad = far_sum(out_half, far_sends(out_half, ()))
+    head_term = sum(head_terms).reshape(2 * HEAD)
+
+    def input_gradient(i, *wait):
+        sent = d_qkv_sent[i].reshape(n, rows, 3, part).transpose(1, 2, 0, 3)
+        d_normed_attn = dot(tie(sent.reshape(rows, 3 * width), *wait), qkv_weight.T)
+        _, pull = jax.vjp(lambda x: rms_scale(x, attn_gain), inputs[i])
+        return (d_mixed[i] + pull(d_normed_attn)[0]).astype(LOW)
 
     qkv_term = sum(
         dot(normed_all[i].reshape(n * rows, width).T, d_qkv[i].reshape(n * rows, 3 * part))
-        for i in each
+        for i in reversed(each)
     ).astype(LOW)
     qkv_term = jnp.swapaxes(qkv_term.reshape(n, m, piece, 3 * part), 0, 1)
-    qkv_sum = scatter_blocks(take_blocks(qkv_term, own_shard, m, 0), "shard").astype(LOW)
+    parts = take_blocks(qkv_term, own_shard, m, 0)
+    qkv_half = [
+        (parts[k].astype(F32) + hop(parts[k + 1], "shard", 1).astype(F32)).astype(LOW)
+        for k in range(0, m, 2)
+    ]
+    qkv_far = [hop(qkv_half[j], "shard", 2 * j) for j in range(1, m // 2)]
+    gate_grad, up_grad, down_grad = (x.astype(F32) for x in (gate_grad, up_grad, down_grad))
+    input_grad = [input_gradient(i, qkv_half[0]) for i in range(micro - 1)]
+    qkv_sum = far_sum(qkv_half, qkv_far).astype(LOW)
+    qkv_sum = tie(qkv_sum, d_qkv_sent[-1], *input_grad)
     qkv_rows = swap(qkv_sum.reshape(n, piece, 3 * part), "expert")
     qkv_grad = (
         qkv_rows.reshape(n, piece, 3, part).transpose(1, 2, 0, 3).reshape(piece, 3 * width)
     ).astype(F32)
+    input_grad.append(input_gradient(micro - 1, qkv_sum))
+    output = [(mixed[i] + moe_part[i].astype(F32)).astype(LOW) for i in each]
     output, input_grad = jnp.stack(output), jnp.stack(input_grad)
+
+    first = (own * m + own_shard) * piece
+    own_rows = lax.dynamic_slice_in_dim(qkv_weight, first, piece, 0).astype(F32)
+    own_gain = lax.dynamic_slice_in_dim(attn_gain, first, piece, 0)
+    attn_gain_grad = jnp.sum(qkv_grad * own_rows, axis=1) / own_gain
 
     world = n * m
     head_piece = 2 * HEAD // world
     small = jnp.concatenate(
         [
             router_term.reshape(world, piece * expert_count),
-            attn_gain_term.reshape(world, piece),
             moe_gain_term.reshape(world, piece),
             head_term.reshape(world, head_piece),
         ],
@@ -622,6 +725,7 @@
     used = small.shape[1]
     padded = -(-used // 1024) * 1024
     small = jnp.pad(small, ((0, 0), (0, padded - used))).reshape(world, padded // 128, 128)
+    small = tie(small, d_qkv_sent[-1])
     small = jnp.sum(swap(small, ("expert", "shard")), axis=0).reshape(padded)
     a = piece * expert_count
     return (
@@ -630,9 +734,9 @@
         qkv_grad,
         out_grad,
         small[:a].reshape(piece, expert_count),
+        attn_gain_grad,
         small[a : a + piece],
-        small[a + piece : a + 2 * piece],
-        small[a + 2 * piece : a + 2 * piece + head_piece],
+        small[a + piece : a + piece + head_piece],
         gate_grad,
         up_grad,
         down_grad,

time: 975 us -> 928 us (0.952)
  starting transfers between devices: 168 us -> 105 us
  waiting for transfers between devices: 362 us -> 330 us
  blocking collectives: 0 us -> 17.7 us
  local copies, waits for them, and re-layouts: 52.4 us -> 66.2 us
    ppermute x83 -> x53, starting transfers between devices: 104 us -> 63.3 us  [hop(): return lax.ppermute(value, axis, [(i, i ^ step) for i in range(size)])]
    all_to_all x12 -> x8, starting transfers between devices: 63.6 us -> 41.5 us  [swap(): return lax.all_to_all(value, axis, split_axis=0, concat_axis=0, tiled=True)]
    all_to_all x0 -> x1, blocking collectives: none -> 17.7 us  [swap(): return lax.all_to_all(value, axis, split_axis=0, concat_axis=0, tiled=True)]
    add x3 -> x8, other arithmetic: 1.91 us -> 19.2 us  [the longest x5 19.2 us: far_sum(): return half[0].astype(F32) + sum((x.astype(F32) for x in received))]
    ppermute x83 -> x53, waiting for transfers between devices: 341 us -> 324 us  [hop(): return lax.ppermute(value, axis, [(i, i ^ step) for i in range(size)])]
    convert_element_type x18 -> x12, other arithmetic: 42.2 us -> 26.8 us  [the longest x2 8.94 us: scatter_blocks(): (blocks[k].astype(F32) + hop(blocks[k + 1], axis, 1).astype(F32)).astype(...]
    all_to_all x12 -> x8, waiting for transfers between devices: 18.7 us -> 4.54 us  [swap(): return lax.all_to_all(value, axis, split_axis=0, concat_axis=0, tiled=True)]
    another operation x2 -> x6, other arithmetic: 0.35 us -> 10.4 us  [the longest x1 3.15 us: local(): moe_far[0] = jnp.stack([hop(x, 'expert', 1) for x in moe_near[0]])]
  transfers between devices with their start and end apart: 101 -> 67, of which waited for: 44 -> 24; matrix products, arithmetic and copies ran while one was open for 24% -> 27% of each run, Pallas kernels for 12% -> 19%
where the time goes in v3:
time: 928 us; the launch traced here: 911 us
  waiting for transfers between devices  330 us (36%)
  Pallas kernels  175 us (19%)
  matrix products  117 us (13%)
  starting transfers between devices  105 us (11%)
  other arithmetic  82.9 us (9%)
  local copies, waits for them, and re-layouts  66.2 us (7%)
  blocking collectives  17.7 us (2%)
  between operations  15.4 us (2%)
    ppermute x53, waiting for transfers between devices, hop(): return lax.ppermute(value, axis, [(i, i ^ step) for i in range(size)])  324 us
    pallas_call x2, Pallas kernels, expert_layer(): pl.pallas_call(functools.partial(expert_kernel, n, 512, grads_near, len(k...  120 us
    ppermute x53, starting transfers between devices, hop(): return lax.ppermute(value, axis, [(i, i ^ step) for i in range(size)])  63.3 us
    dot_general x5, matrix products, ein(): return jnp.einsum(spec, a, b, preferred_element_type=F32)  59.9 us
    dot_general x13, matrix products, dot(): return jnp.dot(a, b, preferred_element_type=F32)  57.6 us
    all_to_all x8, starting transfers between devices, swap(): return lax.all_to_all(value, axis, split_axis=0, concat_axis=0, tiled=True)  41.5 us
    pallas_call x2, Pallas kernels, attend_back(): pl.pallas_call(functools.partial(attend_back_kernel, n, tile), out_shape=...  28.4 us
    pallas_call x2, Pallas kernels, attend(): pl.pallas_call(functools.partial(attend_kernel, n, tile), out_shape=[jax....  26.8 us
  transfers between devices with their start and end apart: 67, of which 24 were waited for; matrix products, arithmetic and copies ran while one was open for 27% of the time, Pallas kernels for 19%

profile of v3, /device:TPU:8, one launch (start us, length us, event | category | flops | bytes accessed | tf_op | source)
XLA Modules:
  0.0 910.6 jit_solution(8566541333285170707)
XLA Ops:
  10.8 3.0 collective-permute-start.3
  16.5 5.4 fusion.38
  21.8 10.8 %collective-permute-done.1.refs_2_ = bf16[128,2048]{1,0:T(8,128)(2,1)} collective-permute-done((bf16[128,2048]{1,0:T(8,128)(2,1)S(1)}, bf16[128,2048]{1,0:T(8,128)(2,1)}, u32[]{:S(2)}, u32[]{:S(2)}) %collective-permute-start.1) | collective-permute-done | bytes 524320 | tf_op jit(solution)/shard_map/ppermute | solution.py:44
  36.5 23.4 %collective-permute-done.3.refs_4_ = bf16[128,2048]{1,0:T(8,128)(2,1)} collective-permute-done((bf16[128,2048]{1,0:T(8,128)(2,1)S(1)}, bf16[128,2048]{1,0:T(8,128)(2,1)}, u32[]{:S(2)}, u32[]{:S(2)}) %collective-permute-start.3) | collective-permute-done | bytes 524320 | tf_op jit(solution)/shard_map/ppermute | solution.py:44
  61.4 10.7 %collective-permute-done.5.refs_6_ = bf16[128,2048]{1,0:T(8,128)(2,1)} collective-permute-done((bf16[128,2048]{1,0:T(8,128)(2,1)S(1)}, bf16[128,2048]{1,0:T(8,128)(2,1)}, u32[]{:S(2)}, u32[]{:S(2)}) %collective-permute-start.5) | collective-permute-done | bytes 524320 | tf_op jit(solution)/shard_map/ppermute | solution.py:44
  81.1 11.2 %collective-permute-done.12.refs_6_ = bf16[128,2048]{1,0:T(8,128)(2,1)} collective-permute-done((bf16[128,2048]{1,0:T(8,128)(2,1)S(1)}, bf16[128,2048]{1,0:T(8,128)(2,1)}, u32[]{:S(2)}, u32[]{:S(2)}) %collective-permute-start.12) | collective-permute-done | bytes 524320 | tf_op jit(solution)/shard_map/ppermute | solution.py:44
  96.0 12.8 %attend.2 = (bf16[8,136,256]{2,1,0:T(8,128)(2,1)}, bf16[8,128,2048]{2,1,0:T(8,128)(2,1)}, f32[1024,512]{1,0:T(8,128)}, bf16[1024,768]{1,0:T(8,128)(2,1)}) custom-call(s32[1]{0:T(128)} %bitcast.1.own_ref, bf16[128,2048]{1,0:T(8,128)(2,1)} %copy-done.26, bf16[128,2048]{1,0:T(8,128)(2,1)} %collective-permute-done.refs_1_, ...), custom_call_target="tpu_custom_call" | custom-call | flops 4294967296 | bytes 16252928 | tf_op jit(solution)/shard_map/attend/pallas_call | solution.py:367
  108.7 7.2 all-to-all-start
  119.9 12.1 %collective-permute-start.9 = (bf16[128,2048]{1,0:T(8,128)(2,1)}, bf16[128,2048]{1,0:T(8,128)(2,1)}, u32[]{:S(2)}, u32[]{:S(2)}) collective-permute-start(bf16[128,2048]{1,0:T(8,128)(2,1)} %collective-permute-done.8.refs_2_), channel_id=1, source_target_pairs={{0,4},{4,0},{8,12},{12,8},{16,20},{20,16},{24,28},{28,24},{1,5},{5... | collective-permute-start | bytes 1572872 | tf_op jit(solution)/shard_map/ppermute | solution.py:44
  140.2 14.0 %attend.3 = (bf16[8,128,256]{2,1,0:T(8,128)(2,1)}, bf16[8,128,2048]{2,1,0:T(8,128)(2,1)}, f32[1024,512]{1,0:T(8,128)}, bf16[1024,768]{1,0:T(8,128)(2,1)}) custom-call(s32[1]{0:T(128)} %bitcast.1.own_ref, bf16[128,2048]{1,0:T(8,128)(2,1)} %copy-done.25, bf16[128,2048]{1,0:T(8,128)(2,1)} %collective-permute-done.7.refs_1_, ...), custom_call_target="tpu_custom_call" | custom-call | flops 4294967296 | bytes 16252928 | tf_op jit(solution)/shard_map/attend/pallas_call | solution.py:367
  154.2 6.4 all-to-all-start.1
  160.7 9.5 %collective-permute-done.16.refs_8_ = bf16[128,2048]{1,0:T(8,128)(2,1)} collective-permute-done((bf16[128,2048]{1,0:T(8,128)(2,1)}, bf16[128,2048]{1,0:T(8,128)(2,1)}, u32[]{:S(2)}, u32[]{:S(2)}) %collective-permute-start.16) | collective-permute-done | bytes 524320 | tf_op jit(solution)/shard_map/ppermute | solution.py:44
  175.4 4.9 multiply_reduce_fusion.5
  180.3 4.9 multiply_reduce_fusion.6
  192.2 5.8 collective-permute-done.18.refs_1_
  200.3 3.6 all-to-all-start.2
  206.4 23.0 %collective-permute-done.19.refs_2_ = bf16[128,2048]{1,0:T(8,128)(2,1)} collective-permute-done((bf16[128,2048]{1,0:T(8,128)(2,1)S(1)}, bf16[128,2048]{1,0:T(8,128)(2,1)}, u32[]{:S(2)}, u32[]{:S(2)}) %collective-permute-start.19) | collective-permute-done | bytes 524320 | tf_op jit(solution)/shard_map/ppermute | solution.py:44
  229.4 40.4 %collective-permute-done.20.refs_3_ = bf16[128,2048]{1,0:T(8,128)(2,1)} collective-permute-done((bf16[128,2048]{1,0:T(8,128)(2,1)S(1)}, bf16[128,2048]{1,0:T(8,128)(2,1)}, u32[]{:S(2)}, u32[]{:S(2)}) %collective-permute-start.20) | collective-permute-done | bytes 524320 | tf_op jit(solution)/shard_map/ppermute | solution.py:44
  270.8 4.4 collective-permute-start.22
  280.2 3.1 pad_maximum_fusion.2.refs_4_
  283.3 8.0 collective-permute-done.21.refs_1_
  291.3 17.2 %collective-permute-done.22.refs_2_ = bf16[128,2048]{1,0:T(8,128)(2,1)} collective-permute-done((bf16[128,2048]{1,0:T(8,128)(2,1)S(1)}, bf16[128,2048]{1,0:T(8,128)(2,1)}, u32[]{:S(2)}, u32[]{:S(2)}) %collective-permute-start.22) | collective-permute-done | bytes 524320 | tf_op jit(solution)/shard_map/ppermute | solution.py:44
  308.5 6.7 collective-permute-done.23.refs_3_
  315.2 3.0 pad_maximum_fusion.1
  318.3 65.2 %experts.2 = (bf16[2,1024,2048]{2,1,0:T(8,128)(2,1)}, bf16[2,1024,2048]{2,1,0:T(8,128)(2,1)}, bf16[2,1024,1024]{2,1,0:T(8,128)(2,1)}, bf16[2,1024,1024]{2,1,0:T(...) custom-call(s32[1]{0:T(128)} %bitcast.1.own_ref, ...), custom_call_target="tpu_custom_call" | custom-call | flops 51539607552 | bytes 41943040 | tf_op jit(solution)/shard_map/experts/pallas_call | solution.py:261
  386.9 54.8 %experts.3 = (bf16[2,1024,2048]{2,1,0:T(8,128)(2,1)}, bf16[2,1024,2048]{2,1,0:T(8,128)(2,1)}, bf16[2,1024,1024]{2,1,0:T(8,128)(2,1)}, bf16[2,1024,1024]{2,1,0:T(...) custom-call(s32[1]{0:T(128)} %bitcast.1.own_ref, ...), custom_call_target="tpu_custom_call", output_to_operand_aliasing={{0}: (13, {}), {1}: (14, {}), {2}: (15, {}), {3}: (16, {}),... | custom-call | flops 51539607552 | bytes 41943040 | tf_op jit(solution)/shard_map/experts/pallas_call | solution.py:261
  441.8 3.1 fusion.24
  444.8 2.9 collective-permute-start.32
  448.3 18.6 %convolution_convert_fusion.2 = bf16[2,2048,1024]{2,1,0:T(8,128)(2,1)} fusion(bf16[2,1024,2048]{2,1,0:T(8,128)(2,1)} %get-tuple-element.81, bf16[2,1024,1024]{2,1,0:T(8,128)(2,1)S(1)} %copy-done.63), kind=kOutput, calls=%fused_computation.4 | convolution fusion | flops 8594128896 | bytes 20971520 | tf_op jit(solution)/shard_map/erd,erf->edf/dot_general | solution.py:111
  467.0 14.2 %collective-permute-done.32 = bf16[136,2048]{1,0:T(8,128)(2,1)} collective-permute-done((bf16[136,2048]{1,0:T(8,128)(2,1)}, bf16[136,2048]{1,0:T(8,128)(2,1)}, u32[]{:S(2)}, u32[]{:S(2)}) %collective-permute-start.32) | collective-permute-done | bytes 557088 | tf_op jit(solution)/shard_map/ppermute | solution.py:44
  481.2 7.4 collective-permute-done.33
  493.4 6.3 convolution_convert_fusion.5
  501.0 3.9 all-to-all-start.3
  504.9 14.9 %convolution_convert_fusion.1 = bf16[2,2048,1024]{2,1,0:T(8,128)(2,1)} fusion(bf16[2,1024,2048]{2,1,0:T(8,128)(2,1)} %get-tuple-element.81, bf16[2,1024,1024]{2,1,0:T(8,128)(2,1)} %get-tuple-element.86), kind=kOutput, calls=%fused_computation.3 | convolution fusion | flops 8594128896 | bytes 20971520 | tf_op jit(solution)/shard_map/erd,erf->edf/dot_general | solution.py:111
  526.1 13.7 %collective-permute-done.34 = bf16[136,2048]{1,0:T(8,128)(2,1)S(1)} collective-permute-done((bf16[136,2048]{1,0:T(8,128)(2,1)S(1)}, bf16[136,2048]{1,0:T(8,128)(2,1)S(1)}, u32[]{:S(2)}, u32[]{:S(2)}) %collective-permute-start.34) | collective-permute-done | bytes 557088 | tf_op jit(solution)/shard_map/ppermute | solution.py:44
  539.8 20.9 %collective-permute-done.35 = bf16[136,2048]{1,0:T(8,128)(2,1)S(1)} collective-permute-done((bf16[136,2048]{1,0:T(8,128)(2,1)S(1)}, bf16[136,2048]{1,0:T(8,128)(2,1)S(1)}, u32[]{:S(2)}, u32[]{:S(2)}) %collective-permute-start.35) | collective-permute-done | bytes 557088 | tf_op jit(solution)/shard_map/ppermute | solution.py:44
  560.8 7.4 collective-permute-done.36
  572.2 14.1 %attend_back.2 = (bf16[8,128,768]{2,1,0:T(8,128)(2,1)}, f32[2,128]{1,0:T(2,128)}) custom-call(bf16[8,128,256]{2,1,0:T(8,128)(2,1)} %copy-done.35, bf16[1024,768]{1,0:T(8,128)(2,1)} %get-tuple-element.88.low_ref, f32[1024,512]{1,0:T(8,128)} %get-tuple-element.89.raw_ref, f32[2,128]{1,0:T(2,128)} %bitcast.269, f32[1024,128]{1,0:T(8,128)} %pad_maximum_fusion.7.refs_12_.cos_ref, ...), custom_call_target="tpu_custom_call" | custom-call | flops 2684354560 | bytes 5767168 | tf_op jit(solution)/shard_map/attend_back/pallas_call | solution.py:485
  586.3 4.8 all-to-all-start.4
  591.2 16.7 %convolution_convert_fusion = bf16[2,1024,2048]{2,1,0:T(8,128)(2,1)} fusion(bf16[2,1024,1024]{2,1,0:T(8,128)(2,1)} %get-tuple-element.92, bf16[2,1024,2048]{2,1,0:T(8,128)(2,1)} %get-tuple-element.93), kind=kOutput, calls=%fused_computation.2 | convolution fusion | flops 8594128896 | bytes 20971520 | tf_op jit(solution)/shard_map/erf,erd->efd/dot_general | solution.py:111
  610.6 6.3 convolution_convert_fusion.4
  617.4 2.9 all-to-all-done.4
  620.3 17.7 %all_to_all.45.d_ref = bf16[8,128,256]{2,1,0:T(8,128)(2,1)} all-to-all(bf16[8,128,256]{2,1,0:T(8,128)(2,1)S(1)} %bitcast.242), channel_id=1, replica_groups=mesh['expert'=8,'shard'=4] {'expert'}, dimensions={0} | all-to-all | bytes 1048576 | tf_op jit(solution)/shard_map/all_to_all | solution.py:103
  640.5 14.3 %attend_back.3 = (bf16[8,128,768]{2,1,0:T(8,128)(2,1)}, f32[2,128]{1,0:T(2,128)}) custom-call(bf16[8,128,256]{2,1,0:T(8,128)(2,1)} %all_to_all.45.d_ref, bf16[1024,768]{1,0:T(8,128)(2,1)} %get-tuple-element.98.low_ref, f32[1024,512]{1,0:T(8,128)} %get-tuple-element.99.raw_ref, f32[2,128]{1,0:T(2,128)} %bitcast.270, ...), custom_call_target="tpu_custom_call" | custom-call | flops 2684354560 | bytes 5767168 | tf_op jit(solution)/shard_map/attend_back/pallas_call | solution.py:485
  654.9 5.7 fusion.56
  660.6 4.0 fusion
  672.2 5.1 all-to-all-start.6
  678.8 4.8 constant_dynamic-slice_fusion
  684.3 5.0 constant_dynamic-slice_fusion.2
  698.0 5.5 collective-permute-done.41
  706.5 13.2 %collective-permute-done.39 = bf16[1,8,64,768]{3,2,1,0:T(8,128)(2,1)S(1)} collective-permute-done((bf16[1,8,64,768]{3,2,1,0:T(8,128)(2,1)S(1)}, bf16[1,8,64,768]{3,2,1,0:T(8,128)(2,1)S(1)}, u32[]{:S(2)}, u32[]{:S(2)}) %collective-permute-start.39) | collective-permute-done | bytes 786464 | tf_op jit(solution)/shard_map/ppermute | solution.py:44
  722.0 14.4 %fusion.16 = (f32[128]{0:T(128)S(1)}, f32[128,2048]{1,0:T(8,128)}) fusion(bf16[2,128,2048]{2,1,0:T(8,128)(2,1)S(1)} %copy-done.1, f32[2048]{0:T(1024)S(1)} %copy-done.40, bf16[128,6144]{0,1:T(8,128)(2,1)} %bitcast.227, bf16[2048,6144]{1,0:T(8,128)(2,1)} %refs_10_.3), kind=kOutput, calls=%fused_computation.66 | convolution fusion | flops 3222274048 | bytes 28320256 | tf_op jit(solution)/shard_map/dot_general | solution.py:107
  738.8 4.6 convolution_convert_fusion.3
  747.9 4.4 add_convert_fusion
  753.7 4.9 all-to-all-start.8
  758.6 28.1 %collective-permute-done.43 = bf16[4,64,2048]{2,1,0:T(8,128)(2,1)} collective-permute-done((bf16[4,64,2048]{2,1,0:T(8,128)(2,1)}, bf16[4,64,2048]{2,1,0:T(8,128)(2,1)}, u32[]{:S(2)}, u32[]{:S(2)}) %collective-permute-start.43) | collective-permute-done | bytes 1048608 | tf_op jit(solution)/shard_map/ppermute | solution.py:44
  791.8 4.5 add_convert_fusion.2
  804.5 5.5 all-to-all-start.7
  811.5 14.4 %fusion.20 = (f32[128]{0:T(128)S(1)}, f32[128,2048]{1,0:T(8,128)}) fusion(bf16[2,128,2048]{2,1,0:T(8,128)(2,1)S(1)} %copy-done.1, f32[2048]{0:T(1024)S(1)} %copy-done.40, bf16[128,6144]{0,1:T(8,128)(2,1)} %bitcast.228, bf16[2048,6144]{1,0:T(8,128)(2,1)} %refs_10_.3), kind=kOutput, calls=%fused_computation.70 | convolution fusion | flops 3222274048 | bytes 28320256 | tf_op jit(solution)/shard_map/dot_general | solution.py:107
  827.9 42.4 %collective-permute-done.46 = bf16[64,2048]{1,0:T(8,128)(2,1)} collective-permute-done((bf16[64,2048]{1,0:T(8,128)(2,1)}, bf16[64,2048]{1,0:T(8,128)(2,1)}, u32[]{:S(2)}, u32[]{:S(2)}) %collective-permute-start.46) | collective-permute-done | bytes 262176 | tf_op jit(solution)/shard_map/ppermute | solution.py:44
  872.5 3.5 reshape.395
  882.2 6.3 convert_add_fusion.1
  888.5 6.1 convert_add_fusion
  894.6 4.1 convert_element_type.554
  (345 shorter events, 147.0 us)
Async XLA Ops:
  7.2 311.1 %all-gather.10.cloned.1.call-start = ((), (), s32[]{:S(2)}) async-start(), calls=%async_computation.13 | async-start | bytes 10485760 | tf_op jit(solution)/shard_map/all_gather | solution.py:532
  7.9 310.3 %all-gather.6.cloned.1.call-start = ((), (), s32[]{:S(2)}) async-start(), calls=%async_computation.11 | async-start | bytes 10485760 | tf_op jit(solution)/shard_map/all_gather | solution.py:530
  8.7 309.6 %all-gather.8.cloned.1.call-start = ((), (), s32[]{:S(2)}) async-start(), calls=%async_computation.12 | async-start | bytes 10485760 | tf_op jit(solution)/shard_map/all_gather | solution.py:531
  10.7 22.0 %collective-permute-start.1 = (bf16[128,2048]{1,0:T(8,128)(2,1)S(1)}, bf16[128,2048]{1,0:T(8,128)(2,1)}, u32[]{:S(2)}, u32[]{:S(2)}) collective-permute-start(bf16[128,2048]{1,0:T(8,128)(2,1)S(1)} %get-tuple-element.186.refs_0_), channel_id=1, source_target_pairs={{0,8},{4,12},{8,0},{12,4},{16,24},{20,28},{24,16},{28,20},{1,9},{5... | collective-permute-start | bytes 1572872 | tf_op jit(solution)/shard_map/ppermute | solution.py:44
  10.8 49.1 %collective-permute-start.3 = (bf16[128,2048]{1,0:T(8,128)(2,1)S(1)}, bf16[128,2048]{1,0:T(8,128)(2,1)}, u32[]{:S(2)}, u32[]{:S(2)}) collective-permute-start(bf16[128,2048]{1,0:T(8,128)(2,1)S(1)} %get-tuple-element.186.refs_0_), channel_id=1, source_target_pairs={{0,16},{4,20},{8,24},{12,28},{16,0},{20,4},{24,8},{28,12},{1,17},{... | collective-permute-start | bytes 1572872 | tf_op jit(solution)/shard_map/ppermute | solution.py:44
  13.8 58.3 %collective-permute-start.5 = (bf16[128,2048]{1,0:T(8,128)(2,1)S(1)}, bf16[128,2048]{1,0:T(8,128)(2,1)}, u32[]{:S(2)}, u32[]{:S(2)}) collective-permute-start(bf16[128,2048]{1,0:T(8,128)(2,1)S(1)} %get-tuple-element.186.refs_0_), channel_id=1, source_target_pairs={{0,24},{4,28},{8,16},{12,20},{16,8},{20,12},{24,0},{28,4},{1,25},{... | collective-permute-start | bytes 1572872 | tf_op jit(solution)/shard_map/ppermute | solution.py:44
  14.2 66.8 %collective-permute-start = (bf16[128,2048]{1,0:T(8,128)(2,1)S(1)}, bf16[128,2048]{1,0:T(8,128)(2,1)}, u32[]{:S(2)}, u32[]{:S(2)}) collective-permute-start(bf16[128,2048]{1,0:T(8,128)(2,1)S(1)} %get-tuple-element.186.refs_0_), channel_id=1, source_target_pairs={{0,4},{4,0},{8,12},{12,8},{16,20},{20,16},{24,28},{28,24},{1,5},{5... | collective-permute-start | bytes 1572872 | tf_op jit(solution)/shard_map/ppermute | solution.py:44
  32.7 59.6 %collective-permute-start.12 = (bf16[128,2048]{1,0:T(8,128)(2,1)S(1)}, bf16[128,2048]{1,0:T(8,128)(2,1)}, u32[]{:S(2)}, u32[]{:S(2)}) collective-permute-start(bf16[128,2048]{1,0:T(8,128)(2,1)S(1)} %get-tuple-element.63.refs_0_), channel_id=1, source_target_pairs={{0,24},{4,28},{8,16},{12,20},{16,8},{20,12},{24,0},{28,4},{1,25},{... | collective-permute-start | bytes 1572872 | tf_op jit(solution)/shard_map/ppermute | solution.py:44
  35.0 58.2 %collective-permute-start.2 = (bf16[128,2048]{1,0:T(8,128)(2,1)}, bf16[128,2048]{1,0:T(8,128)(2,1)}, u32[]{:S(2)}, u32[]{:S(2)}) collective-permute-start(bf16[128,2048]{1,0:T(8,128)(2,1)} %collective-permute-done.1.refs_2_), channel_id=1, source_target_pairs={{0,4},{4,0},{8,12},{12,8},{16,20},{20,16},{24,28},{28,24},{1,5},{5... | collective-permute-start | bytes 1572872 | tf_op jit(solution)/shard_map/ppermute | solution.py:44
  59.8 36.0 %collective-permute-start.4 = (bf16[128,2048]{1,0:T(8,128)(2,1)}, bf16[128,2048]{1,0:T(8,128)(2,1)}, u32[]{:S(2)}, u32[]{:S(2)}) collective-permute-start(bf16[128,2048]{1,0:T(8,128)(2,1)} %collective-permute-done.3.refs_4_), channel_id=1, source_target_pairs={{0,4},{4,0},{8,12},{12,8},{16,20},{20,16},{24,28},{28,24},{1,5},{5... | collective-permute-start | bytes 1572872 | tf_op jit(solution)/shard_map/ppermute | solution.py:44
  72.1 23.9 %collective-permute-start.6 = (bf16[128,2048]{1,0:T(8,128)(2,1)}, bf16[128,2048]{1,0:T(8,128)(2,1)}, u32[]{:S(2)}, u32[]{:S(2)}) collective-permute-start(bf16[128,2048]{1,0:T(8,128)(2,1)} %collective-permute-done.5.refs_6_), channel_id=1, source_target_pairs={{0,4},{4,0},{8,12},{12,8},{16,20},{20,16},{24,28},{28,24},{1,5},{5... | collective-permute-start | bytes 1572872 | tf_op jit(solution)/shard_map/ppermute | solution.py:44
  81.0 35.2 %collective-permute-start.10 = (bf16[128,2048]{1,0:T(8,128)(2,1)S(1)}, bf16[128,2048]{1,0:T(8,128)(2,1)}, u32[]{:S(2)}, u32[]{:S(2)}) collective-permute-start(bf16[128,2048]{1,0:T(8,128)(2,1)S(1)} %get-tuple-element.63.refs_0_), channel_id=1, source_target_pairs={{0,16},{4,20},{8,24},{12,28},{16,0},{20,4},{24,8},{28,12},{1,17},{... | collective-permute-start | bytes 1572872 | tf_op jit(solution)/shard_map/ppermute | solution.py:44
  92.2 27.7 %collective-permute-start.8 = (bf16[128,2048]{1,0:T(8,128)(2,1)S(1)}, bf16[128,2048]{1,0:T(8,128)(2,1)}, u32[]{:S(2)}, u32[]{:S(2)}) collective-permute-start(bf16[128,2048]{1,0:T(8,128)(2,1)S(1)} %get-tuple-element.63.refs_0_), channel_id=1, source_target_pairs={{0,8},{4,12},{8,0},{12,4},{16,24},{20,28},{24,16},{28,20},{1,9},{5... | collective-permute-start | bytes 1572872 | tf_op jit(solution)/shard_map/ppermute | solution.py:44
  93.2 42.6 %collective-permute-start.7 = (bf16[128,2048]{1,0:T(8,128)(2,1)S(1)}, bf16[128,2048]{1,0:T(8,128)(2,1)}, u32[]{:S(2)}, u32[]{:S(2)}) collective-permute-start(bf16[128,2048]{1,0:T(8,128)(2,1)S(1)} %get-tuple-element.63.refs_0_), channel_id=1, source_target_pairs={{0,4},{4,0},{8,12},{12,8},{16,20},{20,16},{24,28},{28,24},{1,5},{5... | collective-permute-start | bytes 1572872 | tf_op jit(solution)/shard_map/ppermute | solution.py:44
  95.9 40.2 %collective-permute-start.13 = (bf16[128,2048]{1,0:T(8,128)(2,1)}, bf16[128,2048]{1,0:T(8,128)(2,1)}, u32[]{:S(2)}, u32[]{:S(2)}) collective-permute-start(bf16[128,2048]{1,0:T(8,128)(2,1)} %collective-permute-done.12.refs_6_), channel_id=1, source_target_pairs={{0,4},{4,0},{8,12},{12,8},{16,20},{20,16},{24,28},{28,24},{1,5},{5... | collective-permute-start | bytes 1572872 | tf_op jit(solution)/shard_map/ppermute | solution.py:44
  108.7 45.5 %all-to-all-start = ((bf16[8,136,256]{2,1,0:T(8,128)(2,1)}), bf16[8,136,256]{2,1,0:T(8,128)(2,1)S(1)}, u32[]{:S(2)}, u32[]{:S(2)}) async-start(bf16[8,136,256]{2,1,0:T(8,128)(2,1)} %get-tuple-element.62), calls=%async_computation | async-start | bytes 1114112 | tf_op jit(solution)/shard_map/all_to_all | solution.py:103
  115.9 269.6 %all-gather.12.cloned.1.call-start = ((), (), s32[]{:S(2)}) async-start(), calls=%async_computation.16 | async-start | bytes 4718592 | tf_op jit(solution)/shard_map/all_gather | solution.py:547
  116.2 22.1 %collective-permute-start.11 = (bf16[128,2048]{1,0:T(8,128)(2,1)}, bf16[128,2048]{1,0:T(8,128)(2,1)}, u32[]{:S(2)}, u32[]{:S(2)}) collective-permute-start(bf16[128,2048]{1,0:T(8,128)(2,1)} %collective-permute-done.10.refs_4_), channel_id=1, source_target_pairs={{0,4},{4,0},{8,12},{12,8},{16,20},{20,16},{24,28},{28,24},{1,5},{5... | collective-permute-start | bytes 1572872 | tf_op jit(solution)/shard_map/ppermute | solution.py:44
  119.9 20.3 %collective-permute-start.9 = (bf16[128,2048]{1,0:T(8,128)(2,1)}, bf16[128,2048]{1,0:T(8,128)(2,1)}, u32[]{:S(2)}, u32[]{:S(2)}) collective-permute-start(bf16[128,2048]{1,0:T(8,128)(2,1)} %collective-permute-done.8.refs_2_), channel_id=1, source_target_pairs={{0,4},{4,0},{8,12},{12,8},{16,20},{20,16},{24,28},{28,24},{1,5},{5... | collective-permute-start | bytes 1572872 | tf_op jit(solution)/shard_map/ppermute | solution.py:44
  133.1 27.5 %collective-permute-start.14 = (bf16[128,2048]{1,0:T(8,128)(2,1)}, bf16[128,2048]{1,0:T(8,128)(2,1)S(1)}, u32[]{:S(2)}, u32[]{:S(2)}) collective-permute-start(bf16[128,2048]{1,0:T(8,128)(2,1)} %get-tuple-element.65.refs_5_), channel_id=1, source_target_pairs={{0,8},{4,12},{8,0},{12,4},{16,24},{20,28},{24,16},{28,20},{1,9},{5... | collective-permute-start | bytes 1572872 | tf_op jit(solution)/shard_map/ppermute | solution.py:44
  135.8 24.8 %collective-permute-start.15 = (bf16[128,2048]{1,0:T(8,128)(2,1)}, bf16[128,2048]{1,0:T(8,128)(2,1)S(1)}, u32[]{:S(2)}, u32[]{:S(2)}) collective-permute-start(bf16[128,2048]{1,0:T(8,128)(2,1)} %get-tuple-element.65.refs_5_), channel_id=1, source_target_pairs={{0,16},{4,20},{8,24},{12,28},{16,0},{20,4},{24,8},{28,12},{1,17},{... | collective-permute-start | bytes 1572872 | tf_op jit(solution)/shard_map/ppermute | solution.py:44
  136.1 34.0 %collective-permute-start.16 = (bf16[128,2048]{1,0:T(8,128)(2,1)}, bf16[128,2048]{1,0:T(8,128)(2,1)}, u32[]{:S(2)}, u32[]{:S(2)}) collective-permute-start(bf16[128,2048]{1,0:T(8,128)(2,1)} %get-tuple-element.65.refs_5_), channel_id=1, source_target_pairs={{0,24},{4,28},{8,16},{12,20},{16,8},{20,12},{24,0},{28,4},{1,25},{... | collective-permute-start | bytes 1572872 | tf_op jit(solution)/shard_map/ppermute | solution.py:44
  154.2 26.0 %all-to-all-start.1 = ((bf16[8,128,256]{2,1,0:T(8,128)(2,1)}), bf16[8,128,256]{2,1,0:T(8,128)(2,1)S(1)}, u32[]{:S(2)}, u32[]{:S(2)}) async-start(bf16[8,128,256]{2,1,0:T(8,128)(2,1)} %get-tuple-element.64), calls=%async_computation.1 | async-start | bytes 1048576 | tf_op jit(solution)/shard_map/all_to_all | solution.py:103
  173.0 97.9 %collective-permute-start.17 = (bf16[4,128,2048]{2,1,0:T(8,128)(2,1)}, bf16[4,128,2048]{2,1,0:T(8,128)(2,1)}, u32[]{:S(2)}, u32[]{:S(2)}) collective-permute-start(bf16[4,128,2048]{2,1,0:T(8,128)(2,1)} %pad_maximum_fusion), channel_id=1, source_target_pairs={{0,4},{4,0},{8,12},{12,8},{16,20},{20,16},{24,28},{28,24},{1,5},{5... | collective-permute-start | bytes 6291464 | tf_op jit(solution)/shard_map/ppermute | solution.py:44
  187.8 41.6 %collective-permute-start.19 = (bf16[128,2048]{1,0:T(8,128)(2,1)S(1)}, bf16[128,2048]{1,0:T(8,128)(2,1)}, u32[]{:S(2)}, u32[]{:S(2)}) collective-permute-start(bf16[128,2048]{1,0:T(8,128)(2,1)S(1)} %get-tuple-element.69.refs_0_), channel_id=1, source_target_pairs={{0,16},{4,20},{8,24},{12,28},{16,0},{20,4},{24,8},{28,12},{1,17},{... | collective-permute-start | bytes 1572872 | tf_op jit(solution)/shard_map/ppermute | solution.py:44
  190.7 79.1 %collective-permute-start.20 = (bf16[128,2048]{1,0:T(8,128)(2,1)S(1)}, bf16[128,2048]{1,0:T(8,128)(2,1)}, u32[]{:S(2)}, u32[]{:S(2)}) collective-permute-start(bf16[128,2048]{1,0:T(8,128)(2,1)S(1)} %get-tuple-element.69.refs_0_), channel_id=1, source_target_pairs={{0,24},{4,28},{8,16},{12,20},{16,8},{20,12},{24,0},{28,4},{1,25},{... | collective-permute-start | bytes 1572872 | tf_op jit(solution)/shard_map/ppermute | solution.py:44
  191.3 79.5 %collective-permute-start.25 = (bf16[128,2048]{1,0:T(8,128)(2,1)S(1)}, bf16[128,2048]{1,0:T(8,128)(2,1)}, u32[]{:S(2)}, u32[]{:S(2)}) collective-permute-start(bf16[128,2048]{1,0:T(8,128)(2,1)S(1)} %get-tuple-element.69.refs_0_), channel_id=1, source_target_pairs={{0,4},{4,0},{8,12},{12,8},{16,20},{20,16},{24,28},{28,24},{1,5},{5... | collective-permute-start | bytes 1572872 | tf_op jit(solution)/shard_map/ppermute | solution.py:44
  198.0 77.2 %collective-permute-start.26 = (bf16[128,2048]{1,0:T(8,128)(2,1)}, bf16[128,2048]{1,0:T(8,128)(2,1)}, u32[]{:S(2)}, u32[]{:S(2)}) collective-permute-start(bf16[128,2048]{1,0:T(8,128)(2,1)} %collective-permute-done.18.refs_1_), channel_id=1, source_target_pairs={{0,4},{4,0},{8,12},{12,8},{16,20},{20,16},{24,28},{28,24},{1,5},{5... | collective-permute-start | bytes 1572872 | tf_op jit(solution)/shard_map/ppermute | solution.py:44
  200.3 75.2 %all-to-all-start.2 = ((bf16[4,2,128,8,64]{2,4,3,1,0:T(8,128)(2,1)}), bf16[4,2,128,8,64]{2,4,3,1,0:T(8,128)(2,1)S(1)}, u32[]{:S(2)}, u32[]{:S(2)}) async-start(bf16[4,2,128,8,64]{2,4,3,1,0:T(8,128)(2,1)} %copy.122), calls=%async_computation.2 | async-start | bytes 2097152 | tf_op jit(solution)/shard_map/all_to_all | solution.py:103
  229.4 50.8 %collective-permute-start.27 = (bf16[128,2048]{1,0:T(8,128)(2,1)}, bf16[128,2048]{1,0:T(8,128)(2,1)}, u32[]{:S(2)}, u32[]{:S(2)}) collective-permute-start(bf16[128,2048]{1,0:T(8,128)(2,1)} %collective-permute-done.19.refs_2_), channel_id=1, source_target_pairs={{0,4},{4,0},{8,12},{12,8},{16,20},{20,16},{24,28},{28,24},{1,5},{5... | collective-permute-start | bytes 1572872 | tf_op jit(solution)/shard_map/ppermute | solution.py:44
  270.8 20.5 %collective-permute-start.21 = (bf16[128,2048]{1,0:T(8,128)(2,1)S(1)}, bf16[128,2048]{1,0:T(8,128)(2,1)}, u32[]{:S(2)}, u32[]{:S(2)}) collective-permute-start(bf16[128,2048]{1,0:T(8,128)(2,1)S(1)} %get-tuple-element.67.refs_0_), channel_id=1, source_target_pairs={{0,8},{4,12},{8,0},{12,4},{16,24},{20,28},{24,16},{28,20},{1,9},{5... | collective-permute-start | bytes 1572872 | tf_op jit(solution)/shard_map/ppermute | solution.py:44
  270.8 37.7 %collective-permute-start.22 = (bf16[128,2048]{1,0:T(8,128)(2,1)S(1)}, bf16[128,2048]{1,0:T(8,128)(2,1)}, u32[]{:S(2)}, u32[]{:S(2)}) collective-permute-start(bf16[128,2048]{1,0:T(8,128)(2,1)S(1)} %get-tuple-element.67.refs_0_), channel_id=1, source_target_pairs={{0,16},{4,20},{8,24},{12,28},{16,0},{20,4},{24,8},{28,12},{1,17},{... | collective-permute-start | bytes 1572872 | tf_op jit(solution)/shard_map/ppermute | solution.py:44
  275.2 40.0 %collective-permute-start.23 = (bf16[128,2048]{1,0:T(8,128)(2,1)S(1)}, bf16[128,2048]{1,0:T(8,128)(2,1)}, u32[]{:S(2)}, u32[]{:S(2)}) collective-permute-start(bf16[128,2048]{1,0:T(8,128)(2,1)S(1)} %get-tuple-element.67.refs_0_), channel_id=1, source_target_pairs={{0,24},{4,28},{8,16},{12,20},{16,8},{20,12},{24,0},{28,4},{1,25},{... | collective-permute-start | bytes 1572872 | tf_op jit(solution)/shard_map/ppermute | solution.py:44
  318.2 67.3 %collective-permute-start.24 = (bf16[4,128,2048]{2,1,0:T(8,128)(2,1)}, bf16[4,128,2048]{2,1,0:T(8,128)(2,1)S(1)}, u32[]{:S(2)}, u32[]{:S(2)}) collective-permute-start(bf16[4,128,2048]{2,1,0:T(8,128)(2,1)} %pad_maximum_fusion.1), channel_id=1, source_target_pairs={{0,4},{4,0},{8,12},{12,8},{16,20},{20,16},{24,28},{28,24},{1,5},{5... | collective-permute-start | bytes 6291464 | tf_op jit(solution)/shard_map/ppermute | solution.py:44
  383.5 58.3 %collective-permute-start.30 = (bf16[4,136,2048]{2,1,0:T(8,128)(2,1)}, bf16[4,136,2048]{2,1,0:T(8,128)(2,1)}, u32[]{:S(2)}, u32[]{:S(2)}) collective-permute-start(bf16[4,136,2048]{2,1,0:T(8,128)(2,1)} %get-tuple-element.80), channel_id=1, source_target_pairs={{0,4},{4,0},{8,12},{12,8},{16,20},{20,16},{24,28},{28,24},{1,5},{5... | collective-permute-start | bytes 6684680 | tf_op jit(solution)/shard_map/ppermute | solution.py:44
  444.8 22.1 %collective-permute-start.31 = (bf16[136,2048]{1,0:T(8,128)(2,1)}, bf16[136,2048]{1,0:T(8,128)(2,1)}, u32[]{:S(2)}, u32[]{:S(2)}) collective-permute-start(bf16[136,2048]{1,0:T(8,128)(2,1)} %get-tuple-element.174), channel_id=1, source_target_pairs={{0,8},{4,12},{8,0},{12,4},{16,24},{20,28},{24,16},{28,20},{1,9},{5... | collective-permute-start | bytes 1671176 | tf_op jit(solution)/shard_map/ppermute | solution.py:44
  444.8 36.4 %collective-permute-start.32 = (bf16[136,2048]{1,0:T(8,128)(2,1)}, bf16[136,2048]{1,0:T(8,128)(2,1)}, u32[]{:S(2)}, u32[]{:S(2)}) collective-permute-start(bf16[136,2048]{1,0:T(8,128)(2,1)} %get-tuple-element.176), channel_id=1, source_target_pairs={{0,16},{4,20},{8,24},{12,28},{16,0},{20,4},{24,8},{28,12},{1,17},{... | collective-permute-start | bytes 1671176 | tf_op jit(solution)/shard_map/ppermute | solution.py:44
  447.8 40.8 %collective-permute-start.33 = (bf16[136,2048]{1,0:T(8,128)(2,1)}, bf16[136,2048]{1,0:T(8,128)(2,1)}, u32[]{:S(2)}, u32[]{:S(2)}) collective-permute-start(bf16[136,2048]{1,0:T(8,128)(2,1)} %get-tuple-element.175), channel_id=1, source_target_pairs={{0,24},{4,28},{8,16},{12,20},{16,8},{20,12},{24,0},{28,4},{1,25},{... | collective-permute-start | bytes 1671176 | tf_op jit(solution)/shard_map/ppermute | solution.py:44
  466.9 52.9 %collective-permute-start.29 = (bf16[4,136,2048]{2,1,0:T(8,128)(2,1)}, bf16[4,136,2048]{2,1,0:T(8,128)(2,1)}, u32[]{:S(2)}, u32[]{:S(2)}) collective-permute-start(bf16[4,136,2048]{2,1,0:T(8,128)(2,1)} %get-tuple-element.78), channel_id=1, source_target_pairs={{0,4},{4,0},{8,12},{12,8},{16,20},{20,16},{24,28},{28,24},{1,5},{5... | collective-permute-start | bytes 6684680 | tf_op jit(solution)/shard_map/ppermute | solution.py:44
  501.0 18.9 %all-to-all-start.3 = ((bf16[8,128,256]{2,1,0:T(8,128)(2,1)}), bf16[8,128,256]{2,1,0:T(8,128)(2,1)S(1)}, u32[]{:S(2)}, u32[]{:S(2)}) async-start(bf16[8,128,256]{2,1,0:T(8,128)(2,1)} %bitcast.50), calls=%async_computation.3 | async-start | bytes 1048576 | tf_op jit(solution)/shard_map/all_to_all | solution.py:103
  504.9 389.7 %reduce-scatter.5.cloned.1.call-start = ((), (), s32[]{:S(2)}) async-start(), calls=%async_computation.15 | async-start | bytes 10485760 | tf_op jit(solution)/shard_map/reduce_scatter | solution.py:622
  522.6 17.3 %collective-permute-start.34 = (bf16[136,2048]{1,0:T(8,128)(2,1)S(1)}, bf16[136,2048]{1,0:T(8,128)(2,1)S(1)}, u32[]{:S(2)}, u32[]{:S(2)}) collective-permute-start(bf16[136,2048]{1,0:T(8,128)(2,1)S(1)} %get-tuple-element.171), channel_id=1, source_target_pairs={{0,8},{4,12},{8,0},{12,4},{16,24},{20,28},{24,16},{28,20},{1,9},{5... | collective-permute-start | bytes 1671176 | tf_op jit(solution)/shard_map/ppermute | solution.py:44
  522.7 38.1 %collective-permute-start.35 = (bf16[136,2048]{1,0:T(8,128)(2,1)S(1)}, bf16[136,2048]{1,0:T(8,128)(2,1)S(1)}, u32[]{:S(2)}, u32[]{:S(2)}) collective-permute-start(bf16[136,2048]{1,0:T(8,128)(2,1)S(1)} %get-tuple-element.173), channel_id=1, source_target_pairs={{0,16},{4,20},{8,24},{12,28},{16,0},{20,4},{24,8},{28,12},{1,17},{... | collective-permute-start | bytes 1671176 | tf_op jit(solution)/shard_map/ppermute | solution.py:44
  525.6 42.6 %collective-permute-start.36 = (bf16[136,2048]{1,0:T(8,128)(2,1)S(1)}, bf16[136,2048]{1,0:T(8,128)(2,1)S(1)}, u32[]{:S(2)}, u32[]{:S(2)}) collective-permute-start(bf16[136,2048]{1,0:T(8,128)(2,1)S(1)} %get-tuple-element.172), channel_id=1, source_target_pairs={{0,24},{4,28},{8,16},{12,20},{16,8},{20,12},{24,0},{28,4},{1,25},{... | collective-permute-start | bytes 1671176 | tf_op jit(solution)/shard_map/ppermute | solution.py:44
  586.3 34.0 %all-to-all-start.4 = ((bf16[8,128,768]{2,1,0:T(8,128)(2,1)}), bf16[8,128,768]{2,1,0:T(8,128)(2,1)}, u32[]{:S(2)}, u32[]{:S(2)}) async-start(bf16[8,128,768]{2,1,0:T(8,128)(2,1)} %get-tuple-element.90), calls=%async_computation.4 | async-start | bytes 3145728 | tf_op jit(solution)/shard_map/all_to_all | solution.py:103
  591.2 307.5 %reduce-scatter.3.cloned.1.call-start = ((), (), s32[]{:S(2)}) async-start(), calls=%async_computation.14 | async-start | bytes 9437184 | tf_op jit(solution)/shard_map/reduce_scatter | solution.py:657
  666.8 22.5 %collective-permute-start.38 = (bf16[1,8,64,768]{3,2,1,0:T(8,128)(2,1)}, bf16[1,8,64,768]{3,2,1,0:T(8,128)(2,1)}, u32[]{:S(2)}, u32[]{:S(2)}) collective-permute-start(bf16[1,8,64,768]{3,2,1,0:T(8,128)(2,1)} %get-tuple-element.181), channel_id=1, source_target_pairs={{0,1},{1,0},{2,3},{3,2},{4,5},{5,4},{6,7},{7,6},{8,9},{9,8},{10,11... | collective-permute-start | bytes 2359304 | tf_op jit(solution)/shard_map/ppermute | solution.py:44
  672.2 81.5 %all-to-all-start.6 = ((bf16[8,128,768]{2,1,0:T(8,128)(2,1)}), bf16[8,128,768]{2,1,0:T(8,128)(2,1)}, u32[]{:S(2)}, u32[]{:S(2)}) async-start(bf16[8,128,768]{2,1,0:T(8,128)(2,1)} %get-tuple-element.100), calls=%async_computation.7 | async-start | bytes 3145728 | tf_op jit(solution)/shard_map/all_to_all | solution.py:103
  677.3 18.5 %collective-permute-start.40 = (bf16[256,2048]{1,0:T(8,128)(2,1)S(1)}, bf16[256,2048]{1,0:T(8,128)(2,1)}, u32[]{:S(2)}, u32[]{:S(2)}) collective-permute-start(bf16[256,2048]{1,0:T(8,128)(2,1)S(1)} %pad_maximum_fusion.5), channel_id=1, source_target_pairs={{0,1},{1,0},{2,3},{3,2},{4,5},{5,4},{6,7},{7,6},{8,9},{9,8},{10,11... | collective-permute-start | bytes 3145736 | tf_op jit(solution)/shard_map/ppermute | solution.py:44
  677.5 26.1 %collective-permute-start.41 = (bf16[256,2048]{1,0:T(8,128)(2,1)S(1)}, bf16[256,2048]{1,0:T(8,128)(2,1)}, u32[]{:S(2)}, u32[]{:S(2)}) collective-permute-start(bf16[256,2048]{1,0:T(8,128)(2,1)S(1)} %pad_maximum_fusion.5), channel_id=1, source_target_pairs={{0,2},{1,3},{2,0},{3,1},{4,6},{5,7},{6,4},{7,5},{8,10},{9,11},{10,... | collective-permute-start | bytes 3145736 | tf_op jit(solution)/shard_map/ppermute | solution.py:44
  683.5 64.4 %collective-permute-start.51 = (bf16[2,256,2048]{2,1,0:T(8,128)(2,1)}, bf16[2,256,2048]{2,1,0:T(8,128)(2,1)}, u32[]{:S(2)}, u32[]{:S(2)}) collective-permute-start(bf16[2,256,2048]{2,1,0:T(8,128)(2,1)} %get-tuple-element.168), channel_id=1, source_target_pairs={{0,1},{1,0},{2,3},{3,2},{4,5},{5,4},{6,7},{7,6},{8,9},{9,8},{10,11... | collective-permute-start | bytes 6291464 | tf_op jit(solution)/shard_map/ppermute | solution.py:44
  683.7 22.2 %collective-permute-start.37 = (bf16[1,8,64,768]{3,2,1,0:T(8,128)(2,1)}, bf16[1,8,64,768]{3,2,1,0:T(8,128)(2,1)}, u32[]{:S(2)}, u32[]{:S(2)}) collective-permute-start(bf16[1,8,64,768]{3,2,1,0:T(8,128)(2,1)} %get-tuple-element.180), channel_id=1, source_target_pairs={{0,1},{1,0},{2,3},{3,2},{4,5},{5,4},{6,7},{7,6},{8,9},{9,8},{10,11... | collective-permute-start | bytes 2359304 | tf_op jit(solution)/shard_map/ppermute | solution.py:44
  690.6 29.1 %collective-permute-start.39 = (bf16[1,8,64,768]{3,2,1,0:T(8,128)(2,1)S(1)}, bf16[1,8,64,768]{3,2,1,0:T(8,128)(2,1)S(1)}, u32[]{:S(2)}, u32[]{:S(2)}) collective-permute-start(bf16[1,8,64,768]{3,2,1,0:T(8,128)(2,1)S(1)} %fusion.5), channel_id=1, source_target_pairs={{0,2},{1,3},{2,0},{3,1},{4,6},{5,7},{6,4},{7,5},{8,10},{9,11},{10,... | collective-permute-start | bytes 2359304 | tf_op jit(solution)/shard_map/ppermute | solution.py:44
  695.7 192.7 %collective-permute-start.50 = (bf16[2,256,2048]{2,1,0:T(8,128)(2,1)}, bf16[2,256,2048]{2,1,0:T(8,128)(2,1)}, u32[]{:S(2)}, u32[]{:S(2)}) collective-permute-start(bf16[2,256,2048]{2,1,0:T(8,128)(2,1)} %get-tuple-element.167), channel_id=1, source_target_pairs={{0,1},{1,0},{2,3},{3,2},{4,5},{5,4},{6,7},{7,6},{8,9},{9,8},{10,11... | collective-permute-start | bytes 6291464 | tf_op jit(solution)/shard_map/ppermute | solution.py:44
  703.6 85.4 %collective-permute-start.48 = (bf16[2,512,1024]{2,1,0:T(8,128)(2,1)}, bf16[2,512,1024]{2,1,0:T(8,128)(2,1)}, u32[]{:S(2)}, u32[]{:S(2)}) collective-permute-start(bf16[2,512,1024]{2,1,0:T(8,128)(2,1)} %get-tuple-element.170), channel_id=1, source_target_pairs={{0,1},{1,0},{2,3},{3,2},{4,5},{5,4},{6,7},{7,6},{8,9},{9,8},{10,11... | collective-permute-start | bytes 6291464 | tf_op jit(solution)/shard_map/ppermute | solution.py:44
  705.9 176.3 %collective-permute-start.47 = (bf16[2,512,1024]{2,1,0:T(8,128)(2,1)}, bf16[2,512,1024]{2,1,0:T(8,128)(2,1)}, u32[]{:S(2)}, u32[]{:S(2)}) collective-permute-start(bf16[2,512,1024]{2,1,0:T(8,128)(2,1)} %get-tuple-element.169), channel_id=1, source_target_pairs={{0,1},{1,0},{2,3},{3,2},{4,5},{5,4},{6,7},{7,6},{8,9},{9,8},{10,11... | collective-permute-start | bytes 6291464 | tf_op jit(solution)/shard_map/ppermute | solution.py:44
  719.7 16.7 %collective-permute-start.42 = (bf16[256,2048]{1,0:T(8,128)(2,1)}, bf16[256,2048]{1,0:T(8,128)(2,1)}, u32[]{:S(2)}, u32[]{:S(2)}) collective-permute-start(bf16[256,2048]{1,0:T(8,128)(2,1)} %collective-permute-done.41), channel_id=1, source_target_pairs={{0,1},{1,0},{2,3},{3,2},{4,5},{5,4},{6,7},{7,6},{8,9},{9,8},{10,11... | collective-permute-start | bytes 3145736 | tf_op jit(solution)/shard_map/ppermute | solution.py:44
  745.0 41.6 %collective-permute-start.43 = (bf16[4,64,2048]{2,1,0:T(8,128)(2,1)}, bf16[4,64,2048]{2,1,0:T(8,128)(2,1)}, u32[]{:S(2)}, u32[]{:S(2)}) collective-permute-start(bf16[4,64,2048]{2,1,0:T(8,128)(2,1)} %pad_maximum_fusion.6), channel_id=1, source_target_pairs={{0,4},{4,0},{8,12},{12,8},{16,20},{20,16},{24,28},{28,24},{1,5},{5... | collective-permute-start | bytes 3145736 | tf_op jit(solution)/shard_map/ppermute | solution.py:44
  752.4 136.1 %collective-permute-start.52 = (bf16[2,256,2048]{2,1,0:T(8,128)(2,1)}, bf16[2,256,2048]{2,1,0:T(8,128)(2,1)}, u32[]{:S(2)}, u32[]{:S(2)}) collective-permute-start(bf16[2,256,2048]{2,1,0:T(8,128)(2,1)} %add_convert_fusion), channel_id=1, source_target_pairs={{0,2},{1,3},{2,0},{3,1},{4,6},{5,7},{6,4},{7,5},{8,10},{9,11},{10,... | collective-permute-start | bytes 6291464 | tf_op jit(solution)/shard_map/ppermute | solution.py:44
  753.7 50.8 %all-to-all-start.8 = ((f32[32,16,128]{2,1,0:T(8,128)}), f32[32,16,128]{2,1,0:T(8,128)S(1)}, u32[]{:S(2)}, u32[]{:S(2)}) async-start(f32[32,16,128]{2,1,0:T(8,128)} %bitcast.107), calls=%async_computation.9 | async-start | bytes 524288 | tf_op jit(solution)/shard_map/all_to_all | solution.py:103
  789.0 21.0 %collective-permute-start.45 = (bf16[64,2048]{1,0:T(8,128)(2,1)}, bf16[64,2048]{1,0:T(8,128)(2,1)}, u32[]{:S(2)}, u32[]{:S(2)}) collective-permute-start(bf16[64,2048]{1,0:T(8,128)(2,1)} %get-tuple-element.179), channel_id=1, source_target_pairs={{0,16},{4,20},{8,24},{12,28},{16,0},{20,4},{24,8},{28,12},{1,17},{... | collective-permute-start | bytes 786440 | tf_op jit(solution)/shard_map/ppermute | solution.py:44
  801.6 80.6 %collective-permute-start.49 = (bf16[2,512,1024]{2,1,0:T(8,128)(2,1)}, bf16[2,512,1024]{2,1,0:T(8,128)(2,1)}, u32[]{:S(2)}, u32[]{:S(2)}) collective-permute-start(bf16[2,512,1024]{2,1,0:T(8,128)(2,1)} %add_convert_fusion.2), channel_id=1, source_target_pairs={{0,2},{1,3},{2,0},{3,1},{4,6},{5,7},{6,4},{7,5},{8,10},{9,11},{10,... | collective-permute-start | bytes 6291464 | tf_op jit(solution)/shard_map/ppermute | solution.py:44
  804.5 68.0 %all-to-all-start.7 = ((bf16[8,64,768]{2,1,0:T(8,128)(2,1)}), bf16[8,64,768]{2,1,0:T(8,128)(2,1)}, u32[]{:S(2)}, u32[]{:S(2)}) async-start(bf16[8,64,768]{2,1,0:T(8,128)(2,1)} %bitcast.240), calls=%async_computation.8 | async-start | bytes 1572864 | tf_op jit(solution)/shard_map/all_to_all | solution.py:103
  810.0 60.3 %collective-permute-start.46 = (bf16[64,2048]{1,0:T(8,128)(2,1)}, bf16[64,2048]{1,0:T(8,128)(2,1)}, u32[]{:S(2)}, u32[]{:S(2)}) collective-permute-start(bf16[64,2048]{1,0:T(8,128)(2,1)} %get-tuple-element.178), channel_id=1, source_target_pairs={{0,24},{4,28},{8,16},{12,20},{16,8},{20,12},{24,0},{28,4},{1,25},{... | collective-permute-start | bytes 786440 | tf_op jit(solution)/shard_map/ppermute | solution.py:44
  (67 other events, 1090.8 us)
Sparse Core Ops, SparseCore 0:
  9.6 59.4 all-gather.9
  70.6 58.2 all-gather.5
  130.5 58.2 all-gather.7
  190.8 114.8 all-gather.11
  571.0 71.2 reduce-scatter.4
  646.3 224.0 reduce-scatter.2
